TPU v7x, 32 devices: a whole 2x2x4 slice. The times are simulated.
32 devices in a mesh: groups: 2 (over y), tmpl: 4 (over z), sta: 2 (over x), comp: 2 (over core).
Axes of the slice: x: 2, y: 2, z: 4, core: 2. Of those that a mesh axis runs over, the one named last changes fastest.
Arguments:
- templates: bfloat16 [1024, 32, 3, 256], P(('groups', 'tmpl'), ('sta', 'comp')), parts along dimension 0, may hold values from -6 to 6
- data: bfloat16 [64, 3, 2048], P(('groups', 'sta', 'comp'), None, 'tmpl'), parts along dimension 0, may hold values from -21 to 21
- tail: bfloat16 [64, 3, 512], P(('groups', 'sta', 'comp')), parts along dimension 0, may hold values from -21 to 21
- offsets: int32 [64], P(('groups', 'sta', 'comp')), parts along dimension 0, may hold values from 0 to 255, as said below
- weights: int32 [64], P(('groups', 'sta', 'comp')), parts along dimension 0, may hold values from 1 to 4
- mask: int32 [1024, 32], P(('groups', 'tmpl'), ('sta', 'comp')), parts along dimension 0, may hold values 0 or 1
Outputs:
- stack: float32 [1024, 2048], P(('groups', 'tmpl'), ('sta', 'comp')), parts along dimension 0
There are 2 independent parts, one for each index of `groups`. A program takes and returns all parts, laid end to end along the dimension named above; each array names one. Nothing has to cross between parts.
Inputs may be any that keep to these rules, and one draw needn't show every extreme that they name: `offsets`: some station's offset is 0 and some station's is 255.
All inputs are finite; a program needn't handle non-finite values. No bound on the sum of `mask` on one device may be relied on, other than what follows from the above.
Results may differ from a plain program's by a relative error of at most 0.0055.
Values may be sent and summed in bfloat16 or wider, within the bound.
No kernel may reach another device: no remote copies, remote signals or barrier semaphores. Data moves between devices by JAX's collectives and lax.ppermute only.
A program may use at most 192 MiB of HBM per device.

v0:
```python
import jax
import jax.numpy as jnp
from jax import lax
from jax.sharding import PartitionSpec as P

EPS = 1e-05


def passed_along(x, axis, by):
    devices = lax.axis_size(axis)
    pairs = [(i, i + by) for i in range(devices) if 0 <= i + by < devices]
    return lax.ppermute(x, axis, pairs)


def unit_templates(templates):
    values = templates.astype(jnp.float32)
    centred = values - jnp.mean(values, axis=-1, keepdims=True)
    spread = jnp.mean(centred * centred, axis=-1, keepdims=True)
    return (centred * lax.rsqrt(spread + EPS)).astype(jnp.bfloat16)


def lag_table(rows, length, span):
    lead = rows.shape[:-1]
    padded = jnp.concatenate([rows, jnp.zeros(lead + (1,), rows.dtype)], axis=-1)
    period = padded.shape[-1]
    tiled = jnp.tile(padded, (1,) * len(lead) + (length + 1,))
    cut = tiled[..., : length * (period + 1)]
    return cut.reshape(lead + (length, period + 1))[..., :span]


def table_factor(table, length):
    values = table.astype(jnp.float32)
    middle = jnp.sum(values, axis=-2) / length
    squares = jnp.sum(values * values, axis=-2) / length
    spread = squares - middle * middle
    return 1.0 / (length * jnp.sqrt(spread + EPS))


def shards(templates, data, tail, offsets, weights, mask):
    length = templates.shape[-1]
    stations = data.shape[0]
    span = data.shape[-1]
    count = templates.shape[0]
    owners = lax.axis_size("tmpl")
    received = passed_along(data, "tmpl", -1)
    closing = lax.axis_index("tmpl") == owners - 1
    extended = jnp.concatenate([data, jnp.where(closing, tail, received)], axis=2)
    units = unit_templates(templates)
    station_units = jnp.transpose(units, (1, 0, 2, 3))
    station_weight = jnp.transpose(mask.astype(jnp.float32) * weights.astype(jnp.float32)[None, :])
    reach = span + length - 1
    width_sent = extended.shape[-1]
    records = lax.all_gather(extended, "tmpl", axis=2, tiled=True)
    parts = records.shape[-1] // width_sent
    grouped = records.reshape(stations, 3, parts, width_sent)

    def add_station(carry, inputs):
        unit_rows, window_rows, begin, column = inputs
        window = lax.dynamic_slice_in_dim(window_rows, begin, reach, 2)
        table = lag_table(window, length, span)
        factor_rows = table_factor(table, length)
        products = jnp.einsum(
            "tck,cpkj->tcpj", unit_rows, table, preferred_element_type=jnp.float32
        )
        scaled = jnp.sum(products * factor_rows[None], axis=1)
        return (carry + column[:, None, None] * scaled, None)

    start_rows = jnp.zeros((count, parts, span), jnp.float32)
    stacked, _ = lax.scan(
        add_station, start_rows, (station_units, grouped, offsets, station_weight)
    )
    stacked = stacked.reshape(count, parts * span)
    return lax.psum_scatter(stacked, ("sta", "comp"), scatter_dimension=1, tiled=True)


def solution(mesh):
    in_specs = (
        P(("groups", "tmpl"), ("sta", "comp"), None, None),
        P(("groups", "sta", "comp"), None, "tmpl"),
        P(("groups", "sta", "comp"), None, None),
        P(("groups", "sta", "comp")),
        P(("groups", "sta", "comp")),
        P(("groups", "tmpl"), ("sta", "comp")),
    )
    out_specs = P(("groups", "tmpl"), ("sta", "comp"))
    return jax.shard_map(shards, mesh=mesh, in_specs=in_specs, out_specs=out_specs, check_vma=False)
```

profile of v0, /device:TPU:0, one launch (start us, length us, event | category | flops | bytes accessed | tf_op | source)
XLA Modules:
  0.0 428.5 jit_solution(4442578683296231122)
XLA Ops:
  8.0 1.9 convert_reduce_fusion.1
  9.9 2.3 fusion.8
  14.3 16.3 %all_gather.3 = bf16[8,3,4096]{2,0,1:T(8,128)(2,1)S(1)} all-gather(bf16[8,3,1024]{2,0,1:T(8,128)(2,1)S(1)} %pad_maximum_fusion), channel_id=1, replica_groups=mesh['groups'=2,'tmpl'=4,'sta'=2,'comp'=2] {'tmpl'}, dimensions={2}, use_global_device_ids=true | all-gather | bytes 245760 | tf_op jit(solution)/shard_map/all_gather | solution.py:53
  30.8 361.8 %while.14 = (s32[]{:T(128)}, f32[128,4,512]{0,2,1:T(8,128)}, f32[8,128]{1,0:T(8,128)S(1)}, s32[8]{0:T(128)S(1)}, bf16[8,3,4,1024]{3,2,0,1:T(4,128)(2,1)S(1)}, /*...) while((s32[]{:T(128)}, f32[128,4,512]{0,2,1:T(8,128)}, ...), condition=%wide.region_6.7_spmd.clone, body=%wide.region_2.6_spmd.clone.sunk | while | flops 411072512 | bytes 68151520 | solution.py:69
  33.4 2.5 tile.17
  35.9 6.8 %tile.18 = bf16[3,4,197376]{2,1,0:T(4,128)(2,1)} reshape(bf16[3,4,257,768]{3,2,1,0:T(8,128)(2,1)} %tile.17) | data formatting | bytes 9474048 | tf_op jit(solution)/shard_map/while/body/eval_jaxpr/tile | solution.py:26
  42.7 6.9 %slice.24 = bf16[3,4,196864]{2,1,0:T(4,128)(2,1)} slice(bf16[3,4,197376]{2,1,0:T(4,128)(2,1)} %tile.18), slice={[0:3], [0:4], [0:196864]} | slice | bytes 9449472 | tf_op jit(solution)/shard_map/while/body/eval_jaxpr/slice | solution.py:27
  49.6 12.9 %reshape.56 = bf16[3,4,256,769]{3,2,1,0:T(8,128)(2,1)} reshape(bf16[3,4,196864]{2,1,0:T(4,128)(2,1)} %slice.24) | data formatting | bytes 9449472 | tf_op jit(solution)/shard_map/while/body/eval_jaxpr/reshape | solution.py:28
  62.5 1.9 slice-done
  64.4 2.8 copy.24
  67.2 3.6 fusion.17
  70.9 3.8 multiply_reduce_fusion.2
  78.6 2.5 tile.17
  81.1 6.8 %tile.18 = bf16[3,4,197376]{2,1,0:T(4,128)(2,1)} reshape(bf16[3,4,257,768]{3,2,1,0:T(8,128)(2,1)} %tile.17) | data formatting | bytes 9474048 | tf_op jit(solution)/shard_map/while/body/eval_jaxpr/tile | solution.py:26
  87.9 6.9 %slice.24 = bf16[3,4,196864]{2,1,0:T(4,128)(2,1)} slice(bf16[3,4,197376]{2,1,0:T(4,128)(2,1)} %tile.18), slice={[0:3], [0:4], [0:196864]} | slice | bytes 9449472 | tf_op jit(solution)/shard_map/while/body/eval_jaxpr/slice | solution.py:27
  94.8 12.9 %reshape.56 = bf16[3,4,256,769]{3,2,1,0:T(8,128)(2,1)} reshape(bf16[3,4,196864]{2,1,0:T(4,128)(2,1)} %slice.24) | data formatting | bytes 9449472 | tf_op jit(solution)/shard_map/while/body/eval_jaxpr/reshape | solution.py:28
  109.6 2.8 copy.24
  112.4 3.6 fusion.17
  116.1 3.8 multiply_reduce_fusion.2
  123.8 2.5 tile.17
  126.3 6.8 %tile.18 = bf16[3,4,197376]{2,1,0:T(4,128)(2,1)} reshape(bf16[3,4,257,768]{3,2,1,0:T(8,128)(2,1)} %tile.17) | data formatting | bytes 9474048 | tf_op jit(solution)/shard_map/while/body/eval_jaxpr/tile | solution.py:26
  133.1 6.9 %slice.24 = bf16[3,4,196864]{2,1,0:T(4,128)(2,1)} slice(bf16[3,4,197376]{2,1,0:T(4,128)(2,1)} %tile.18), slice={[0:3], [0:4], [0:196864]} | slice | bytes 9449472 | tf_op jit(solution)/shard_map/while/body/eval_jaxpr/slice | solution.py:27
  140.1 12.9 %reshape.56 = bf16[3,4,256,769]{3,2,1,0:T(8,128)(2,1)} reshape(bf16[3,4,196864]{2,1,0:T(4,128)(2,1)} %slice.24) | data formatting | bytes 9449472 | tf_op jit(solution)/shard_map/while/body/eval_jaxpr/reshape | solution.py:28
  154.8 2.8 copy.24
  157.7 3.6 fusion.17
  161.3 3.8 multiply_reduce_fusion.2
  169.0 2.5 tile.17
  171.6 6.8 %tile.18 = bf16[3,4,197376]{2,1,0:T(4,128)(2,1)} reshape(bf16[3,4,257,768]{3,2,1,0:T(8,128)(2,1)} %tile.17) | data formatting | bytes 9474048 | tf_op jit(solution)/shard_map/while/body/eval_jaxpr/tile | solution.py:26
  178.4 6.9 %slice.24 = bf16[3,4,196864]{2,1,0:T(4,128)(2,1)} slice(bf16[3,4,197376]{2,1,0:T(4,128)(2,1)} %tile.18), slice={[0:3], [0:4], [0:196864]} | slice | bytes 9449472 | tf_op jit(solution)/shard_map/while/body/eval_jaxpr/slice | solution.py:27
  185.3 12.9 %reshape.56 = bf16[3,4,256,769]{3,2,1,0:T(8,128)(2,1)} reshape(bf16[3,4,196864]{2,1,0:T(4,128)(2,1)} %slice.24) | data formatting | bytes 9449472 | tf_op jit(solution)/shard_map/while/body/eval_jaxpr/reshape | solution.py:28
  198.1 1.9 slice-done
  200.0 2.8 copy.24
  202.9 3.6 fusion.17
  206.5 3.8 multiply_reduce_fusion.2
  214.3 2.5 tile.17
  216.8 6.8 %tile.18 = bf16[3,4,197376]{2,1,0:T(4,128)(2,1)} reshape(bf16[3,4,257,768]{3,2,1,0:T(8,128)(2,1)} %tile.17) | data formatting | bytes 9474048 | tf_op jit(solution)/shard_map/while/body/eval_jaxpr/tile | solution.py:26
  223.6 6.9 %slice.24 = bf16[3,4,196864]{2,1,0:T(4,128)(2,1)} slice(bf16[3,4,197376]{2,1,0:T(4,128)(2,1)} %tile.18), slice={[0:3], [0:4], [0:196864]} | slice | bytes 9449472 | tf_op jit(solution)/shard_map/while/body/eval_jaxpr/slice | solution.py:27
  230.5 12.9 %reshape.56 = bf16[3,4,256,769]{3,2,1,0:T(8,128)(2,1)} reshape(bf16[3,4,196864]{2,1,0:T(4,128)(2,1)} %slice.24) | data formatting | bytes 9449472 | tf_op jit(solution)/shard_map/while/body/eval_jaxpr/reshape | solution.py:28
  245.3 2.8 copy.24
  248.1 3.6 fusion.17
  251.7 3.8 multiply_reduce_fusion.2
  259.5 2.5 tile.17
  262.0 6.8 %tile.18 = bf16[3,4,197376]{2,1,0:T(4,128)(2,1)} reshape(bf16[3,4,257,768]{3,2,1,0:T(8,128)(2,1)} %tile.17) | data formatting | bytes 9474048 | tf_op jit(solution)/shard_map/while/body/eval_jaxpr/tile | solution.py:26
  268.8 6.9 %slice.24 = bf16[3,4,196864]{2,1,0:T(4,128)(2,1)} slice(bf16[3,4,197376]{2,1,0:T(4,128)(2,1)} %tile.18), slice={[0:3], [0:4], [0:196864]} | slice | bytes 9449472 | tf_op jit(solution)/shard_map/while/body/eval_jaxpr/slice | solution.py:27
  275.7 12.9 %reshape.56 = bf16[3,4,256,769]{3,2,1,0:T(8,128)(2,1)} reshape(bf16[3,4,196864]{2,1,0:T(4,128)(2,1)} %slice.24) | data formatting | bytes 9449472 | tf_op jit(solution)/shard_map/while/body/eval_jaxpr/reshape | solution.py:28
  290.5 2.8 copy.24
  293.3 3.6 fusion.17
  297.0 3.8 multiply_reduce_fusion.2
  304.7 2.5 tile.17
  307.2 6.8 %tile.18 = bf16[3,4,197376]{2,1,0:T(4,128)(2,1)} reshape(bf16[3,4,257,768]{3,2,1,0:T(8,128)(2,1)} %tile.17) | data formatting | bytes 9474048 | tf_op jit(solution)/shard_map/while/body/eval_jaxpr/tile | solution.py:26
  314.0 6.9 %slice.24 = bf16[3,4,196864]{2,1,0:T(4,128)(2,1)} slice(bf16[3,4,197376]{2,1,0:T(4,128)(2,1)} %tile.18), slice={[0:3], [0:4], [0:196864]} | slice | bytes 9449472 | tf_op jit(solution)/shard_map/while/body/eval_jaxpr/slice | solution.py:27
  320.9 12.9 %reshape.56 = bf16[3,4,256,769]{3,2,1,0:T(8,128)(2,1)} reshape(bf16[3,4,196864]{2,1,0:T(4,128)(2,1)} %slice.24) | data formatting | bytes 9449472 | tf_op jit(solution)/shard_map/while/body/eval_jaxpr/reshape | solution.py:28
  335.7 2.8 copy.24
  338.5 3.6 fusion.17
  342.2 3.8 multiply_reduce_fusion.2
  349.9 2.5 tile.17
  352.4 6.8 %tile.18 = bf16[3,4,197376]{2,1,0:T(4,128)(2,1)} reshape(bf16[3,4,257,768]{3,2,1,0:T(8,128)(2,1)} %tile.17) | data formatting | bytes 9474048 | tf_op jit(solution)/shard_map/while/body/eval_jaxpr/tile | solution.py:26
  359.2 6.9 %slice.24 = bf16[3,4,196864]{2,1,0:T(4,128)(2,1)} slice(bf16[3,4,197376]{2,1,0:T(4,128)(2,1)} %tile.18), slice={[0:3], [0:4], [0:196864]} | slice | bytes 9449472 | tf_op jit(solution)/shard_map/while/body/eval_jaxpr/slice | solution.py:27
  366.1 12.9 %reshape.56 = bf16[3,4,256,769]{3,2,1,0:T(8,128)(2,1)} reshape(bf16[3,4,196864]{2,1,0:T(4,128)(2,1)} %slice.24) | data formatting | bytes 9449472 | tf_op jit(solution)/shard_map/while/body/eval_jaxpr/reshape | solution.py:28
  380.9 2.8 copy.24
  383.7 3.6 fusion.17
  387.4 3.8 multiply_reduce_fusion.2
  392.6 2.6 copy.17
  395.2 26.5 %reduce-scatter.2.cloned.1.call-done = f32[128,512]{1,0:T(8,128)} async-done(((f32[128,2048]{1,0:T(8,128)}), f32[128,512]{1,0:T(8,128)}) %reduce-scatter.2.cloned.1.call-update) | async-done | bytes 262160 | tf_op jit(solution)/shard_map/reduce_scatter | solution.py:73
  (119 shorter events, 31.6 us)
Async XLA Ops:
  6.5 7.7 %copy-start.4 = (bf16[8,3,512]{2,0,1:T(8,128)(2,1)S(1)}, bf16[8,3,512]{2,0,1:T(8,128)(2,1)}, u32[]{:S(2)}) copy-start(bf16[8,3,512]{2,0,1:T(8,128)(2,1)} %param.9) | copy-start | bytes 73732
  6.5 5.8 %copy-start.2 = (bf16[128,8,3,256]{3,1,2,0:T(8,128)(2,1)S(1)}, bf16[128,8,3,256]{3,1,2,0:T(8,128)(2,1)}, u32[]{:S(2)}) copy-start(bf16[128,8,3,256]{3,1,2,0:T(8,128)(2,1)} %param.8) | copy-start | bytes 4718596
  6.5 7.6 %copy-start.6 = (s32[8]{0:T(128)S(1)}, s32[8]{0:T(128)}, u32[]{:S(2)}) copy-start(s32[8]{0:T(128)} %param.12) | copy-start | bytes 100
  6.5 7.6 %copy-start.5 = (s32[128,8]{0,1:T(8,128)S(1)}, s32[128,8]{0,1:T(8,128)}, u32[]{:S(2)}) copy-start(s32[128,8]{0,1:T(8,128)} %param.13) | copy-start | bytes 12292
  6.5 7.7 %copy-start.3 = (bf16[8,3,512]{2,0,1:T(8,128)(2,1)S(1)}, bf16[8,3,512]{2,0,1:T(8,128)(2,1)}, u32[]{:S(2)}) copy-start(bf16[8,3,512]{2,0,1:T(8,128)(2,1)} %param.10) | copy-start | bytes 73732
  6.5 415.1 %reduce-scatter.2.cloned.1.call-start = ((), (), s32[]{:S(2)}) async-start(), calls=%async_computation.1 | async-start | bytes 1310720 | tf_op jit(solution)/shard_map/reduce_scatter | solution.py:73
  6.6 7.7 %collective-permute-start = (bf16[8,3,512]{2,0,1:T(8,128)(2,1)}, bf16[8,3,512]{2,0,1:T(8,128)(2,1)S(1)}, u32[]{:S(2)}, u32[]{:S(2)}) collective-permute-start(bf16[8,3,512]{2,0,1:T(8,128)(2,1)} %param.9), channel_id=1, source_target_pairs={{4,0},{8,4},{12,8},{5,1},{9,5},{13,9},{6,2},{10,6},{14,10},{7,3},{... | collective-permute-start | bytes 73736 | tf_op jit(solution)/shard_map/ppermute | solution.py:12
  9.9 20.9 %copy-start.7 = (s32[8]{0:T(128)S(1)}, s32[8]{0:T(128)}, u32[]{:S(2)}) copy-start(s32[8]{0:T(128)} %param.11) | copy-start | bytes 100
  62.5 1.9 slice-start
  70.9 3.8 copy-start
  75.0 1.0 copy-start.1
  107.7 1.9 slice-start
  116.1 3.8 copy-start
  120.3 1.0 copy-start.1
  152.9 1.9 slice-start
  161.3 3.8 copy-start
  165.5 1.0 copy-start.1
  198.1 1.9 slice-start
  206.5 3.8 copy-start
  210.7 1.0 copy-start.1
  243.4 1.9 slice-start
  251.7 3.8 copy-start
  255.9 1.0 copy-start.1
  288.6 1.9 slice-start
  297.0 3.8 copy-start
  301.1 1.0 copy-start.1
  333.8 1.9 slice-start
  342.2 3.8 copy-start
  346.3 1.0 copy-start.1
  379.0 1.9 slice-start
  387.4 3.8 copy-start
  391.6 1.0 copy-start.1
Sparse Core Ops, SparseCore 0:
  395.3 26.3 reduce-scatter.1
where the time goes:
time: 431 us; the launch traced here: 428 us
  local copies, waits for them, and re-layouts  287 us (67%)
  other arithmetic  38.1 us (9%)
  matrix products  30 us (7%)
  waiting for transfers between devices  26.5 us (6%)
  blocking collectives  16.3 us (4%)
  loops' own time  15.6 us (4%)
  between operations  13.5 us (3%)
    reshape x8, local copies, waits for them, and re-layouts, lag_table(): return cut.reshape(lead + (length, period + 1))[..., :span]  103 us
    another operation x16, local copies, waits for them, and re-layouts, lag_table(): tiled = jnp.tile(padded, (1,) * len(lead) + (length + 1,))  74.7 us
    slice x8, local copies, waits for them, and re-layouts, lag_table(): cut = tiled[..., :length * (period + 1)]  55.2 us
    while x56, local copies, waits for them, and re-layouts  45.7 us
    dot_general x8, matrix products, add_station(): jnp.einsum('tck,cpkj->tcpj', unit_rows, table, preferred_element_type=jnp...  30 us
    reduce_sum x8, other arithmetic, table_factor(): squares = jnp.sum(values * values, axis=-2) / length  28.8 us
    reduce_scatter x1, waiting for transfers between devices, shards(): lax.psum_scatter(stacked, ('sta', 'comp'), scatter_dimension=1, tiled=True)  26.5 us
    all_gather x1, blocking collectives, shards(): records = lax.all_gather(extended, 'tmpl', axis=2, tiled=True)  16.3 us
  transfers between devices with their start and end apart: 2, of which 1 were waited for; matrix products, arithmetic and copies ran while one was open for 1% of the time, Pallas kernels for 0%

commit v1 on v0

v1 whole, which is shorter than its diff:
```python
import functools

import jax
import jax.numpy as jnp
from jax import lax
from jax.experimental import pallas as pl
from jax.experimental.pallas import tpu as pltpu
from jax.sharding import PartitionSpec as P

EPS = 1e-05
S = 4
LANES = 128
VMEM = pl.BlockSpec(memory_space=pltpu.VMEM)
SMEM = pl.BlockSpec(memory_space=pltpu.SMEM)
PIECES = (((0, 0), (1, 0)), ((2, 0), (3, 0)), ((2, 1), (3, 1)), ((3, 1), (0, 0)), ((1, 0), (2, 0)), ((1, 1), (2, 1)))
PHASE_COLUMNS = ((0, 1), (3, 4), (2, 0), (5, 3))


def iota(shape, axis):
    return lax.broadcasted_iota(jnp.int32, shape, axis)


def template_kernel(x_ref, mask_ref, wide_ref, last_ref, unit_ref, rows_ref):
    count, comps, stations, length = x_ref.shape
    pairs = comps * stations
    group = 8
    for at in range(0, count, group):
        values = x_ref[at : at + group].astype(jnp.float32).reshape(group * pairs, length)
        centred = values - jnp.sum(values, axis=-1, keepdims=True) * (1.0 / length)
        spread = jnp.sum(centred * centred, axis=-1, keepdims=True) * (1.0 / length)
        unit = centred * lax.rsqrt(spread + EPS)
        for h in range(length // LANES):
            unit_ref[h, at * pairs : (at + group) * pairs, :] = unit[:, LANES * h : LANES * (h + 1)]
    available = jnp.transpose(mask_ref[...].astype(jnp.float32))
    for s in range(stations):
        column = available[:, s : s + 1]
        for c in range(comps):
            pair = c * stations + s
            rows = jnp.concatenate(
                [unit_ref[h, pl.ds(pair, count, stride=pairs), :] for h in range(length // LANES)], axis=1
            )
            rows_ref[pair * count : (pair + 1) * count, :] = (rows * column).astype(jnp.bfloat16)
    group_rows = length // S
    sample = iota((length, LANES), 0)
    lane = iota((length, LANES), 1)
    place = lane % group_rows
    first = lane < group_rows
    lane_row = iota((count, LANES), 1)
    last = jnp.zeros((count, LANES), jnp.float32)
    wanted = []
    for low, high in PIECES:
        base = jnp.where(first, low[0] - S * low[1], high[0] - S * high[1])
        wanted.append(jnp.where(sample == S * (group_rows - 1 - place) + base, 1.0, 0.0).astype(jnp.bfloat16))
    batch = 8
    for at in range(0, pairs, batch):
        span = rows_ref[at * count : (at + batch) * count, :]
        for v in range(0, len(PIECES), 2):
            moved = jnp.dot(span, jnp.concatenate(wanted[v : v + 2], axis=1), preferred_element_type=jnp.float32)
            for i in range(batch):
                part = moved[i * count : (i + 1) * count]
                wide_ref[at + i, :, LANES * v : LANES * v + 2 * LANES] = part.astype(jnp.bfloat16)
                pair = at + i
                if v == 0:
                    turned = pltpu.roll(part[:, LANES:], (pair - 32) % LANES, axis=1)
                    last = jnp.where(lane_row == 32 + pair, turned, last)
                if v == 4:
                    turned = pltpu.roll(part[:, :LANES], pair, axis=1)
                    last = jnp.where((lane_row == pair) | (lane_row == 64 + pair), turned, last)
    last_ref[...] = last.astype(jnp.bfloat16)


def templates_prepared(templates, mask):
    count, stations, comps, length = templates.shape
    pairs = stations * comps
    return pl.pallas_call(
        template_kernel,
        out_shape=(
            jax.ShapeDtypeStruct((pairs, count, LANES * len(PIECES)), jnp.bfloat16),
            jax.ShapeDtypeStruct((count, LANES), jnp.bfloat16),
        ),
        in_specs=[VMEM, VMEM],
        out_specs=(VMEM, VMEM),
        scratch_shapes=[
            pltpu.VMEM((length // LANES, pairs * count, LANES), jnp.float32),
            pltpu.VMEM((pairs * count, length), jnp.bfloat16),
        ],
        compiler_params=pltpu.CompilerParams(vmem_limit_bytes=24 << 20),
        cost_estimate=pl.CostEstimate(flops=2 * 10**9, bytes_accessed=8 * 10**6, transcendentals=0),
        name="templates",
    )(jnp.transpose(templates, (0, 2, 1, 3)), jnp.transpose(mask))


def later(x, by):
    return pltpu.roll(x, x.shape[-1] - by, axis=1)


def data_kernel(blocks, scal_ref, offsets_ref, weights_ref, *refs):
    block_refs, (phases_ref, ahead_ref, factor_ref, raw_ref) = refs[: blocks + 1], refs[blocks + 1 :]
    comps, stations, width = block_refs[0].shape
    pairs = comps * stations
    unitw = S * LANES
    per = width // unitw
    for i in range(blocks + 1):
        values = block_refs[i][...].astype(jnp.float32).reshape(pairs, block_refs[i].shape[-1])
        home = blocks if i == blocks else lax.rem(scal_ref[0] + i, blocks)
        for j in range(block_refs[i].shape[-1] // unitw):
            raw_ref[home * per + j] = values[:, unitw * j : unitw * (j + 1)]
    parts = raw_ref.shape[0]
    sample = iota((unitw, unitw), 0)
    lane = iota((unitw, unitw), 1)
    pick = jnp.where(sample == S * (lane % LANES) + lane // LANES, 1.0, 0.0).astype(jnp.bfloat16)
    flat = raw_ref[...].reshape(parts * pairs, unitw).astype(jnp.bfloat16)
    split = jnp.dot(flat, pick, preferred_element_type=jnp.float32)
    full = parts * LANES
    row = iota((stations, full), 0)
    offset = jnp.zeros((stations, full), jnp.int32)
    weight = jnp.zeros((stations, full), jnp.float32)
    for s in range(stations):
        offset = jnp.where(row == s, offsets_ref[s], offset)
        weight = jnp.where(row == s, weights_ref[s].astype(jnp.float32), weight)
    length = 256
    group_rows = length // S
    for c in range(comps):
        at = c * stations
        v = [
            jnp.concatenate(
                [split[b * pairs + at : b * pairs + at + stations, LANES * p : LANES * (p + 1)] for b in range(parts)], axis=1
            )
            for p in range(S)
        ]
        step = 1
        while S * step < length:
            taken = (offset & (S * step)) != 0
            v = [jnp.where(taken, later(x, step), x) for x in v]
            step *= 2
        for bit in (2, 1):
            taken = (offset & bit) != 0
            v = [jnp.where(taken, v[p + bit] if p + bit < S else later(v[p + bit - S], 1), v[p]) for p in range(S)]
        ahead = [later(x, group_rows) for x in v]
        mean = v[0] + v[1] + v[2] + v[3]
        power = v[0] * v[0] + v[1] * v[1] + v[2] * v[2] + v[3] * v[3]
        step = 1
        while step < group_rows:
            mean = mean + later(mean, step)
            power = power + later(power, step)
            step *= 2
        for r in range(S):
            middle = mean * (1.0 / length)
            spread = power * (1.0 / length) - middle * middle
            factor_ref[r, at : at + stations, :] = weight / (length * jnp.sqrt(spread + EPS))
            if r + 1 < S:
                mean = mean + (ahead[r] - v[r])
                power = power + (ahead[r] * ahead[r] - v[r] * v[r])
                ahead_ref[r, at : at + stations, :] = ahead[r]
            phases_ref[r, at : at + stations, :] = v[r]


def data_prepared(place, offsets, weights, blocks, tail):
    comps, stations, width = blocks[0].shape
    pairs = comps * stations
    unitw = S * LANES
    parts = (len(blocks) * width + tail.shape[-1]) // unitw
    full = parts * LANES
    return pl.pallas_call(
        functools.partial(data_kernel, len(blocks)),
        out_shape=(
            jax.ShapeDtypeStruct((S, pairs, full), jnp.float32),
            jax.ShapeDtypeStruct((S - 1, pairs, full), jnp.float32),
            jax.ShapeDtypeStruct((S, pairs, full), jnp.float32),
        ),
        in_specs=[SMEM, SMEM, SMEM] + [VMEM] * (len(blocks) + 1),
        out_specs=(VMEM, VMEM, VMEM),
        scratch_shapes=[pltpu.VMEM((parts, pairs, unitw), jnp.float32)],
        compiler_params=pltpu.CompilerParams(vmem_limit_bytes=24 << 20),
        cost_estimate=pl.CostEstimate(flops=10**9, bytes_accessed=2 * 10**6, transcendentals=0),
        name="records",
    )(place, offsets, weights, *blocks, tail)


def chunk_kernel(lags, scal_ref, wide_ref, last_ref, phases_ref, ahead_ref, factor_ref, away_ref, keep_ref, sum_ref):
    pairs, count, _ = wide_ref.shape
    group_rows = 64
    half = lags // S // 2
    chunk, mine = scal_ref[0], scal_ref[1]
    start = pl.multiple_of(chunk * (lags // S), LANES)
    lane = iota((8, LANES), 1)
    sub = iota((8, LANES), 0)
    tile = 2 * LANES
    for n in range(lags // S // tile):
        begin = start + n * tile
        begin = pl.multiple_of(begin, LANES)

        def factor_of(r, row):
            return factor_ref[r, row, pl.ds(begin, tile)]

        extra = []
        for r in range(S):
            held = {}
            for i in range(3):
                j = i - (3 - r)
                if j >= 0:
                    scaled = ahead_ref[j, :, pl.ds(begin, tile)] * factor_ref[r, :, pl.ds(begin, tile)]
                    held[i] = jnp.concatenate([scaled, jnp.zeros((32 - pairs, tile), jnp.float32)], axis=0)
            if held:
                none = jnp.zeros((32, tile), jnp.float32)
                table = jnp.concatenate([held.get(0, none), held.get(2, none), held.get(1, none), none], axis=0)
                extra.append(jnp.dot(last_ref[...], table.astype(jnp.bfloat16), preferred_element_type=jnp.float32))
            else:
                extra.append(None)
        for pair in range(pairs):
            rows = []
            for p in range(S):
                line = [
                    jnp.broadcast_to(phases_ref[p, pair : pair + 1, pl.ds(begin + LANES * j, LANES)], (8, LANES))
                    for j in range(3)
                ]
                for g in range(0, group_rows, 16):
                    sides = []
                    for j in range(2):
                        pieces = []
                        for h in (g, g + 8):
                            ahead = group_rows - 1 - h - sub
                            mixed = jnp.where(lane >= ahead, line[j], line[j + 1])
                            pieces.append(
                                pltpu.roll(mixed, LANES - (group_rows - 1) + h, axis=1, stride=1, stride_axis=0)
                            )
                        sides.append(jnp.concatenate(pieces, axis=0).astype(jnp.bfloat16))
                    rows.append(jnp.concatenate(sides, axis=1))
            table = jnp.concatenate(rows, axis=0)
            units = jnp.concatenate(
                [
                    jnp.concatenate([wide_ref[pair, :, LANES * v : LANES * (v + 1)] for v in PHASE_COLUMNS[r]], axis=1)
                    for r in range(S)
                ],
                axis=0,
            )
            products = jnp.dot(units, table, preferred_element_type=jnp.float32)
            for r in range(S):
                factor = factor_ref[r, pair : pair + 1, pl.ds(begin, tile)]
                scaled = products[r * count : (r + 1) * count] * factor
                where = (slice(r * count, (r + 1) * count), slice(n * tile, (n + 1) * tile))
                if pair == 0:
                    sum_ref[where] = scaled if extra[r] is None else scaled + extra[r]
                else:
                    sum_ref[where] += scaled
    other = pl.multiple_of((1 - mine) * half, LANES)
    own = pl.multiple_of(mine * half, LANES)
    for r in range(S):
        away_ref[:, r * half : (r + 1) * half] = sum_ref[r * count : (r + 1) * count, pl.ds(other, half)].astype(jnp.bfloat16)
        keep_ref[:, r * half : (r + 1) * half] = sum_ref[r * count : (r + 1) * count, pl.ds(own, half)]


def chunk_sum(lags, chunk, mine, wide, last, phases, ahead, factor):
    pairs, count, _ = wide.shape
    return pl.pallas_call(
        functools.partial(chunk_kernel, lags),
        out_shape=(
            jax.ShapeDtypeStruct((count, lags // 2), jnp.bfloat16),
            jax.ShapeDtypeStruct((count, lags // 2), jnp.float32),
        ),
        in_specs=[SMEM] + [VMEM] * 5,
        out_specs=(VMEM, VMEM),
        scratch_shapes=[pltpu.VMEM((S * count, lags // S), jnp.float32)],
        compiler_params=pltpu.CompilerParams(vmem_limit_bytes=24 << 20),
        cost_estimate=pl.CostEstimate(
            flops=2 * count * pairs * 256 * lags, bytes_accessed=8 * 10**6, transcendentals=0
        ),
        name="chunk",
    )(jnp.stack([chunk, mine]).astype(jnp.int32), wide, last, phases, ahead, factor)


def finish_kernel(take, *refs):
    terms, out_ref = refs[:-1], refs[-1]
    total = terms[0][...].astype(jnp.float32)
    for term in terms[1:]:
        total = total + term[...].astype(jnp.float32)
    width = total.shape[-1]
    half = width // S
    lane = iota((width, width), 1)
    sample = iota((width, width), 0)
    pick = jnp.where(sample == (lane % S) * half + lane // S, 1.0, 0.0).astype(jnp.bfloat16)
    left = total
    result = None
    for _ in range(take):
        piece = left.astype(jnp.bfloat16)
        moved = jnp.dot(piece, pick, preferred_element_type=jnp.float32)
        result = moved if result is None else result + moved
        left = left - piece.astype(jnp.float32)
    out_ref[...] = result


def finished(*terms):
    return pl.pallas_call(
        functools.partial(finish_kernel, 2),
        out_shape=jax.ShapeDtypeStruct(terms[0].shape, jnp.float32),
        in_specs=[VMEM] * len(terms),
        out_specs=VMEM,
        compiler_params=pltpu.CompilerParams(vmem_limit_bytes=24 << 20),
        name="finish",
    )(*terms)


def shards(templates, data, tail, offsets, weights, mask):
    owners = lax.axis_size("tmpl")
    sides = lax.axis_size("sta")
    span = data.shape[-1]
    lags = owners * span // sides
    place = lax.axis_index("tmpl")
    side = lax.axis_index("sta")
    core = lax.axis_index("comp")
    block = jnp.transpose(data, (1, 0, 2))
    closing = jnp.transpose(tail, (1, 0, 2))
    if owners <= 4:
        blocks = [block] + [
            lax.ppermute(block, "tmpl", [(i, (i - d) % owners) for i in range(owners)]) for d in range(1, owners)
        ]
    else:
        gathered = lax.all_gather(block, "tmpl", axis=0, tiled=False)
        blocks = [lax.dynamic_index_in_dim(gathered, lax.rem(place + d, owners), 0, False) for d in range(owners)]
    wide, last = templates_prepared(templates, mask)
    phases, ahead, factor = data_prepared(place.reshape(1).astype(jnp.int32), offsets, weights, blocks, closing)
    terms = []
    for d in range(1, sides + 1):
        chunk = lax.rem(side + d, sides)
        away, keep = chunk_sum(lags, chunk, core, wide, last, phases, ahead, factor)
        got = lax.ppermute(away, "comp", [(0, 1), (1, 0)])
        if d < sides:
            both = (keep + got.astype(jnp.float32)).astype(jnp.bfloat16)
            terms.append(lax.ppermute(both, "sta", [(i, (i + d) % sides) for i in range(sides)]))
        else:
            terms += [keep, got]
    return finished(*terms)


def solution(mesh):
    in_specs = (
        P(("groups", "tmpl"), ("sta", "comp"), None, None),
        P(("groups", "sta", "comp"), None, "tmpl"),
        P(("groups", "sta", "comp"), None, None),
        P(("groups", "sta", "comp")),
        P(("groups", "sta", "comp")),
        P(("groups", "tmpl"), ("sta", "comp")),
    )
    out_specs = P(("groups", "tmpl"), ("sta", "comp"))
    return jax.shard_map(shards, mesh=mesh, in_specs=in_specs, out_specs=out_specs, check_vma=False)
```

time: 431 us -> 30.5 us (0.07)
  local copies, waits for them, and re-layouts: 287 us -> 6.56 us
  other arithmetic: 38.1 us -> 0.11 us
  matrix products: 30 us -> 0 us
  waiting for transfers between devices: 26.5 us -> 3.94 us
  blocking collectives: 16.3 us -> 0 us
  loops' own time: 15.6 us -> 0 us
  between operations: 13.5 us -> 0.1 us
  Pallas kernels: 0 us -> 11.3 us
  starting transfers between devices: 1.46 us -> 8.31 us
    reshape x10 -> x0, local copies, waits for them, and re-layouts: 106 us -> none  [the longest x8 103 us: lag_table(): return cut.reshape(lead + (length, period + 1))[..., :span]]
    another operation x16 -> x0, local copies, waits for them, and re-layouts: 74.7 us -> none  [lag_table(): tiled = jnp.tile(padded, (1,) * len(lead) + (length + 1,))]
    slice x8 -> x0, local copies, waits for them, and re-layouts: 55.2 us -> none  [lag_table(): cut = tiled[..., :length * (period + 1)]]
    while x56 -> x0, local copies, waits for them, and re-layouts: 45.7 us -> none
    reduce_sum x10 -> x0, other arithmetic: 33 us -> none  [the longest x8 28.8 us: table_factor(): squares = jnp.sum(values * values, axis=-2) / length]
    dot_general x8 -> x0, matrix products: 30 us -> none  [add_station(): jnp.einsum('tck,cpkj->tcpj', unit_rows, table, preferred_element_type=jnp...]
    reduce_scatter x1 -> x0, waiting for transfers between devices: 26.5 us -> none  [shards(): lax.psum_scatter(stacked, ('sta', 'comp'), scatter_dimension=1, tiled=True)]
    all_gather x1 -> x0, blocking collectives: 16.3 us -> none  [shards(): records = lax.all_gather(extended, 'tmpl', axis=2, tiled=True)]
  transfers between devices with their start and end apart: 2 -> 6, of which waited for: 1 -> 1; matrix products, arithmetic and copies ran while one was open for 1% -> 0% of each run, Pallas kernels for 0% -> 19%
where the time goes in v1:
time: 30.5 us; the launch traced here: 30.3 us
  Pallas kernels  11.3 us (37%)
  starting transfers between devices  8.31 us (27%)
  local copies, waits for them, and re-layouts  6.56 us (22%)
  waiting for transfers between devices  3.94 us (13%)
    unnamed x16, local copies, waits for them, and re-layouts  6.56 us
    ppermute x3, starting transfers between devices, shards(): lax.ppermute(block, 'tmpl', [(i, (i - d) % owners) for i in range(owners)])  6.12 us
    pallas_call x2, Pallas kernels, chunk_sum(): pl.pallas_call(functools.partial(chunk_kernel, lags), out_shape=(jax.Shap...  5.13 us
    ppermute x1, waiting for transfers between devices, shards(): lax.ppermute(both, 'sta', [(i, (i + d) % sides) for i in range(sides)])  3.93 us
    pallas_call x1, Pallas kernels, templates_prepared(): pl.pallas_call(template_kernel, out_shape=(jax.ShapeDtypeStruct((pairs, c...  3.18 us
    pallas_call x1, Pallas kernels, data_prepared(): pl.pallas_call(functools.partial(data_kernel, len(blocks)), out_shape=(ja...  1.92 us
    ppermute x1, starting transfers between devices, shards(): lax.ppermute(both, 'sta', [(i, (i + d) % sides) for i in range(sides)])  1.56 us
    pallas_call x1, Pallas kernels, finished(): pl.pallas_call(functools.partial(finish_kernel, 2), out_shape=jax.ShapeDt...  1.11 us
  transfers between devices with their start and end apart: 6, of which 1 were waited for; matrix products, arithmetic and copies ran while one was open for 0% of the time, Pallas kernels for 19%

profile of v1, /device:TPU:0, one launch (start us, length us, event | category | flops | bytes accessed | tf_op | source)
XLA Modules:
  0.0 30.3 jit_solution(10650583306844323747)
XLA Ops:
  0.0 0.0 copy-start.1
  0.0 0.0 copy-start.4
  0.0 0.0 copy-start.5
  0.0 5.1 %collective-permute-start = (bf16[3,8,512]{2,1,0:T(8,128)(2,1)}, bf16[3,8,512]{2,1,0:T(8,128)(2,1)S(1)}, u32[]{:S(2)}, u32[]{:S(2)}) collective-permute-start(bf16[3,8,512]{2,1,0:T(8,128)(2,1)} %bitcast.9), channel_id=1, source_target_pairs={{0,12},{4,0},{8,4},{12,8},{1,13},{5,1},{9,5},{13,9},{2,14},{6,2},{... | collective-permute-start | bytes 73736 | tf_op jit(solution)/shard_map/ppermute | solution.py:315
  5.1 0.0 collective-permute-start.1
  5.1 1.0 %collective-permute-start.2 = (bf16[3,8,512]{2,1,0:T(8,128)(2,1)}, bf16[3,8,512]{2,1,0:T(8,128)(2,1)S(1)}, u32[]{:S(2)}, u32[]{:S(2)}) collective-permute-start(bf16[3,8,512]{2,1,0:T(8,128)(2,1)} %bitcast.11), channel_id=1, source_target_pairs={{0,4},{4,8},{8,12},{12,0},{1,5},{5,9},{9,13},{13,1},{2,6},{6,10},{... | collective-permute-start | bytes 73736 | tf_op jit(solution)/shard_map/ppermute | solution.py:315
  6.1 0.0 copy-start
  6.1 1.4 %copy-done = bf16[128,8,3,256]{3,1,2,0:T(8,128)(2,1)S(1)} copy-done((bf16[128,8,3,256]{3,1,2,0:T(8,128)(2,1)S(1)}, bf16[128,8,3,256]{3,1,2,0:T(8,128)(2,1)}, u32[]{:S(2)}) %copy-start) | copy-done | bytes 1572888
  7.5 0.0 copy-start.3
  7.5 0.7 %copy-done.3 = s32[128,8]{0,1:T(8,128)S(1)} copy-done((s32[128,8]{0,1:T(8,128)S(1)}, s32[128,8]{0,1:T(8,128)}, u32[]{:S(2)}) %copy-start.3) | copy-done | bytes 4120
  8.2 0.0 copy-start.2
  8.2 3.2 %templates.1 = (bf16[24,128,768]{2,1,0:T(8,128)(2,1)S(1)}, bf16[128,128]{1,0:T(8,128)(2,1)S(1)}) custom-call(bf16[128,3,8,256]{3,2,1,0:T(8,128)(2,1)S(1)} %bitcast.8, s32[8,128]{1,0:T(8,128)S(1)} %bitcast.14), custom_call_target="tpu_custom_call" | custom-call | flops 2000000000 | bytes 8000000 | tf_op jit(solution)/shard_map/templates/pallas_call | solution.py:75
  11.4 0.0 copy-start.6
  11.4 2.1 %copy-done.6 = bf16[24,128,768]{2,1,0:T(8,128)(2,1)} copy-done((bf16[24,128,768]{2,1,0:T(8,128)(2,1)}, bf16[24,128,768]{2,1,0:T(8,128)(2,1)S(1)}, u32[]{:S(2)}) %copy-start.6) | copy-done | bytes 4718616
  13.5 0.1 pad_add_fusion
  13.6 0.0 collective-permute-done.refs_1_
  13.6 0.0 collective-permute-done.1.refs_2_
  13.6 0.0 collective-permute-done.2.refs_3_
  13.6 0.0 copy-done.1
  13.6 0.0 copy-done.4
  13.6 0.0 copy-done.5
  13.7 0.0 copy-done.2
  13.7 1.9 %records.1 = (f32[4,24,640]{2,1,0:T(8,128)S(1)}, f32[3,24,640]{2,1,0:T(8,128)S(1)}, f32[4,24,640]{2,1,0:T(8,128)S(1)}) custom-call(s32[1]{0:T(128)} %bitcast.4.scal_ref, s32[8]{0:T(128)S(1)} %copy-done.4, s32[8]{0:T(128)S(1)} %copy-done.5, bf16[3,8,512]{2,1,0:T(8,128)(2,1)S(1)} %bitcast.12, bf16[3,8,512]{2,1,0:T(8,128)(2,1)S(1)} %collective-permute-done.refs_1_, ...), custom_call_target="tpu_custom_call" | custom-call | flops 1000000000 | bytes 2000000 | tf_op jit(solution)/shard_map/records/pallas_call | solution.py:164
  15.6 0.0 copy-start.7
  15.6 2.3 %copy-done.7 = bf16[24,128,768]{2,1,0:T(8,128)(2,1)S(1)} copy-done((bf16[24,128,768]{2,1,0:T(8,128)(2,1)S(1)}, bf16[24,128,768]{2,1,0:T(8,128)(2,1)}, u32[]{:S(2)}) %copy-start.7) | copy-done | bytes 4718616
  17.9 2.6 %chunk.2 = (bf16[128,512]{1,0:T(8,128)(2,1)S(1)}, f32[128,512]{1,0:T(8,128)S(1)}) custom-call(s32[2]{0:T(128)S(1)} %get-tuple-element.23.scal_ref, bf16[24,128,768]{2,1,0:T(8,128)(2,1)S(1)} %copy-done.7, bf16[128,128]{1,0:T(8,128)(2,1)S(1)} %get-tuple-element.15.last_ref, f32[4,24,640]{2,1,0:T(8,128)S(1)} %get-tuple-element.16.phases_ref, ...), custom_call_target="tpu_custom_call" | custom-call | flops 1610612736 | bytes 8000000 | tf_op jit(solution)/shard_map/chunk/pallas_call | solution.py:255
  20.5 0.1 collective-permute-start.3
  20.6 2.6 %chunk.3 = (bf16[128,512]{1,0:T(8,128)(2,1)S(1)}, f32[128,512]{1,0:T(8,128)S(1)}) custom-call(s32[2]{0:T(128)S(1)} %get-tuple-element.24.scal_ref, bf16[24,128,768]{2,1,0:T(8,128)(2,1)S(1)} %copy-done.7, bf16[128,128]{1,0:T(8,128)(2,1)S(1)} %get-tuple-element.15.last_ref, f32[4,24,640]{2,1,0:T(8,128)S(1)} %get-tuple-element.16.phases_ref, ...), custom_call_target="tpu_custom_call" | custom-call | flops 1610612736 | bytes 8000000 | tf_op jit(solution)/shard_map/chunk/pallas_call | solution.py:255
  23.1 0.6 %collective-permute-start.5 = (bf16[128,512]{1,0:T(8,128)(2,1)S(1)}, bf16[128,512]{1,0:T(8,128)(2,1)S(1)}, u32[]{:S(2)}, u32[]{:S(2)}) collective-permute-start(bf16[128,512]{1,0:T(8,128)(2,1)S(1)} %get-tuple-element.22), channel_id=1, source_target_pairs={{0,1},{1,0},{2,3},{3,2},{4,5},{5,4},{6,7},{7,6},{8,9},{9,8},{10,11... | collective-permute-start | bytes 393224 | tf_op jit(solution)/shard_map/ppermute | solution.py:326
  23.7 0.0 collective-permute-done.3
  23.7 1.6 %collective-permute-start.4 = (bf16[128,512]{1,0:T(8,128)(2,1)S(1)}, bf16[128,512]{1,0:T(8,128)(2,1)S(1)}, u32[]{:S(2)}, u32[]{:S(2)}) collective-permute-start(bf16[128,512]{1,0:T(8,128)(2,1)S(1)} %add_convert_fusion), channel_id=1, source_target_pairs={{0,2},{2,0},{1,3},{3,1},{4,6},{6,4},{5,7},{7,5},{8,10},{10,8},{9,1... | collective-permute-start | bytes 393224 | tf_op jit(solution)/shard_map/ppermute | solution.py:329
  25.3 0.0 collective-permute-done.5.refs_2_
  25.3 3.9 %collective-permute-done.4.refs_0_ = bf16[128,512]{1,0:T(8,128)(2,1)S(1)} collective-permute-done((bf16[128,512]{1,0:T(8,128)(2,1)S(1)}, bf16[128,512]{1,0:T(8,128)(2,1)S(1)}, u32[]{:S(2)}, u32[]{:S(2)}) %collective-permute-start.4) | collective-permute-done | bytes 131104 | tf_op jit(solution)/shard_map/ppermute | solution.py:329
  29.2 1.1 %finish.1 = f32[128,512]{1,0:T(8,128)} custom-call(bf16[128,512]{1,0:T(8,128)(2,1)S(1)} %collective-permute-done.4.refs_0_, f32[128,512]{1,0:T(8,128)S(1)} %get-tuple-element.21.refs_1_, bf16[128,512]{1,0:T(8,128)(2,1)S(1)} %collective-permute-done.5.refs_2_), custom_call_target="tpu_custom_call" | custom-call | tf_op jit(solution)/shard_map/finish/pallas_call | solution.py:293
  (1 shorter events, 0.0 us)
Async XLA Ops:
  0.0 13.6 %copy-start.1 = (bf16[8,3,512]{2,0,1:T(8,128)(2,1)S(1)}, bf16[8,3,512]{2,0,1:T(8,128)(2,1)}, u32[]{:S(2)}) copy-start(bf16[8,3,512]{2,0,1:T(8,128)(2,1)} %param.7) | copy-start | bytes 73732
  0.0 13.6 %copy-start.4 = (s32[8]{0:T(128)S(1)}, s32[8]{0:T(128)}, u32[]{:S(2)}) copy-start(s32[8]{0:T(128)} %offsets_ref.1) | copy-start | bytes 100
  0.0 13.6 %copy-start.5 = (s32[8]{0:T(128)S(1)}, s32[8]{0:T(128)}, u32[]{:S(2)}) copy-start(s32[8]{0:T(128)} %weights_ref.1) | copy-start | bytes 100
  0.0 13.6 %collective-permute-start = (bf16[3,8,512]{2,1,0:T(8,128)(2,1)}, bf16[3,8,512]{2,1,0:T(8,128)(2,1)S(1)}, u32[]{:S(2)}, u32[]{:S(2)}) collective-permute-start(bf16[3,8,512]{2,1,0:T(8,128)(2,1)} %bitcast.9), channel_id=1, source_target_pairs={{0,12},{4,0},{8,4},{12,8},{1,13},{5,1},{9,5},{13,9},{2,14},{6,2},{... | collective-permute-start | bytes 73736 | tf_op jit(solution)/shard_map/ppermute | solution.py:315
  5.1 8.5 %collective-permute-start.1 = (bf16[3,8,512]{2,1,0:T(8,128)(2,1)}, bf16[3,8,512]{2,1,0:T(8,128)(2,1)S(1)}, u32[]{:S(2)}, u32[]{:S(2)}) collective-permute-start(bf16[3,8,512]{2,1,0:T(8,128)(2,1)} %bitcast.10), channel_id=1, source_target_pairs={{0,8},{4,12},{8,0},{12,4},{1,9},{5,13},{9,1},{13,5},{2,10},{6,14},... | collective-permute-start | bytes 73736 | tf_op jit(solution)/shard_map/ppermute | solution.py:315
  5.1 8.5 %collective-permute-start.2 = (bf16[3,8,512]{2,1,0:T(8,128)(2,1)}, bf16[3,8,512]{2,1,0:T(8,128)(2,1)S(1)}, u32[]{:S(2)}, u32[]{:S(2)}) collective-permute-start(bf16[3,8,512]{2,1,0:T(8,128)(2,1)} %bitcast.11), channel_id=1, source_target_pairs={{0,4},{4,8},{8,12},{12,0},{1,5},{5,9},{9,13},{13,1},{2,6},{6,10},{... | collective-permute-start | bytes 73736 | tf_op jit(solution)/shard_map/ppermute | solution.py:315
  6.1 1.4 %copy-start = (bf16[128,8,3,256]{3,1,2,0:T(8,128)(2,1)S(1)}, bf16[128,8,3,256]{3,1,2,0:T(8,128)(2,1)}, u32[]{:S(2)}) copy-start(bf16[128,8,3,256]{3,1,2,0:T(8,128)(2,1)} %param.6) | copy-start | bytes 4718596
  7.5 0.7 %copy-start.3 = (s32[128,8]{0,1:T(8,128)S(1)}, s32[128,8]{0,1:T(8,128)}, u32[]{:S(2)}) copy-start(s32[128,8]{0,1:T(8,128)} %param.11) | copy-start | bytes 12292
  8.2 5.4 %copy-start.2 = (bf16[8,3,512]{2,0,1:T(8,128)(2,1)S(1)}, bf16[8,3,512]{2,0,1:T(8,128)(2,1)}, u32[]{:S(2)}) copy-start(bf16[8,3,512]{2,0,1:T(8,128)(2,1)} %param.8) | copy-start | bytes 73732
  11.4 2.1 %copy-start.6 = (bf16[24,128,768]{2,1,0:T(8,128)(2,1)}, bf16[24,128,768]{2,1,0:T(8,128)(2,1)S(1)}, u32[]{:S(2)}) copy-start(bf16[24,128,768]{2,1,0:T(8,128)(2,1)S(1)} %get-tuple-element.14.wide_ref) | copy-start | bytes 14155780
  15.6 2.3 %copy-start.7 = (bf16[24,128,768]{2,1,0:T(8,128)(2,1)S(1)}, bf16[24,128,768]{2,1,0:T(8,128)(2,1)}, u32[]{:S(2)}) copy-start(bf16[24,128,768]{2,1,0:T(8,128)(2,1)} %copy-done.6) | copy-start | bytes 14155780
  20.5 3.2 %collective-permute-start.3 = (bf16[128,512]{1,0:T(8,128)(2,1)S(1)}, bf16[128,512]{1,0:T(8,128)(2,1)S(1)}, u32[]{:S(2)}, u32[]{:S(2)}) collective-permute-start(bf16[128,512]{1,0:T(8,128)(2,1)S(1)} %get-tuple-element.20), channel_id=1, source_target_pairs={{0,1},{1,0},{2,3},{3,2},{4,5},{5,4},{6,7},{7,6},{8,9},{9,8},{10,11... | collective-permute-start | bytes 393224 | tf_op jit(solution)/shard_map/ppermute | solution.py:326
  23.1 2.2 %collective-permute-start.5 = (bf16[128,512]{1,0:T(8,128)(2,1)S(1)}, bf16[128,512]{1,0:T(8,128)(2,1)S(1)}, u32[]{:S(2)}, u32[]{:S(2)}) collective-permute-start(bf16[128,512]{1,0:T(8,128)(2,1)S(1)} %get-tuple-element.22), channel_id=1, source_target_pairs={{0,1},{1,0},{2,3},{3,2},{4,5},{5,4},{6,7},{7,6},{8,9},{9,8},{10,11... | collective-permute-start | bytes 393224 | tf_op jit(solution)/shard_map/ppermute | solution.py:326
  23.7 5.5 %collective-permute-start.4 = (bf16[128,512]{1,0:T(8,128)(2,1)S(1)}, bf16[128,512]{1,0:T(8,128)(2,1)S(1)}, u32[]{:S(2)}, u32[]{:S(2)}) collective-permute-start(bf16[128,512]{1,0:T(8,128)(2,1)S(1)} %add_convert_fusion), channel_id=1, source_target_pairs={{0,2},{2,0},{1,3},{3,1},{4,6},{6,4},{5,7},{7,5},{8,10},{10,8},{9,1... | collective-permute-start | bytes 393224 | tf_op jit(solution)/shard_map/ppermute | solution.py:329

commit v2 on v1

--- a/solution.py
+++ b/solution.py
@@ -8,9 +8,11 @@
 from jax.sharding import PartitionSpec as P
 
 EPS = 1e-05
+BATCH = 3
 S = 4
 LANES = 128
 VMEM = pl.BlockSpec(memory_space=pltpu.VMEM)
+HBM = pl.BlockSpec(memory_space=pltpu.HBM)
 SMEM = pl.BlockSpec(memory_space=pltpu.SMEM)
 PIECES = (((0, 0), (1, 0)), ((2, 0), (3, 0)), ((2, 1), (3, 1)), ((3, 1), (0, 0)), ((1, 0), (2, 0)), ((1, 1), (2, 1)))
 PHASE_COLUMNS = ((0, 1), (3, 4), (2, 0), (5, 3))
@@ -20,18 +22,31 @@
     return lax.broadcasted_iota(jnp.int32, shape, axis)
 
 
-def template_kernel(x_ref, mask_ref, wide_ref, last_ref, unit_ref, rows_ref):
+def template_kernel(source_ref, mask_ref, wide_ref, last_ref, x_ref, unit_ref, rows_ref, held_ref, flag_ref, arrived, sent):
     count, comps, stations, length = x_ref.shape
     pairs = comps * stations
     group = 8
+    quarter = count // 4
+    copies = [
+        pltpu.make_async_copy(
+            source_ref.at[i * quarter : (i + 1) * quarter], x_ref.at[i * quarter : (i + 1) * quarter], arrived.at[i]
+        )
+        for i in range(4)
+    ]
+    flags = pltpu.make_async_copy(mask_ref, flag_ref, arrived.at[4])
+    for copy in copies + [flags]:
+        copy.start()
     for at in range(0, count, group):
+        if at % quarter == 0:
+            copies[at // quarter].wait()
         values = x_ref[at : at + group].astype(jnp.float32).reshape(group * pairs, length)
         centred = values - jnp.sum(values, axis=-1, keepdims=True) * (1.0 / length)
         spread = jnp.sum(centred * centred, axis=-1, keepdims=True) * (1.0 / length)
         unit = centred * lax.rsqrt(spread + EPS)
         for h in range(length // LANES):
             unit_ref[h, at * pairs : (at + group) * pairs, :] = unit[:, LANES * h : LANES * (h + 1)]
-    available = jnp.transpose(mask_ref[...].astype(jnp.float32))
+    flags.wait()
+    available = jnp.transpose(flag_ref[...].astype(jnp.float32))
     for s in range(stations):
         column = available[:, s : s + 1]
         for c in range(comps):
@@ -52,13 +67,14 @@
         base = jnp.where(first, low[0] - S * low[1], high[0] - S * high[1])
         wanted.append(jnp.where(sample == S * (group_rows - 1 - place) + base, 1.0, 0.0).astype(jnp.bfloat16))
     batch = 8
+    leaving = []
     for at in range(0, pairs, batch):
         span = rows_ref[at * count : (at + batch) * count, :]
         for v in range(0, len(PIECES), 2):
             moved = jnp.dot(span, jnp.concatenate(wanted[v : v + 2], axis=1), preferred_element_type=jnp.float32)
             for i in range(batch):
                 part = moved[i * count : (i + 1) * count]
-                wide_ref[at + i, :, LANES * v : LANES * v + 2 * LANES] = part.astype(jnp.bfloat16)
+                held_ref[at + i, :, LANES * v : LANES * v + 2 * LANES] = part.astype(jnp.bfloat16)
                 pair = at + i
                 if v == 0:
                     turned = pltpu.roll(part[:, LANES:], (pair - 32) % LANES, axis=1)
@@ -66,36 +82,49 @@
                 if v == 4:
                     turned = pltpu.roll(part[:, :LANES], pair, axis=1)
                     last = jnp.where((lane_row == pair) | (lane_row == 64 + pair), turned, last)
+        copy = pltpu.make_async_copy(held_ref.at[at : at + batch], wide_ref.at[at : at + batch], sent.at[at // batch])
+        copy.start()
+        leaving.append(copy)
     last_ref[...] = last.astype(jnp.bfloat16)
+    for copy in leaving:
+        copy.wait()
+
+
+def in_hbm(x):
+    return pltpu.with_memory_space_constraint(x, pltpu.HBM)
 
 
 def templates_prepared(templates, mask):
     count, stations, comps, length = templates.shape
     pairs = stations * comps
-    return pl.pallas_call(
+    wide = (pairs, count, LANES * len(PIECES))
+    wide, last = pl.pallas_call(
         template_kernel,
-        out_shape=(
-            jax.ShapeDtypeStruct((pairs, count, LANES * len(PIECES)), jnp.bfloat16),
-            jax.ShapeDtypeStruct((count, LANES), jnp.bfloat16),
-        ),
-        in_specs=[VMEM, VMEM],
-        out_specs=(VMEM, VMEM),
+        out_shape=(pltpu.HBM(wide, jnp.bfloat16), jax.ShapeDtypeStruct((count, LANES), jnp.bfloat16)),
+        in_specs=[HBM, HBM],
+        out_specs=(HBM, VMEM),
         scratch_shapes=[
+            pltpu.VMEM((count, comps, stations, length), jnp.bfloat16),
             pltpu.VMEM((length // LANES, pairs * count, LANES), jnp.float32),
             pltpu.VMEM((pairs * count, length), jnp.bfloat16),
+            pltpu.VMEM(wide, jnp.bfloat16),
+            pltpu.VMEM((stations, count), jnp.int32),
+            pltpu.SemaphoreType.DMA((5,)),
+            pltpu.SemaphoreType.DMA((pairs // 8,)),
         ],
         compiler_params=pltpu.CompilerParams(vmem_limit_bytes=24 << 20),
         cost_estimate=pl.CostEstimate(flops=2 * 10**9, bytes_accessed=8 * 10**6, transcendentals=0),
         name="templates",
-    )(jnp.transpose(templates, (0, 2, 1, 3)), jnp.transpose(mask))
+    )(in_hbm(jnp.transpose(templates, (0, 2, 1, 3))), in_hbm(jnp.transpose(mask)))
+    return wide, last
 
 
 def later(x, by):
     return pltpu.roll(x, x.shape[-1] - by, axis=1)
 
 
-def data_kernel(blocks, scal_ref, offsets_ref, weights_ref, *refs):
-    block_refs, (phases_ref, ahead_ref, factor_ref, raw_ref) = refs[: blocks + 1], refs[blocks + 1 :]
+def records(scal_ref, offsets_ref, weights_ref, block_refs, phases_ref, ahead_ref, factor_ref, raw_ref):
+    blocks = len(block_refs) - 1
     comps, stations, width = block_refs[0].shape
     pairs = comps * stations
     unitw = S * LANES
@@ -106,9 +135,8 @@
         for j in range(block_refs[i].shape[-1] // unitw):
             raw_ref[home * per + j] = values[:, unitw * j : unitw * (j + 1)]
     parts = raw_ref.shape[0]
-    sample = iota((unitw, unitw), 0)
-    lane = iota((unitw, unitw), 1)
-    pick = jnp.where(sample == S * (lane % LANES) + lane // LANES, 1.0, 0.0).astype(jnp.bfloat16)
+    column = iota((1, unitw), 1)
+    pick = jnp.where(iota((unitw, unitw), 0) == S * (column % LANES) + column // LANES, 1.0, 0.0).astype(jnp.bfloat16)
     flat = raw_ref[...].reshape(parts * pairs, unitw).astype(jnp.bfloat16)
     split = jnp.dot(flat, pick, preferred_element_type=jnp.float32)
     full = parts * LANES
@@ -155,33 +183,10 @@
             phases_ref[r, at : at + stations, :] = v[r]
 
 
-def data_prepared(place, offsets, weights, blocks, tail):
-    comps, stations, width = blocks[0].shape
-    pairs = comps * stations
-    unitw = S * LANES
-    parts = (len(blocks) * width + tail.shape[-1]) // unitw
-    full = parts * LANES
-    return pl.pallas_call(
-        functools.partial(data_kernel, len(blocks)),
-        out_shape=(
-            jax.ShapeDtypeStruct((S, pairs, full), jnp.float32),
-            jax.ShapeDtypeStruct((S - 1, pairs, full), jnp.float32),
-            jax.ShapeDtypeStruct((S, pairs, full), jnp.float32),
-        ),
-        in_specs=[SMEM, SMEM, SMEM] + [VMEM] * (len(blocks) + 1),
-        out_specs=(VMEM, VMEM, VMEM),
-        scratch_shapes=[pltpu.VMEM((parts, pairs, unitw), jnp.float32)],
-        compiler_params=pltpu.CompilerParams(vmem_limit_bytes=24 << 20),
-        cost_estimate=pl.CostEstimate(flops=10**9, bytes_accessed=2 * 10**6, transcendentals=0),
-        name="records",
-    )(place, offsets, weights, *blocks, tail)
-
-
-def chunk_kernel(lags, scal_ref, wide_ref, last_ref, phases_ref, ahead_ref, factor_ref, away_ref, keep_ref, sum_ref):
+def chunk_sum(lags, precise, chunk, mine, arrivals, wide_ref, last_ref, phases_ref, ahead_ref, factor_ref, away_ref, keep_ref, sum_ref):
     pairs, count, _ = wide_ref.shape
     group_rows = 64
     half = lags // S // 2
-    chunk, mine = scal_ref[0], scal_ref[1]
     start = pl.multiple_of(chunk * (lags // S), LANES)
     lane = iota((8, LANES), 1)
     sub = iota((8, LANES), 0)
@@ -208,6 +213,8 @@
             else:
                 extra.append(None)
         for pair in range(pairs):
+            if n == 0 and pair % BATCH == 0:
+                arrivals[pair // BATCH].wait()
             rows = []
             for p in range(S):
                 line = [
@@ -245,59 +252,94 @@
                     sum_ref[where] += scaled
     other = pl.multiple_of((1 - mine) * half, LANES)
     own = pl.multiple_of(mine * half, LANES)
-    for r in range(S):
-        away_ref[:, r * half : (r + 1) * half] = sum_ref[r * count : (r + 1) * count, pl.ds(other, half)].astype(jnp.bfloat16)
-        keep_ref[:, r * half : (r + 1) * half] = sum_ref[r * count : (r + 1) * count, pl.ds(own, half)]
-
-
-def chunk_sum(lags, chunk, mine, wide, last, phases, ahead, factor):
-    pairs, count, _ = wide.shape
+    width = S * half
+    row = iota((width, 1), 0)
+    pick = jnp.where(iota((width, width), 1) == S * (row % half) + row // half, 1.0, 0.0).astype(jnp.bfloat16)
+    halves = [
+        jnp.concatenate([sum_ref[r * count : (r + 1) * count, pl.ds(at, half)] for r in range(S)], axis=1) for at in (other, own)
+    ]
+    pieces = [x.astype(jnp.bfloat16) for x in halves]
+    if precise:
+        pieces.append((halves[1] - pieces[1].astype(jnp.float32)).astype(jnp.bfloat16))
+    moved = jnp.dot(jnp.concatenate(pieces, axis=0), pick, preferred_element_type=jnp.float32)
+    away_ref[...] = moved[:count].astype(jnp.bfloat16)
+    kept = moved[count : 2 * count]
+    keep_ref[...] = kept + moved[2 * count :] if precise else kept.astype(jnp.bfloat16)
+
+
+def arriving(wide_ref, held_ref, arrived):
+    copies = [
+        pltpu.make_async_copy(wide_ref.at[at : at + BATCH], held_ref.at[at : at + BATCH], arrived.at[at // BATCH])
+        for at in range(0, wide_ref.shape[0], BATCH)
+    ]
+    for copy in copies:
+        copy.start()
+    return copies
+
+
+def first_kernel(blocks, lags, precise, scal_ref, offsets_ref, weights_ref, wide_ref, last_ref, *refs):
+    block_refs = refs[: blocks + 1]
+    phases_ref, ahead_ref, factor_ref, away_ref, keep_ref, raw_ref, held_ref, sum_ref, arrived = refs[blocks + 1 :]
+    copies = arriving(wide_ref, held_ref, arrived)
+    records(scal_ref, offsets_ref, weights_ref, block_refs, phases_ref, ahead_ref, factor_ref, raw_ref)
+    chunk_sum(
+        lags, precise, scal_ref[1], scal_ref[2], copies, held_ref, last_ref, phases_ref, ahead_ref, factor_ref, away_ref, keep_ref, sum_ref
+    )
+
+
+def later_kernel(lags, precise, scal_ref, wide_ref, last_ref, phases_ref, ahead_ref, factor_ref, away_ref, keep_ref, held_ref, sum_ref, arrived):
+    copies = arriving(wide_ref, held_ref, arrived)
+    chunk_sum(
+        lags, precise, scal_ref[1], scal_ref[2], copies, held_ref, last_ref, phases_ref, ahead_ref, factor_ref, away_ref, keep_ref, sum_ref
+    )
+
+
+def sums_of(lags, precise, wide):
+    pairs, count, columns = wide.shape
+    shapes = (
+        jax.ShapeDtypeStruct((count, lags // 2), jnp.bfloat16),
+        jax.ShapeDtypeStruct((count, lags // 2), jnp.float32 if precise else jnp.bfloat16),
+    )
+    scratch = [
+        pltpu.VMEM((pairs, count, columns), jnp.bfloat16),
+        pltpu.VMEM((S * count, lags // S), jnp.float32),
+        pltpu.SemaphoreType.DMA((pairs // BATCH,)),
+    ]
+    params = dict(
+        compiler_params=pltpu.CompilerParams(vmem_limit_bytes=24 << 20),
+        cost_estimate=pl.CostEstimate(flops=2 * count * pairs * 256 * lags, bytes_accessed=8 * 10**6, transcendentals=0),
+    )
+    return shapes, scratch, params
+
+
+def first_sums(lags, precise, scal, offsets, weights, wide, last, blocks, tail):
+    comps, stations, width = blocks[0].shape
+    pairs = comps * stations
+    parts = (len(blocks) * width + tail.shape[-1]) // (S * LANES)
+    full = parts * LANES
+    shapes, scratch, params = sums_of(lags, precise, wide)
     return pl.pallas_call(
-        functools.partial(chunk_kernel, lags),
-        out_shape=(
-            jax.ShapeDtypeStruct((count, lags // 2), jnp.bfloat16),
-            jax.ShapeDtypeStruct((count, lags // 2), jnp.float32),
-        ),
-        in_specs=[SMEM] + [VMEM] * 5,
+        functools.partial(first_kernel, len(blocks), lags, precise),
+        out_shape=tuple(jax.ShapeDtypeStruct((n, pairs, full), jnp.float32) for n in (S, S - 1, S)) + shapes,
+        in_specs=[SMEM, SMEM, SMEM, HBM, VMEM] + [VMEM] * (len(blocks) + 1),
+        out_specs=(VMEM,) * 5,
+        scratch_shapes=[pltpu.VMEM((parts, pairs, S * LANES), jnp.float32)] + scratch,
+        name="records_chunk",
+        **params,
+    )(scal, offsets, weights, in_hbm(wide), last, *blocks, tail)
+
+
+def later_sums(lags, precise, scal, wide, last, tables):
+    shapes, scratch, params = sums_of(lags, precise, wide)
+    return pl.pallas_call(
+        functools.partial(later_kernel, lags, precise),
+        out_shape=shapes,
+        in_specs=[SMEM, HBM] + [VMEM] * 4,
         out_specs=(VMEM, VMEM),
-        scratch_shapes=[pltpu.VMEM((S * count, lags // S), jnp.float32)],
-        compiler_params=pltpu.CompilerParams(vmem_limit_bytes=24 << 20),
-        cost_estimate=pl.CostEstimate(
-            flops=2 * count * pairs * 256 * lags, bytes_accessed=8 * 10**6, transcendentals=0
-        ),
+        scratch_shapes=scratch,
         name="chunk",
-    )(jnp.stack([chunk, mine]).astype(jnp.int32), wide, last, phases, ahead, factor)
-
-
-def finish_kernel(take, *refs):
-    terms, out_ref = refs[:-1], refs[-1]
-    total = terms[0][...].astype(jnp.float32)
-    for term in terms[1:]:
-        total = total + term[...].astype(jnp.float32)
-    width = total.shape[-1]
-    half = width // S
-    lane = iota((width, width), 1)
-    sample = iota((width, width), 0)
-    pick = jnp.where(sample == (lane % S) * half + lane // S, 1.0, 0.0).astype(jnp.bfloat16)
-    left = total
-    result = None
-    for _ in range(take):
-        piece = left.astype(jnp.bfloat16)
-        moved = jnp.dot(piece, pick, preferred_element_type=jnp.float32)
-        result = moved if result is None else result + moved
-        left = left - piece.astype(jnp.float32)
-    out_ref[...] = result
-
-
-def finished(*terms):
-    return pl.pallas_call(
-        functools.partial(finish_kernel, 2),
-        out_shape=jax.ShapeDtypeStruct(terms[0].shape, jnp.float32),
-        in_specs=[VMEM] * len(terms),
-        out_specs=VMEM,
-        compiler_params=pltpu.CompilerParams(vmem_limit_bytes=24 << 20),
-        name="finish",
-    )(*terms)
+        **params,
+    )(scal, in_hbm(wide), last, *tables)
 
 
 def shards(templates, data, tail, offsets, weights, mask):
@@ -318,18 +360,28 @@
         gathered = lax.all_gather(block, "tmpl", axis=0, tiled=False)
         blocks = [lax.dynamic_index_in_dim(gathered, lax.rem(place + d, owners), 0, False) for d in range(owners)]
     wide, last = templates_prepared(templates, mask)
-    phases, ahead, factor = data_prepared(place.reshape(1).astype(jnp.int32), offsets, weights, blocks, closing)
-    terms = []
+    gotten = []
+    both = None
     for d in range(1, sides + 1):
         chunk = lax.rem(side + d, sides)
-        away, keep = chunk_sum(lags, chunk, core, wide, last, phases, ahead, factor)
+        if both is not None:
+            chunk, _ = lax.optimization_barrier((chunk, both))
+        scal = jnp.stack([place, chunk, core]).astype(jnp.int32)
+        precise = d == sides
+        if d == 1:
+            *tables, away, keep = first_sums(lags, precise, scal, offsets, weights, wide, last, blocks, closing)
+        else:
+            away, keep = later_sums(lags, precise, scal, wide, last, tables)
         got = lax.ppermute(away, "comp", [(0, 1), (1, 0)])
         if d < sides:
-            both = (keep + got.astype(jnp.float32)).astype(jnp.bfloat16)
-            terms.append(lax.ppermute(both, "sta", [(i, (i + d) % sides) for i in range(sides)]))
-        else:
-            terms += [keep, got]
-    return finished(*terms)
+            both = (keep.astype(jnp.float32) + got.astype(jnp.float32)).astype(jnp.bfloat16)
+            gotten.append(lax.ppermute(both, "sta", [(i, (i + d) % sides) for i in range(sides)]))
+    total = keep
+    for term in gotten:
+        total = total + term.astype(jnp.float32)
+    if gotten:
+        total = lax.optimization_barrier(total)
+    return total + got.astype(jnp.float32)
 
 
 def solution(mesh):

time: 30.5 us -> 31.5 us (1.033)
  Pallas kernels: 11.3 us -> 18.9 us
  local copies, waits for them, and re-layouts: 6.56 us -> 0.01 us
  waiting for transfers between devices: 3.94 us -> 2.63 us
  other arithmetic: 0.11 us -> 0.95 us
  starting transfers between devices: 8.31 us -> 8.71 us
    pallas_call x5 -> x3, Pallas kernels: 11.3 us -> 18.9 us  [the longest x1 7.39 us: first_sums(): pl.pallas_call(functools.partial(first_kernel, len(blocks), lags, precise...]
    unnamed x16 -> x8, local copies, waits for them, and re-layouts: 6.56 us -> 0.01 us
    ppermute x1, waiting for transfers between devices: 3.93 us -> 0.01 us  [shards(): lax.ppermute(both, 'sta', [(i, (i + d) % sides) for i in range(sides)])]
    ppermute x2, waiting for transfers between devices: 0.01 us -> 2.62 us  [shards(): got = lax.ppermute(away, 'comp', [(0, 1), (1, 0)])]
    ppermute x3, starting transfers between devices: 6.12 us -> 7.02 us  [shards(): lax.ppermute(block, 'tmpl', [(i, (i - d) % owners) for i in range(owners)])]
    add x0 -> x2, other arithmetic: none -> 0.77 us  [the longest x1 0.73 us: shards(): return total + got.astype(jnp.float32)]
    ppermute x2, starting transfers between devices: 0.63 us -> 0.14 us  [shards(): got = lax.ppermute(away, 'comp', [(0, 1), (1, 0)])]
  transfers between devices with their start and end apart: 6 -> 6, of which waited for: 1 -> 2; matrix products, arithmetic and copies ran while one was open for 0% -> 1% of each run, Pallas kernels for 19% -> 37%
where the time goes in v2:
time: 31.5 us; the launch traced here: 31.3 us
  Pallas kernels  18.9 us (60%)
  starting transfers between devices  8.71 us (28%)
  waiting for transfers between devices  2.63 us (8%)
  other arithmetic  0.95 us (3%)
    pallas_call x1, Pallas kernels, first_sums(): pl.pallas_call(functools.partial(first_kernel, len(blocks), lags, precise...  7.39 us
    ppermute x3, starting transfers between devices, shards(): lax.ppermute(block, 'tmpl', [(i, (i - d) % owners) for i in range(owners)])  7.02 us
    pallas_call x1, Pallas kernels, later_sums(): pl.pallas_call(functools.partial(later_kernel, lags, precise), out_shape=...  6.05 us
    pallas_call x1, Pallas kernels, templates_prepared(): pl.pallas_call(template_kernel, out_shape=(pltpu.HBM(wide, jnp.bfloat16),...  5.5 us
    ppermute x2, waiting for transfers between devices, shards(): got = lax.ppermute(away, 'comp', [(0, 1), (1, 0)])  2.62 us
    ppermute x1, starting transfers between devices, shards(): lax.ppermute(both, 'sta', [(i, (i + d) % sides) for i in range(sides)])  1.54 us
    add x1, other arithmetic, shards(): return total + got.astype(jnp.float32)  0.73 us
  transfers between devices with their start and end apart: 6, of which 2 were waited for; matrix products, arithmetic and copies ran while one was open for 1% of the time, Pallas kernels for 37%

profile of v2, /device:TPU:0, one launch (start us, length us, event | category | flops | bytes accessed | tf_op | source)
XLA Modules:
  0.0 31.3 jit_solution(12685209940833773929)
XLA Ops:
  0.0 0.0 copy-start
  0.0 0.0 copy-start.3
  0.0 0.0 copy-start.2
  0.0 0.0 copy-start.1
  0.0 3.1 %collective-permute-start.2 = (bf16[3,8,512]{2,1,0:T(8,128)(2,1)}, bf16[3,8,512]{2,1,0:T(8,128)(2,1)S(1)}, u32[]{:S(2)}, u32[]{:S(2)}) collective-permute-start(bf16[3,8,512]{2,1,0:T(8,128)(2,1)} %bitcast.8), channel_id=1, source_target_pairs={{0,4},{4,8},{8,12},{12,0},{1,5},{5,9},{9,13},{13,1},{2,6},{6,10},{... | collective-permute-start | bytes 73736 | tf_op jit(solution)/shard_map/ppermute | solution.py:357
  3.1 2.6 %collective-permute-start.1 = (bf16[3,8,512]{2,1,0:T(8,128)(2,1)}, bf16[3,8,512]{2,1,0:T(8,128)(2,1)S(1)}, u32[]{:S(2)}, u32[]{:S(2)}) collective-permute-start(bf16[3,8,512]{2,1,0:T(8,128)(2,1)} %bitcast.9), channel_id=1, source_target_pairs={{0,8},{4,12},{8,0},{12,4},{1,9},{5,13},{9,1},{13,5},{2,10},{6,14},... | collective-permute-start | bytes 73736 | tf_op jit(solution)/shard_map/ppermute | solution.py:357
  5.7 1.3 %collective-permute-start = (bf16[3,8,512]{2,1,0:T(8,128)(2,1)}, bf16[3,8,512]{2,1,0:T(8,128)(2,1)S(1)}, u32[]{:S(2)}, u32[]{:S(2)}) collective-permute-start(bf16[3,8,512]{2,1,0:T(8,128)(2,1)} %bitcast.10), channel_id=1, source_target_pairs={{0,12},{4,0},{8,4},{12,8},{1,13},{5,1},{9,5},{13,9},{2,14},{6,2},{... | collective-permute-start | bytes 73736 | tf_op jit(solution)/shard_map/ppermute | solution.py:357
  7.0 5.5 %templates.1 = (bf16[24,128,768]{2,1,0:T(8,128)(2,1)}, bf16[128,128]{1,0:T(8,128)(2,1)S(1)}) custom-call(bf16[128,3,8,256]{3,2,1,0:T(8,128)(2,1)} %bitcast.13, s32[8,128]{1,0:T(8,128)} %bitcast.14), custom_call_target="tpu_custom_call" | custom-call | flops 2000000000 | bytes 8000000 | tf_op jit(solution)/shard_map/templates/pallas_call | solution.py:101
  12.5 0.1 add_add_fusion.scal_ref
  12.6 0.0 collective-permute-done.2.refs_3_
  12.6 0.0 collective-permute-done.1.refs_2_
  12.6 0.0 collective-permute-done.refs_1_
  12.6 0.0 copy-done
  12.6 0.0 copy-done.3
  12.7 0.0 copy-done.2
  12.7 0.0 copy-done.1
  12.7 7.4 %records_chunk.1 = (f32[4,24,640]{2,1,0:T(8,128)S(1)}, f32[3,24,640]{2,1,0:T(8,128)S(1)}, f32[4,24,640]{2,1,0:T(8,128)S(1)}, bf16[128,512]{1,0:T(8,128)(2,1)S(1)}, bf16[128,512]{1,0:T(8,128)(2,1)S(1)}) custom-call(s32[3]{0:T(128)S(1)} %add_add_fusion.scal_ref, s32[8]{0:T(128)S(1)} %copy-done.2, s32[8]{0:T(128)S(1)} %copy-done.3, ...), custom_call_target="tpu_custom_call" | custom-call | flops 1610612736 | bytes 8000000 | tf_op jit(solution)/shard_map/records_chunk/pallas_call | solution.py:321
  20.1 0.1 collective-permute-start.3
  20.2 1.3 %collective-permute-done.3 = bf16[128,512]{1,0:T(8,128)(2,1)S(1)} collective-permute-done((bf16[128,512]{1,0:T(8,128)(2,1)S(1)}, bf16[128,512]{1,0:T(8,128)(2,1)S(1)}, u32[]{:S(2)}, u32[]{:S(2)}) %collective-permute-start.3) | collective-permute-done | bytes 131104 | tf_op jit(solution)/shard_map/ppermute | solution.py:375
  21.5 1.5 %collective-permute-start.4 = (bf16[128,512]{1,0:T(8,128)(2,1)S(1)}, bf16[128,512]{1,0:T(8,128)(2,1)S(1)}, u32[]{:S(2)}, u32[]{:S(2)}) collective-permute-start(bf16[128,512]{1,0:T(8,128)(2,1)S(1)} %add_convert_fusion), channel_id=1, source_target_pairs={{0,2},{2,0},{1,3},{3,1},{4,6},{6,4},{5,7},{7,5},{8,10},{10,8},{9,1... | collective-permute-start | bytes 393224 | tf_op jit(solution)/shard_map/ppermute | solution.py:378
  23.1 0.1 add_add_fusion.1.scal_ref
  23.1 6.1 %chunk.1 = (bf16[128,512]{1,0:T(8,128)(2,1)S(1)}, f32[128,512]{1,0:T(8,128)S(1)}) custom-call(s32[3]{0:T(128)S(1)} %add_add_fusion.1.scal_ref, bf16[24,128,768]{2,1,0:T(8,128)(2,1)} %get-tuple-element.15.wide_ref, bf16[128,128]{1,0:T(8,128)(2,1)S(1)} %get-tuple-element.16.last_ref, f32[4,24,640]{2,1,0:T(8,128)S(1)} %get-tuple-element.20.phases_ref, ...), custom_call_target="tpu_custom_call" | custom-call | flops 1610612736 | bytes 8000000 | tf_op jit(solution)/shard_map/chunk/pallas_call | solution.py:334
  29.2 0.1 collective-permute-start.5
  29.3 0.0 collective-permute-done.4
  29.3 1.3 %collective-permute-done.5 = bf16[128,512]{1,0:T(8,128)(2,1)S(1)} collective-permute-done((bf16[128,512]{1,0:T(8,128)(2,1)S(1)}, bf16[128,512]{1,0:T(8,128)(2,1)S(1)}, u32[]{:S(2)}, u32[]{:S(2)}) %collective-permute-start.5) | collective-permute-done | bytes 131104 | tf_op jit(solution)/shard_map/ppermute | solution.py:375
  30.6 0.7 %convert_add_fusion = f32[128,512]{1,0:T(8,128)} fusion(f32[128,512]{1,0:T(8,128)S(1)} %convert_add_fusion.1, bf16[128,512]{1,0:T(8,128)(2,1)S(1)} %collective-permute-done.5), kind=kLoop, calls=%fused_computation | loop fusion | flops 131072 | bytes 655360 | tf_op jit(solution)/shard_map/add | solution.py:384
  (2 shorter events, 0.1 us)
Async XLA Ops:
  0.0 12.6 %copy-start = (bf16[8,3,512]{2,0,1:T(8,128)(2,1)S(1)}, bf16[8,3,512]{2,0,1:T(8,128)(2,1)}, u32[]{:S(2)}) copy-start(bf16[8,3,512]{2,0,1:T(8,128)(2,1)} %param.7) | copy-start | bytes 73732
  0.0 12.6 %copy-start.3 = (s32[8]{0:T(128)S(1)}, s32[8]{0:T(128)}, u32[]{:S(2)}) copy-start(s32[8]{0:T(128)} %weights_ref.1) | copy-start | bytes 100
  0.0 12.7 %copy-start.2 = (s32[8]{0:T(128)S(1)}, s32[8]{0:T(128)}, u32[]{:S(2)}) copy-start(s32[8]{0:T(128)} %offsets_ref.1) | copy-start | bytes 100
  0.0 12.7 %copy-start.1 = (bf16[8,3,512]{2,0,1:T(8,128)(2,1)S(1)}, bf16[8,3,512]{2,0,1:T(8,128)(2,1)}, u32[]{:S(2)}) copy-start(bf16[8,3,512]{2,0,1:T(8,128)(2,1)} %param.8) | copy-start | bytes 73732
  0.0 12.6 %collective-permute-start.2 = (bf16[3,8,512]{2,1,0:T(8,128)(2,1)}, bf16[3,8,512]{2,1,0:T(8,128)(2,1)S(1)}, u32[]{:S(2)}, u32[]{:S(2)}) collective-permute-start(bf16[3,8,512]{2,1,0:T(8,128)(2,1)} %bitcast.8), channel_id=1, source_target_pairs={{0,4},{4,8},{8,12},{12,0},{1,5},{5,9},{9,13},{13,1},{2,6},{6,10},{... | collective-permute-start | bytes 73736 | tf_op jit(solution)/shard_map/ppermute | solution.py:357
  3.1 9.5 %collective-permute-start.1 = (bf16[3,8,512]{2,1,0:T(8,128)(2,1)}, bf16[3,8,512]{2,1,0:T(8,128)(2,1)S(1)}, u32[]{:S(2)}, u32[]{:S(2)}) collective-permute-start(bf16[3,8,512]{2,1,0:T(8,128)(2,1)} %bitcast.9), channel_id=1, source_target_pairs={{0,8},{4,12},{8,0},{12,4},{1,9},{5,13},{9,1},{13,5},{2,10},{6,14},... | collective-permute-start | bytes 73736 | tf_op jit(solution)/shard_map/ppermute | solution.py:357
  5.7 6.9 %collective-permute-start = (bf16[3,8,512]{2,1,0:T(8,128)(2,1)}, bf16[3,8,512]{2,1,0:T(8,128)(2,1)S(1)}, u32[]{:S(2)}, u32[]{:S(2)}) collective-permute-start(bf16[3,8,512]{2,1,0:T(8,128)(2,1)} %bitcast.10), channel_id=1, source_target_pairs={{0,12},{4,0},{8,4},{12,8},{1,13},{5,1},{9,5},{13,9},{2,14},{6,2},{... | collective-permute-start | bytes 73736 | tf_op jit(solution)/shard_map/ppermute | solution.py:357
  20.1 1.4 %collective-permute-start.3 = (bf16[128,512]{1,0:T(8,128)(2,1)S(1)}, bf16[128,512]{1,0:T(8,128)(2,1)S(1)}, u32[]{:S(2)}, u32[]{:S(2)}) collective-permute-start(bf16[128,512]{1,0:T(8,128)(2,1)S(1)} %get-tuple-element.18), channel_id=1, source_target_pairs={{0,1},{1,0},{2,3},{3,2},{4,5},{5,4},{6,7},{7,6},{8,9},{9,8},{10,11... | collective-permute-start | bytes 393224 | tf_op jit(solution)/shard_map/ppermute | solution.py:375
  21.5 7.8 %collective-permute-start.4 = (bf16[128,512]{1,0:T(8,128)(2,1)S(1)}, bf16[128,512]{1,0:T(8,128)(2,1)S(1)}, u32[]{:S(2)}, u32[]{:S(2)}) collective-permute-start(bf16[128,512]{1,0:T(8,128)(2,1)S(1)} %add_convert_fusion), channel_id=1, source_target_pairs={{0,2},{2,0},{1,3},{3,1},{4,6},{6,4},{5,7},{7,5},{8,10},{10,8},{9,1... | collective-permute-start | bytes 393224 | tf_op jit(solution)/shard_map/ppermute | solution.py:378
  29.2 1.4 %collective-permute-start.5 = (bf16[128,512]{1,0:T(8,128)(2,1)S(1)}, bf16[128,512]{1,0:T(8,128)(2,1)S(1)}, u32[]{:S(2)}, u32[]{:S(2)}) collective-permute-start(bf16[128,512]{1,0:T(8,128)(2,1)S(1)} %get-tuple-element.24), channel_id=1, source_target_pairs={{0,1},{1,0},{2,3},{3,2},{4,5},{5,4},{6,7},{7,6},{8,9},{9,8},{10,11... | collective-permute-start | bytes 393224 | tf_op jit(solution)/shard_map/ppermute | solution.py:375

commit v3 on v2

--- a/solution.py
+++ b/solution.py
@@ -8,7 +8,6 @@
 from jax.sharding import PartitionSpec as P
 
 EPS = 1e-05
-BATCH = 3
 S = 4
 LANES = 128
 VMEM = pl.BlockSpec(memory_space=pltpu.VMEM)
@@ -22,7 +21,7 @@
     return lax.broadcasted_iota(jnp.int32, shape, axis)
 
 
-def template_kernel(source_ref, mask_ref, wide_ref, last_ref, x_ref, unit_ref, rows_ref, held_ref, flag_ref, arrived, sent):
+def template_kernel(source_ref, mask_ref, wide_ref, last_ref, x_ref, unit_ref, rows_ref, flag_ref, arrived):
     count, comps, stations, length = x_ref.shape
     pairs = comps * stations
     group = 8
@@ -67,14 +66,13 @@
         base = jnp.where(first, low[0] - S * low[1], high[0] - S * high[1])
         wanted.append(jnp.where(sample == S * (group_rows - 1 - place) + base, 1.0, 0.0).astype(jnp.bfloat16))
     batch = 8
-    leaving = []
     for at in range(0, pairs, batch):
         span = rows_ref[at * count : (at + batch) * count, :]
         for v in range(0, len(PIECES), 2):
             moved = jnp.dot(span, jnp.concatenate(wanted[v : v + 2], axis=1), preferred_element_type=jnp.float32)
             for i in range(batch):
                 part = moved[i * count : (i + 1) * count]
-                held_ref[at + i, :, LANES * v : LANES * v + 2 * LANES] = part.astype(jnp.bfloat16)
+                wide_ref[at + i, :, LANES * v : LANES * v + 2 * LANES] = part.astype(jnp.bfloat16)
                 pair = at + i
                 if v == 0:
                     turned = pltpu.roll(part[:, LANES:], (pair - 32) % LANES, axis=1)
@@ -82,12 +80,7 @@
                 if v == 4:
                     turned = pltpu.roll(part[:, :LANES], pair, axis=1)
                     last = jnp.where((lane_row == pair) | (lane_row == 64 + pair), turned, last)
-        copy = pltpu.make_async_copy(held_ref.at[at : at + batch], wide_ref.at[at : at + batch], sent.at[at // batch])
-        copy.start()
-        leaving.append(copy)
     last_ref[...] = last.astype(jnp.bfloat16)
-    for copy in leaving:
-        copy.wait()
 
 
 def in_hbm(x):
@@ -100,19 +93,17 @@
     wide = (pairs, count, LANES * len(PIECES))
     wide, last = pl.pallas_call(
         template_kernel,
-        out_shape=(pltpu.HBM(wide, jnp.bfloat16), jax.ShapeDtypeStruct((count, LANES), jnp.bfloat16)),
+        out_shape=(jax.ShapeDtypeStruct(wide, jnp.bfloat16), jax.ShapeDtypeStruct((count, LANES), jnp.bfloat16)),
         in_specs=[HBM, HBM],
-        out_specs=(HBM, VMEM),
+        out_specs=(VMEM, VMEM),
         scratch_shapes=[
             pltpu.VMEM((count, comps, stations, length), jnp.bfloat16),
             pltpu.VMEM((length // LANES, pairs * count, LANES), jnp.float32),
             pltpu.VMEM((pairs * count, length), jnp.bfloat16),
-            pltpu.VMEM(wide, jnp.bfloat16),
             pltpu.VMEM((stations, count), jnp.int32),
             pltpu.SemaphoreType.DMA((5,)),
-            pltpu.SemaphoreType.DMA((pairs // 8,)),
         ],
-        compiler_params=pltpu.CompilerParams(vmem_limit_bytes=24 << 20),
+        compiler_params=pltpu.CompilerParams(vmem_limit_bytes=16 << 20),
         cost_estimate=pl.CostEstimate(flops=2 * 10**9, bytes_accessed=8 * 10**6, transcendentals=0),
         name="templates",
     )(in_hbm(jnp.transpose(templates, (0, 2, 1, 3))), in_hbm(jnp.transpose(mask)))
@@ -183,7 +174,7 @@
             phases_ref[r, at : at + stations, :] = v[r]
 
 
-def chunk_sum(lags, precise, chunk, mine, arrivals, wide_ref, last_ref, phases_ref, ahead_ref, factor_ref, away_ref, keep_ref, sum_ref):
+def chunk_sum(lags, precise, chunk, mine, wide_ref, last_ref, phases_ref, ahead_ref, factor_ref, away_ref, keep_ref, sum_ref):
     pairs, count, _ = wide_ref.shape
     group_rows = 64
     half = lags // S // 2
@@ -213,8 +204,6 @@
             else:
                 extra.append(None)
         for pair in range(pairs):
-            if n == 0 and pair % BATCH == 0:
-                arrivals[pair // BATCH].wait()
             rows = []
             for p in range(S):
                 line = [
@@ -267,30 +256,18 @@
     keep_ref[...] = kept + moved[2 * count :] if precise else kept.astype(jnp.bfloat16)
 
 
-def arriving(wide_ref, held_ref, arrived):
-    copies = [
-        pltpu.make_async_copy(wide_ref.at[at : at + BATCH], held_ref.at[at : at + BATCH], arrived.at[at // BATCH])
-        for at in range(0, wide_ref.shape[0], BATCH)
-    ]
-    for copy in copies:
-        copy.start()
-    return copies
-
-
-def first_kernel(blocks, lags, precise, scal_ref, offsets_ref, weights_ref, wide_ref, last_ref, *refs):
+def first_kernel(blocks, lags, precise, step, sides, scal_ref, offsets_ref, weights_ref, wide_ref, last_ref, *refs):
     block_refs = refs[: blocks + 1]
-    phases_ref, ahead_ref, factor_ref, away_ref, keep_ref, raw_ref, held_ref, sum_ref, arrived = refs[blocks + 1 :]
-    copies = arriving(wide_ref, held_ref, arrived)
+    phases_ref, ahead_ref, factor_ref, away_ref, keep_ref, raw_ref, sum_ref = refs[blocks + 1 :]
     records(scal_ref, offsets_ref, weights_ref, block_refs, phases_ref, ahead_ref, factor_ref, raw_ref)
     chunk_sum(
-        lags, precise, scal_ref[1], scal_ref[2], copies, held_ref, last_ref, phases_ref, ahead_ref, factor_ref, away_ref, keep_ref, sum_ref
-    )
-
-
-def later_kernel(lags, precise, scal_ref, wide_ref, last_ref, phases_ref, ahead_ref, factor_ref, away_ref, keep_ref, held_ref, sum_ref, arrived):
-    copies = arriving(wide_ref, held_ref, arrived)
+        lags, precise, lax.rem(scal_ref[1] + step, sides), scal_ref[2], wide_ref, last_ref, phases_ref, ahead_ref, factor_ref, away_ref, keep_ref, sum_ref
+    )
+
+
+def later_kernel(lags, precise, step, sides, scal_ref, wide_ref, last_ref, phases_ref, ahead_ref, factor_ref, away_ref, keep_ref, sum_ref):
     chunk_sum(
-        lags, precise, scal_ref[1], scal_ref[2], copies, held_ref, last_ref, phases_ref, ahead_ref, factor_ref, away_ref, keep_ref, sum_ref
+        lags, precise, lax.rem(scal_ref[1] + step, sides), scal_ref[2], wide_ref, last_ref, phases_ref, ahead_ref, factor_ref, away_ref, keep_ref, sum_ref
     )
 
 
@@ -301,45 +278,43 @@
         jax.ShapeDtypeStruct((count, lags // 2), jnp.float32 if precise else jnp.bfloat16),
     )
     scratch = [
-        pltpu.VMEM((pairs, count, columns), jnp.bfloat16),
         pltpu.VMEM((S * count, lags // S), jnp.float32),
-        pltpu.SemaphoreType.DMA((pairs // BATCH,)),
     ]
     params = dict(
-        compiler_params=pltpu.CompilerParams(vmem_limit_bytes=24 << 20),
+        compiler_params=pltpu.CompilerParams(vmem_limit_bytes=16 << 20),
         cost_estimate=pl.CostEstimate(flops=2 * count * pairs * 256 * lags, bytes_accessed=8 * 10**6, transcendentals=0),
     )
     return shapes, scratch, params
 
 
-def first_sums(lags, precise, scal, offsets, weights, wide, last, blocks, tail):
+def first_sums(lags, precise, step, sides, scal, offsets, weights, wide, last, blocks, tail):
     comps, stations, width = blocks[0].shape
     pairs = comps * stations
     parts = (len(blocks) * width + tail.shape[-1]) // (S * LANES)
     full = parts * LANES
     shapes, scratch, params = sums_of(lags, precise, wide)
     return pl.pallas_call(
-        functools.partial(first_kernel, len(blocks), lags, precise),
+        functools.partial(first_kernel, len(blocks), lags, precise, step, sides),
         out_shape=tuple(jax.ShapeDtypeStruct((n, pairs, full), jnp.float32) for n in (S, S - 1, S)) + shapes,
-        in_specs=[SMEM, SMEM, SMEM, HBM, VMEM] + [VMEM] * (len(blocks) + 1),
+        in_specs=[SMEM, SMEM, SMEM, VMEM, VMEM] + [VMEM] * (len(blocks) + 1),
         out_specs=(VMEM,) * 5,
         scratch_shapes=[pltpu.VMEM((parts, pairs, S * LANES), jnp.float32)] + scratch,
         name="records_chunk",
         **params,
-    )(scal, offsets, weights, in_hbm(wide), last, *blocks, tail)
-
-
-def later_sums(lags, precise, scal, wide, last, tables):
+    )(scal, offsets, weights, wide, last, *blocks, tail)
+
+
+def later_sums(lags, precise, step, sides, scal, wide, last, tables):
     shapes, scratch, params = sums_of(lags, precise, wide)
     return pl.pallas_call(
-        functools.partial(later_kernel, lags, precise),
+        functools.partial(later_kernel, lags, precise, step, sides),
         out_shape=shapes,
-        in_specs=[SMEM, HBM] + [VMEM] * 4,
+        in_specs=[SMEM, VMEM] + [VMEM] * 4,
         out_specs=(VMEM, VMEM),
         scratch_shapes=scratch,
         name="chunk",
         **params,
-    )(scal, in_hbm(wide), last, *tables)
+    )(scal, wide, last, *tables)
 
 
 def shards(templates, data, tail, offsets, weights, mask):
@@ -361,17 +336,14 @@
         blocks = [lax.dynamic_index_in_dim(gathered, lax.rem(place + d, owners), 0, False) for d in range(owners)]
     wide, last = templates_prepared(templates, mask)
     gotten = []
-    both = None
+    scal = jnp.stack([place, side, core]).astype(jnp.int32)
     for d in range(1, sides + 1):
-        chunk = lax.rem(side + d, sides)
-        if both is not None:
-            chunk, _ = lax.optimization_barrier((chunk, both))
-        scal = jnp.stack([place, chunk, core]).astype(jnp.int32)
         precise = d == sides
         if d == 1:
-            *tables, away, keep = first_sums(lags, precise, scal, offsets, weights, wide, last, blocks, closing)
+            *tables, away, keep = first_sums(lags, precise, d, sides, scal, offsets, weights, wide, last, blocks, closing)
         else:
-            away, keep = later_sums(lags, precise, scal, wide, last, tables)
+            scal, _ = lax.optimization_barrier((scal, both))
+            away, keep = later_sums(lags, precise, d, sides, scal, wide, last, tables)
         got = lax.ppermute(away, "comp", [(0, 1), (1, 0)])
         if d < sides:
             both = (keep.astype(jnp.float32) + got.astype(jnp.float32)).astype(jnp.bfloat16)

time: 31.5 us -> 24 us (0.76)
  Pallas kernels: 18.9 us -> 11.5 us
    pallas_call x2, Pallas kernels: 11.6 us -> 7.08 us  [the longest x1 4.15 us: templates_prepared(): pl.pallas_call(template_kernel, out_shape=(jax.ShapeDtypeStruct(wide, jnp...]
    pallas_call x1, Pallas kernels: 7.39 us -> 4.42 us  [first_sums(): pl.pallas_call(functools.partial(first_kernel, len(blocks), lags, precise...]
    ppermute x1, waiting for transfers between devices: 0.01 us -> 1.05 us  [shards(): lax.ppermute(both, 'sta', [(i, (i + d) % sides) for i in range(sides)])]
    ppermute x2, waiting for transfers between devices: 2.62 us -> 1.58 us  [shards(): got = lax.ppermute(away, 'comp', [(0, 1), (1, 0)])]
  transfers between devices with their start and end apart: 6 -> 6, of which waited for: 2 -> 3; matrix products, arithmetic and copies ran while one was open for 1% -> 0% of each run, Pallas kernels for 37% -> 30%
where the time goes in v3:
time: 24 us; the launch traced here: 23.8 us
  Pallas kernels  11.5 us (48%)
  starting transfers between devices  8.71 us (36%)
  waiting for transfers between devices  2.64 us (11%)
  other arithmetic  0.88 us (4%)
    ppermute x3, starting transfers between devices, shards(): lax.ppermute(block, 'tmpl', [(i, (i - d) % owners) for i in range(owners)])  7.02 us
    pallas_call x1, Pallas kernels, first_sums(): pl.pallas_call(functools.partial(first_kernel, len(blocks), lags, precise...  4.42 us
    pallas_call x1, Pallas kernels, templates_prepared(): pl.pallas_call(template_kernel, out_shape=(jax.ShapeDtypeStruct(wide, jnp...  4.15 us
    pallas_call x1, Pallas kernels, later_sums(): pl.pallas_call(functools.partial(later_kernel, lags, precise, step, sides...  2.93 us
    ppermute x2, waiting for transfers between devices, shards(): got = lax.ppermute(away, 'comp', [(0, 1), (1, 0)])  1.58 us
    ppermute x1, starting transfers between devices, shards(): lax.ppermute(both, 'sta', [(i, (i + d) % sides) for i in range(sides)])  1.55 us
    ppermute x1, waiting for transfers between devices, shards(): lax.ppermute(both, 'sta', [(i, (i + d) % sides) for i in range(sides)])  1.05 us
    add x1, other arithmetic, shards(): return total + got.astype(jnp.float32)  0.74 us
  transfers between devices with their start and end apart: 6, of which 3 were waited for; matrix products, arithmetic and copies ran while one was open for 0% of the time, Pallas kernels for 30%

profile of v3, /device:TPU:0, one launch (start us, length us, event | category | flops | bytes accessed | tf_op | source)
XLA Modules:
  0.0 23.8 jit_solution(12255551379518662416)
XLA Ops:
  0.0 0.0 copy-start
  0.0 0.0 copy-start.3
  0.0 0.0 copy-start.2
  0.0 0.0 copy-start.1
  0.0 3.1 %collective-permute-start.2 = (bf16[3,8,512]{2,1,0:T(8,128)(2,1)}, bf16[3,8,512]{2,1,0:T(8,128)(2,1)S(1)}, u32[]{:S(2)}, u32[]{:S(2)}) collective-permute-start(bf16[3,8,512]{2,1,0:T(8,128)(2,1)} %bitcast.7), channel_id=1, source_target_pairs={{0,4},{4,8},{8,12},{12,0},{1,5},{5,9},{9,13},{13,1},{2,6},{6,10},{... | collective-permute-start | bytes 73736 | tf_op jit(solution)/shard_map/ppermute | solution.py:332
  3.1 2.6 %collective-permute-start.1 = (bf16[3,8,512]{2,1,0:T(8,128)(2,1)}, bf16[3,8,512]{2,1,0:T(8,128)(2,1)S(1)}, u32[]{:S(2)}, u32[]{:S(2)}) collective-permute-start(bf16[3,8,512]{2,1,0:T(8,128)(2,1)} %bitcast.8), channel_id=1, source_target_pairs={{0,8},{4,12},{8,0},{12,4},{1,9},{5,13},{9,1},{13,5},{2,10},{6,14},... | collective-permute-start | bytes 73736 | tf_op jit(solution)/shard_map/ppermute | solution.py:332
  5.7 1.3 %collective-permute-start = (bf16[3,8,512]{2,1,0:T(8,128)(2,1)}, bf16[3,8,512]{2,1,0:T(8,128)(2,1)S(1)}, u32[]{:S(2)}, u32[]{:S(2)}) collective-permute-start(bf16[3,8,512]{2,1,0:T(8,128)(2,1)} %bitcast.9), channel_id=1, source_target_pairs={{0,12},{4,0},{8,4},{12,8},{1,13},{5,1},{9,5},{13,9},{2,14},{6,2},{... | collective-permute-start | bytes 73736 | tf_op jit(solution)/shard_map/ppermute | solution.py:332
  7.0 4.2 %templates.1 = (bf16[24,128,768]{2,1,0:T(8,128)(2,1)S(1)}, bf16[128,128]{1,0:T(8,128)(2,1)S(1)}) custom-call(bf16[128,3,8,256]{3,2,1,0:T(8,128)(2,1)} %bitcast.12, s32[8,128]{1,0:T(8,128)} %bitcast.13), custom_call_target="tpu_custom_call" | custom-call | flops 2000000000 | bytes 8000000 | tf_op jit(solution)/shard_map/templates/pallas_call | solution.py:94
  11.2 0.1 pad_add_fusion.scal_ref
  11.3 0.0 collective-permute-done.2.refs_3_
  11.3 0.0 collective-permute-done.1.refs_2_
  11.3 0.0 collective-permute-done.refs_1_
  11.3 0.0 copy-done
  11.3 0.0 copy-done.3
  11.3 0.0 copy-done.2
  11.3 0.0 copy-done.1
  11.3 4.4 %records_chunk.1 = (f32[4,24,640]{2,1,0:T(8,128)S(1)}, f32[3,24,640]{2,1,0:T(8,128)S(1)}, f32[4,24,640]{2,1,0:T(8,128)S(1)}, bf16[128,512]{1,0:T(8,128)(2,1)S(1)}, bf16[128,512]{1,0:T(8,128)(2,1)S(1)}) custom-call(s32[3]{0:T(128)S(1)} %pad_add_fusion.scal_ref, s32[8]{0:T(128)S(1)} %copy-done.2, s32[8]{0:T(128)S(1)} %copy-done.3, ...), custom_call_target="tpu_custom_call" | custom-call | flops 1610612736 | bytes 8000000 | tf_op jit(solution)/shard_map/records_chunk/pallas_call | solution.py:296
  15.8 0.1 collective-permute-start.3
  15.8 1.3 %collective-permute-done.3 = bf16[128,512]{1,0:T(8,128)(2,1)S(1)} collective-permute-done((bf16[128,512]{1,0:T(8,128)(2,1)S(1)}, bf16[128,512]{1,0:T(8,128)(2,1)S(1)}, u32[]{:S(2)}, u32[]{:S(2)}) %collective-permute-start.3) | collective-permute-done | bytes 131104 | tf_op jit(solution)/shard_map/ppermute | solution.py:347
  17.2 1.5 %collective-permute-start.4 = (bf16[128,512]{1,0:T(8,128)(2,1)S(1)}, bf16[128,512]{1,0:T(8,128)(2,1)S(1)}, u32[]{:S(2)}, u32[]{:S(2)}) collective-permute-start(bf16[128,512]{1,0:T(8,128)(2,1)S(1)} %add_convert_fusion), channel_id=1, source_target_pairs={{0,2},{2,0},{1,3},{3,1},{4,6},{6,4},{5,7},{7,5},{8,10},{10,8},{9,1... | collective-permute-start | bytes 393224 | tf_op jit(solution)/shard_map/ppermute | solution.py:350
  18.8 2.9 %chunk.1 = (bf16[128,512]{1,0:T(8,128)(2,1)S(1)}, f32[128,512]{1,0:T(8,128)S(1)}) custom-call(s32[3]{0:T(128)S(1)} %pad_add_fusion.scal_ref, bf16[24,128,768]{2,1,0:T(8,128)(2,1)S(1)} %get-tuple-element.15.wide_ref, bf16[128,128]{1,0:T(8,128)(2,1)S(1)} %get-tuple-element.16.last_ref, f32[4,24,640]{2,1,0:T(8,128)S(1)} %get-tuple-element.20.phases_ref, ...), custom_call_target="tpu_custom_call" | custom-call | flops 1610612736 | bytes 8000000 | tf_op jit(solution)/shard_map/chunk/pallas_call | solution.py:309
  21.7 0.1 collective-permute-start.5
  21.8 1.1 %collective-permute-done.4 = bf16[128,512]{1,0:T(8,128)(2,1)S(1)} collective-permute-done((bf16[128,512]{1,0:T(8,128)(2,1)S(1)}, bf16[128,512]{1,0:T(8,128)(2,1)S(1)}, u32[]{:S(2)}, u32[]{:S(2)}) %collective-permute-start.4) | collective-permute-done | bytes 131104 | tf_op jit(solution)/shard_map/ppermute | solution.py:350
  22.9 0.2 %collective-permute-done.5 = bf16[128,512]{1,0:T(8,128)(2,1)S(1)} collective-permute-done((bf16[128,512]{1,0:T(8,128)(2,1)S(1)}, bf16[128,512]{1,0:T(8,128)(2,1)S(1)}, u32[]{:S(2)}, u32[]{:S(2)}) %collective-permute-start.5) | collective-permute-done | bytes 131104 | tf_op jit(solution)/shard_map/ppermute | solution.py:347
  23.1 0.7 %convert_add_fusion = f32[128,512]{1,0:T(8,128)} fusion(f32[128,512]{1,0:T(8,128)S(1)} %convert_add_fusion.1, bf16[128,512]{1,0:T(8,128)(2,1)S(1)} %collective-permute-done.5), kind=kLoop, calls=%fused_computation | loop fusion | flops 131072 | bytes 655360 | tf_op jit(solution)/shard_map/add | solution.py:356
  (2 shorter events, 0.1 us)
Async XLA Ops:
  0.0 11.3 %copy-start = (bf16[8,3,512]{2,0,1:T(8,128)(2,1)S(1)}, bf16[8,3,512]{2,0,1:T(8,128)(2,1)}, u32[]{:S(2)}) copy-start(bf16[8,3,512]{2,0,1:T(8,128)(2,1)} %param.7) | copy-start | bytes 73732
  0.0 11.3 %copy-start.3 = (s32[8]{0:T(128)S(1)}, s32[8]{0:T(128)}, u32[]{:S(2)}) copy-start(s32[8]{0:T(128)} %weights_ref.1) | copy-start | bytes 100
  0.0 11.3 %copy-start.2 = (s32[8]{0:T(128)S(1)}, s32[8]{0:T(128)}, u32[]{:S(2)}) copy-start(s32[8]{0:T(128)} %offsets_ref.1) | copy-start | bytes 100
  0.0 11.3 %copy-start.1 = (bf16[8,3,512]{2,0,1:T(8,128)(2,1)S(1)}, bf16[8,3,512]{2,0,1:T(8,128)(2,1)}, u32[]{:S(2)}) copy-start(bf16[8,3,512]{2,0,1:T(8,128)(2,1)} %param.8) | copy-start | bytes 73732
  0.0 11.3 %collective-permute-start.2 = (bf16[3,8,512]{2,1,0:T(8,128)(2,1)}, bf16[3,8,512]{2,1,0:T(8,128)(2,1)S(1)}, u32[]{:S(2)}, u32[]{:S(2)}) collective-permute-start(bf16[3,8,512]{2,1,0:T(8,128)(2,1)} %bitcast.7), channel_id=1, source_target_pairs={{0,4},{4,8},{8,12},{12,0},{1,5},{5,9},{9,13},{13,1},{2,6},{6,10},{... | collective-permute-start | bytes 73736 | tf_op jit(solution)/shard_map/ppermute | solution.py:332
  3.1 8.2 %collective-permute-start.1 = (bf16[3,8,512]{2,1,0:T(8,128)(2,1)}, bf16[3,8,512]{2,1,0:T(8,128)(2,1)S(1)}, u32[]{:S(2)}, u32[]{:S(2)}) collective-permute-start(bf16[3,8,512]{2,1,0:T(8,128)(2,1)} %bitcast.8), channel_id=1, source_target_pairs={{0,8},{4,12},{8,0},{12,4},{1,9},{5,13},{9,1},{13,5},{2,10},{6,14},... | collective-permute-start | bytes 73736 | tf_op jit(solution)/shard_map/ppermute | solution.py:332
  5.7 5.6 %collective-permute-start = (bf16[3,8,512]{2,1,0:T(8,128)(2,1)}, bf16[3,8,512]{2,1,0:T(8,128)(2,1)S(1)}, u32[]{:S(2)}, u32[]{:S(2)}) collective-permute-start(bf16[3,8,512]{2,1,0:T(8,128)(2,1)} %bitcast.9), channel_id=1, source_target_pairs={{0,12},{4,0},{8,4},{12,8},{1,13},{5,1},{9,5},{13,9},{2,14},{6,2},{... | collective-permute-start | bytes 73736 | tf_op jit(solution)/shard_map/ppermute | solution.py:332
  15.8 1.4 %collective-permute-start.3 = (bf16[128,512]{1,0:T(8,128)(2,1)S(1)}, bf16[128,512]{1,0:T(8,128)(2,1)S(1)}, u32[]{:S(2)}, u32[]{:S(2)}) collective-permute-start(bf16[128,512]{1,0:T(8,128)(2,1)S(1)} %get-tuple-element.18), channel_id=1, source_target_pairs={{0,1},{1,0},{2,3},{3,2},{4,5},{5,4},{6,7},{7,6},{8,9},{9,8},{10,11... | collective-permute-start | bytes 393224 | tf_op jit(solution)/shard_map/ppermute | solution.py:347
  17.2 5.6 %collective-permute-start.4 = (bf16[128,512]{1,0:T(8,128)(2,1)S(1)}, bf16[128,512]{1,0:T(8,128)(2,1)S(1)}, u32[]{:S(2)}, u32[]{:S(2)}) collective-permute-start(bf16[128,512]{1,0:T(8,128)(2,1)S(1)} %add_convert_fusion), channel_id=1, source_target_pairs={{0,2},{2,0},{1,3},{3,1},{4,6},{6,4},{5,7},{7,5},{8,10},{10,8},{9,1... | collective-permute-start | bytes 393224 | tf_op jit(solution)/shard_map/ppermute | solution.py:350
  21.7 1.4 %collective-permute-start.5 = (bf16[128,512]{1,0:T(8,128)(2,1)S(1)}, bf16[128,512]{1,0:T(8,128)(2,1)S(1)}, u32[]{:S(2)}, u32[]{:S(2)}) collective-permute-start(bf16[128,512]{1,0:T(8,128)(2,1)S(1)} %get-tuple-element.24), channel_id=1, source_target_pairs={{0,1},{1,0},{2,3},{3,2},{4,5},{5,4},{6,7},{7,6},{8,9},{9,8},{10,11... | collective-permute-start | bytes 393224 | tf_op jit(solution)/shard_map/ppermute | solution.py:347

commit v4 on v0

v4 whole, which is shorter than its diff:
```python
import functools

import jax
import jax.numpy as jnp
from jax import lax
from jax.experimental import pallas as pl
from jax.experimental.pallas import tpu as pltpu
from jax.sharding import PartitionSpec as P

EPS = 1e-05
S = 2
LANES = 128
LENGTH = S * LANES
TILE = 2 * LANES
VMEM = pl.BlockSpec(memory_space=pltpu.VMEM)
SMEM = pl.BlockSpec(memory_space=pltpu.SMEM)
PHASE_PIECES = ((0, 1), (2, 0))


def iota(shape, axis):
    return lax.broadcasted_iota(jnp.int32, shape, axis)


def ones_where(condition):
    return jnp.where(condition, 1.0, 0.0).astype(jnp.bfloat16)


def later(x, by):
    return pltpu.roll(x, x.shape[-1] - by, axis=1)


def template_kernel(x_ref, mask_ref, order_ref, wide_ref, last_ref, unit_ref, rows_ref):
    count, comps, stations, length = x_ref.shape
    pairs = comps * stations
    group = min(8, count)
    lane = iota((count, LANES), 1)
    last = jnp.zeros((count, LANES), jnp.float32)
    available = jnp.transpose(mask_ref[...].astype(jnp.float32))
    for at in range(0, count, group):
        values = x_ref[at : at + group].astype(jnp.float32).reshape(group * pairs, length)
        centred = values - jnp.sum(values, axis=-1, keepdims=True) * (1.0 / length)
        spread = jnp.sum(centred * centred, axis=-1, keepdims=True) * (1.0 / length)
        unit = centred * lax.rsqrt(spread + EPS)
        for h in range(length // LANES):
            unit_ref[h, at * pairs : (at + group) * pairs, :] = unit[:, LANES * h : LANES * (h + 1)]
    for s in range(stations):
        column = available[:, s : s + 1]
        for c in range(comps):
            pair = c * stations + s
            rows = jnp.concatenate(
                [unit_ref[h, pl.ds(pair, count, stride=pairs), :] for h in range(length // LANES)], axis=1
            )
            rows_ref[pair * count : (pair + 1) * count, :] = (rows * column).astype(jnp.bfloat16)
    batch = 8
    for at in range(0, pairs, batch):
        moved = jnp.dot(rows_ref[at * count : (at + batch) * count, :], order_ref[...], preferred_element_type=jnp.float32)
        for i in range(batch):
            pair = at + i
            even = moved[i * count : (i + 1) * count, :LANES]
            odd = moved[i * count : (i + 1) * count, LANES:]
            wide_ref[pair, 0] = even.astype(jnp.bfloat16)
            wide_ref[pair, 1] = odd.astype(jnp.bfloat16)
            wide_ref[pair, 2] = jnp.where(lane == LANES - 1, 0.0, later(odd, 1)).astype(jnp.bfloat16)
            last = jnp.where(lane == pair, pltpu.roll(odd, pair, axis=1), last)
    last_ref[...] = last.astype(jnp.bfloat16)


def templates_prepared(templates, mask, order):
    count, stations, comps, length = templates.shape
    pairs = stations * comps
    return pl.pallas_call(
        template_kernel,
        out_shape=(
            jax.ShapeDtypeStruct((pairs, 3, count, LANES), jnp.bfloat16),
            jax.ShapeDtypeStruct((count, LANES), jnp.bfloat16),
        ),
        in_specs=[VMEM, VMEM, VMEM],
        out_specs=(VMEM, VMEM),
        scratch_shapes=[
            pltpu.VMEM((length // LANES, pairs * count, LANES), jnp.float32),
            pltpu.VMEM((pairs * count, length), jnp.bfloat16),
        ],
        compiler_params=pltpu.CompilerParams(vmem_limit_bytes=16 << 20),
        cost_estimate=pl.CostEstimate(flops=2 * 10**9, bytes_accessed=8 * 10**6, transcendentals=0),
        name="templates",
    )(jnp.transpose(templates, (0, 2, 1, 3)), jnp.transpose(mask), order)


def records(offsets_ref, weights_ref, split_ref, block_refs, phases_ref, factor_ref, raw_ref):
    blocks = len(block_refs) - 1
    comps, stations, width = block_refs[0].shape
    pairs = comps * stations
    unit = S * LANES
    per = width // unit
    for i in range(blocks + 1):
        values = block_refs[i][...].astype(jnp.float32).reshape(pairs, block_refs[i].shape[-1])
        home = blocks if i == blocks else lax.rem(lax.axis_index("tmpl") + i, blocks)
        for j in range(block_refs[i].shape[-1] // unit):
            raw_ref[home * per + j] = values[:, unit * j : unit * (j + 1)]
    parts = raw_ref.shape[0]
    flat = raw_ref[...].reshape(parts * pairs, unit).astype(jnp.bfloat16)
    split = jnp.dot(flat, split_ref[...], preferred_element_type=jnp.float32)
    full = parts * LANES
    row = iota((stations, full), 0)
    offset = jnp.zeros((stations, full), jnp.int32)
    weight = jnp.zeros((stations, full), jnp.float32)
    for s in range(stations):
        offset = jnp.where(row == s, offsets_ref[s], offset)
        weight = jnp.where(row == s, weights_ref[s].astype(jnp.float32), weight)
    for c in range(comps):
        at = c * stations
        v = [
            jnp.concatenate(
                [split[b * pairs + at : b * pairs + at + stations, LANES * p : LANES * (p + 1)] for b in range(parts)], axis=1
            )
            for p in range(S)
        ]
        step = 1
        while S * step < LENGTH:
            taken = (offset & (S * step)) != 0
            v = [jnp.where(taken, later(x, step), x) for x in v]
            step *= 2
        taken = (offset & 1) != 0
        v = [jnp.where(taken, v[1], v[0]), jnp.where(taken, later(v[0], 1), v[1])]
        mean = v[0] + v[1]
        power = v[0] * v[0] + v[1] * v[1]
        step = 1
        while step < LANES:
            mean = mean + later(mean, step)
            power = power + later(power, step)
            step *= 2
        ahead = later(v[0], LANES)
        for r in range(S):
            middle = mean * (1.0 / LENGTH)
            spread = power * (1.0 / LENGTH) - middle * middle
            factor_ref[r, at : at + stations, :] = weight / (LENGTH * jnp.sqrt(spread + EPS))
            phases_ref[r, at : at + stations, :] = v[r]
            mean = mean + (ahead - v[0])
            power = power + (ahead * ahead - v[0] * v[0])


def owner_sum(lags, precise, step, sides, away, restore_ref, wide_ref, last_ref, phases_ref, factor_ref, out_ref, sum_ref):
    pairs, _, count, _ = wide_ref.shape
    side, core = lax.rem(lax.axis_index("sta") + step, sides), lax.axis_index("comp")
    owner = 2 * side + (1 - core if away else core)
    lane = iota((8, LANES), 1)
    sub = iota((8, LANES), 0)
    width = lags // S
    for n in range(width // TILE):
        begin = pl.multiple_of(owner * width + n * TILE, LANES)
        extra = phases_ref[0, :, pl.ds(begin + LANES, TILE)] * factor_ref[1, :, pl.ds(begin, TILE)]
        extra = jnp.concatenate([extra, jnp.zeros((LANES - pairs, TILE), jnp.float32)], axis=0).astype(jnp.bfloat16)
        past = jnp.dot(last_ref[...], extra, preferred_element_type=jnp.float32)
        for pair in range(pairs):
            rows = []
            for p in range(S):
                line = [
                    jnp.broadcast_to(phases_ref[p, pair : pair + 1, pl.ds(begin + LANES * j, LANES)], (8, LANES))
                    for j in range(3)
                ]
                for g in range(0, LANES, 16):
                    sides_of = []
                    for j in range(2):
                        pieces = []
                        for h in (g, g + 8):
                            mixed = jnp.where(lane >= LANES - 1 - h - sub, line[j], line[j + 1])
                            pieces.append(pltpu.roll(mixed, 1 + h, axis=1, stride=1, stride_axis=0))
                        sides_of.append(jnp.concatenate(pieces, axis=0).astype(jnp.bfloat16))
                    rows.append(jnp.concatenate(sides_of, axis=1))
            table = jnp.concatenate(rows, axis=0)
            units = jnp.concatenate(
                [jnp.concatenate([wide_ref[pair, v] for v in PHASE_PIECES[r]], axis=1) for r in range(S)], axis=0
            )
            products = jnp.dot(units, table, preferred_element_type=jnp.float32)
            for r in range(S):
                scaled = products[r * count : (r + 1) * count] * factor_ref[r, pair : pair + 1, pl.ds(begin, TILE)]
                where = (slice(r * count, (r + 1) * count), slice(n * TILE, (n + 1) * TILE))
                if pair:
                    sum_ref[where] += scaled
                else:
                    sum_ref[where] = scaled + past if r == 1 else scaled
    total = jnp.concatenate([sum_ref[r * count : (r + 1) * count, :] for r in range(S)], axis=1)
    pieces = [total.astype(jnp.bfloat16)]
    if precise:
        pieces.append((total - pieces[0].astype(jnp.float32)).astype(jnp.bfloat16))
    moved = jnp.dot(jnp.concatenate(pieces, axis=0), restore_ref[...], preferred_element_type=jnp.float32)
    out_ref[...] = moved[:count] + moved[count:] if precise else moved.astype(jnp.bfloat16)


def first_kernel(blocks, static, offsets_ref, weights_ref, split_ref, restore_ref, wide_ref, last_ref, *refs):
    block_refs = refs[: blocks + 1]
    phases_ref, factor_ref, out_ref, raw_ref, sum_ref = refs[blocks + 1 :]
    records(offsets_ref, weights_ref, split_ref, block_refs, phases_ref, factor_ref, raw_ref)
    owner_sum(*static, restore_ref, wide_ref, last_ref, phases_ref, factor_ref, out_ref, sum_ref)


def later_kernel(static, *refs):
    owner_sum(*static, *refs)


def call_parts(static, wide):
    lags, precise = static[:2]
    pairs, _, count, _ = wide.shape
    shape = jax.ShapeDtypeStruct((count, lags), jnp.float32 if precise else jnp.bfloat16)
    scratch = pltpu.VMEM((S * count, lags // S), jnp.float32)
    params = dict(
        compiler_params=pltpu.CompilerParams(vmem_limit_bytes=16 << 20),
        cost_estimate=pl.CostEstimate(flops=2 * count * pairs * LENGTH * lags, bytes_accessed=4 * 10**6, transcendentals=0),
    )
    return shape, scratch, params


def first_sum(static, offsets, weights, split, restore, wide, last, blocks, tail):
    comps, stations, width = blocks[0].shape
    pairs = comps * stations
    parts = (len(blocks) * width + tail.shape[-1]) // (S * LANES)
    table = jax.ShapeDtypeStruct((S, pairs, parts * LANES), jnp.float32)
    shape, scratch, params = call_parts(static, wide)
    return pl.pallas_call(
        functools.partial(first_kernel, len(blocks), static),
        out_shape=(table, table, shape),
        in_specs=[SMEM, SMEM] + [VMEM] * 4 + [VMEM] * (len(blocks) + 1),
        out_specs=(VMEM,) * 3,
        scratch_shapes=[pltpu.VMEM((parts, pairs, S * LANES), jnp.float32), scratch],
        name="records_sum",
        **params,
    )(offsets, weights, split, restore, wide, last, *blocks, tail)


def later_sum(static, restore, wide, last, tables):
    shape, scratch, params = call_parts(static, wide)
    return pl.pallas_call(
        functools.partial(later_kernel, static),
        out_shape=shape,
        in_specs=[VMEM] * 5,
        out_specs=VMEM,
        scratch_shapes=[scratch],
        name="sum",
        **params,
    )(restore, wide, last, *tables)


def pick_kernel(restore_ref, split_ref, order_ref):
    lags = restore_ref.shape[0]
    width = lags // S
    row = iota((lags, 1), 0)
    restore_ref[...] = ones_where(iota((lags, lags), 1) == S * (row % width) + row // width)
    sample = iota((LENGTH, LENGTH), 0)
    column = iota((1, LENGTH), 1)
    split_ref[...] = ones_where(sample == S * (column % LANES) + column // LANES)
    order_ref[...] = ones_where(sample == S * (LANES - 1 - column % LANES) + column // LANES)


def picks(lags):
    return pl.pallas_call(
        pick_kernel,
        out_shape=tuple(jax.ShapeDtypeStruct((n, n), jnp.bfloat16) for n in (lags, LENGTH, LENGTH)),
        out_specs=(VMEM,) * 3,
        compiler_params=pltpu.CompilerParams(vmem_limit_bytes=4 << 20),
        cost_estimate=pl.CostEstimate(flops=4 * 10**9, bytes_accessed=4096, transcendentals=0),
        name="picks",
    )()


def shards(templates, data, tail, offsets, weights, mask):
    owners = lax.axis_size("tmpl")
    sides = lax.axis_size("sta")
    lags = owners * data.shape[-1] // (2 * sides)
    block = jnp.transpose(data, (1, 0, 2))
    closing = jnp.transpose(tail, (1, 0, 2))
    restore, split, order = picks(lags)
    if owners <= 4:
        blocks = [block] + [
            lax.ppermute(block, "tmpl", [(i, (i - d) % owners) for i in range(owners)]) for d in range(1, owners)
        ]
    else:
        gathered = lax.all_gather(block, "tmpl", axis=0, tiled=False)
        place = lax.axis_index("tmpl")
        blocks = [lax.dynamic_index_in_dim(gathered, lax.rem(place + d, owners), 0, False) for d in range(owners)]
    wide, last = templates_prepared(templates, mask, order)
    gotten = []
    for d in range(1, sides + 1):
        precise = d == sides
        if d == 1:
            *tables, away = first_sum((lags, False, d, sides, True), offsets, weights, split, restore, wide, last, blocks, closing)
        else:
            held, _ = lax.optimization_barrier((last, both))
            away = later_sum((lags, False, d, sides, True), restore, wide, held, tables)
        got = lax.ppermute(away, "comp", [(0, 1), (1, 0)])
        held, _ = lax.optimization_barrier((last, away))
        keep = later_sum((lags, precise, d, sides, False), restore, wide, held, tables)
        if d < sides:
            both = (keep.astype(jnp.float32) + got.astype(jnp.float32)).astype(jnp.bfloat16)
            gotten.append(lax.ppermute(both, "sta", [(i, (i + d) % sides) for i in range(sides)]))
    total = keep
    for term in gotten:
        total = total + term.astype(jnp.float32)
    if gotten:
        total = lax.optimization_barrier(total)
    return total + got.astype(jnp.float32)


def solution(mesh):
    in_specs = (
        P(("groups", "tmpl"), ("sta", "comp"), None, None),
        P(("groups", "sta", "comp"), None, "tmpl"),
        P(("groups", "sta", "comp"), None, None),
        P(("groups", "sta", "comp")),
        P(("groups", "sta", "comp")),
        P(("groups", "tmpl"), ("sta", "comp")),
    )
    out_specs = P(("groups", "tmpl"), ("sta", "comp"))
    return jax.shard_map(shards, mesh=mesh, in_specs=in_specs, out_specs=out_specs, check_vma=False)
```

time: 431 us -> 22 us (0.05)
  local copies, waits for them, and re-layouts: 287 us -> 0.03 us
  other arithmetic: 38.1 us -> 0.8 us
  matrix products: 30 us -> 0 us
  waiting for transfers between devices: 26.5 us -> 0.98 us
  blocking collectives: 16.3 us -> 0 us
  loops' own time: 15.6 us -> 0 us
  between operations: 13.5 us -> 0.18 us
  Pallas kernels: 0 us -> 11 us
  starting transfers between devices: 1.46 us -> 8.86 us
    reshape x10 -> x0, local copies, waits for them, and re-layouts: 106 us -> none  [the longest x8 103 us: lag_table(): return cut.reshape(lead + (length, period + 1))[..., :span]]
    another operation x16 -> x0, local copies, waits for them, and re-layouts: 74.7 us -> none  [lag_table(): tiled = jnp.tile(padded, (1,) * len(lead) + (length + 1,))]
    slice x8 -> x0, local copies, waits for them, and re-layouts: 55.2 us -> none  [lag_table(): cut = tiled[..., :length * (period + 1)]]
    while x56 -> x0, local copies, waits for them, and re-layouts: 45.7 us -> none
    reduce_sum x10 -> x0, other arithmetic: 33 us -> none  [the longest x8 28.8 us: table_factor(): squares = jnp.sum(values * values, axis=-2) / length]
    dot_general x8 -> x0, matrix products: 30 us -> none  [add_station(): jnp.einsum('tck,cpkj->tcpj', unit_rows, table, preferred_element_type=jnp...]
    reduce_scatter x1 -> x0, waiting for transfers between devices: 26.5 us -> none  [shards(): lax.psum_scatter(stacked, ('sta', 'comp'), scatter_dimension=1, tiled=True)]
    all_gather x1 -> x0, blocking collectives: 16.3 us -> none  [shards(): records = lax.all_gather(extended, 'tmpl', axis=2, tiled=True)]
  transfers between devices with their start and end apart: 2 -> 6, of which waited for: 1 -> 1; matrix products, arithmetic and copies ran while one was open for 1% -> 0% of each run, Pallas kernels for 0% -> 35%
where the time goes in v4:
time: 22 us; the launch traced here: 21.9 us
  Pallas kernels  11 us (50%)
  starting transfers between devices  8.86 us (40%)
  waiting for transfers between devices  0.98 us (4%)
  other arithmetic  0.8 us (4%)
    ppermute x3, starting transfers between devices, shards(): lax.ppermute(block, 'tmpl', [(i, (i - d) % owners) for i in range(owners)])  6.96 us
    pallas_call x3, Pallas kernels, later_sum(): pl.pallas_call(functools.partial(later_kernel, static), out_shape=shape,...  4.7 us
    pallas_call x1, Pallas kernels, first_sum(): pl.pallas_call(functools.partial(first_kernel, len(blocks), static), out_...  3.28 us
    pallas_call x1, Pallas kernels, templates_prepared(): pl.pallas_call(template_kernel, out_shape=(jax.ShapeDtypeStruct((pairs, 3...  2.88 us
    ppermute x1, starting transfers between devices, shards(): lax.ppermute(both, 'sta', [(i, (i + d) % sides) for i in range(sides)])  1.56 us
    ppermute x1, waiting for transfers between devices, shards(): lax.ppermute(both, 'sta', [(i, (i + d) % sides) for i in range(sides)])  0.97 us
    add x1, other arithmetic, shards(): return total + got.astype(jnp.float32)  0.73 us
  transfers between devices with their start and end apart: 6, of which 1 were waited for; matrix products, arithmetic and copies ran while one was open for 0% of the time, Pallas kernels for 35%

profile of v4, /device:TPU:0, one launch (start us, length us, event | category | flops | bytes accessed | tf_op | source)
XLA Modules:
  0.0 21.9 jit_solution(6106761202118552776)
XLA Ops:
  0.0 0.0 copy-start.4
  0.0 0.0 copy-start.5
  0.0 3.0 %collective-permute-start.2 = (bf16[3,8,512]{2,1,0:T(8,128)(2,1)}, bf16[3,8,512]{2,1,0:T(8,128)(2,1)S(1)}, u32[]{:S(2)}, u32[]{:S(2)}) collective-permute-start(bf16[3,8,512]{2,1,0:T(8,128)(2,1)} %bitcast.4), channel_id=1, source_target_pairs={{0,4},{4,8},{8,12},{12,0},{1,5},{5,9},{9,13},{13,1},{2,6},{6,10},{... | collective-permute-start | bytes 73736 | tf_op jit(solution)/shard_map/ppermute | solution.py:274
  3.0 2.6 %collective-permute-start.1 = (bf16[3,8,512]{2,1,0:T(8,128)(2,1)}, bf16[3,8,512]{2,1,0:T(8,128)(2,1)S(1)}, u32[]{:S(2)}, u32[]{:S(2)}) collective-permute-start(bf16[3,8,512]{2,1,0:T(8,128)(2,1)} %bitcast.5), channel_id=1, source_target_pairs={{0,8},{4,12},{8,0},{12,4},{1,9},{5,13},{9,1},{13,5},{2,10},{6,14},... | collective-permute-start | bytes 73736 | tf_op jit(solution)/shard_map/ppermute | solution.py:274
  5.6 1.3 %collective-permute-start = (bf16[3,8,512]{2,1,0:T(8,128)(2,1)}, bf16[3,8,512]{2,1,0:T(8,128)(2,1)S(1)}, u32[]{:S(2)}, u32[]{:S(2)}) collective-permute-start(bf16[3,8,512]{2,1,0:T(8,128)(2,1)} %bitcast.6), channel_id=1, source_target_pairs={{0,12},{4,0},{8,4},{12,8},{1,13},{5,1},{9,5},{13,9},{2,14},{6,2},{... | collective-permute-start | bytes 73736 | tf_op jit(solution)/shard_map/ppermute | solution.py:274
  7.0 0.2 picks.1
  7.1 0.0 copy-done.4
  7.2 0.0 copy-done.5
  7.2 0.0 copy-start
  7.2 0.0 copy-start.1
  7.2 0.0 copy-start.2
  7.2 0.0 copy-start.3
  7.2 2.9 %templates.1 = (bf16[24,3,128,128]{3,2,1,0:T(8,128)(2,1)S(1)}, bf16[128,128]{1,0:T(8,128)(2,1)S(1)}) custom-call(bf16[128,3,8,256]{3,2,1,0:T(8,128)(2,1)S(1)} %bitcast.9, s32[8,128]{1,0:T(8,128)S(1)} %bitcast.10, bf16[256,256]{1,0:T(8,128)(2,1)S(1)} %get-tuple-element.17.order_ref), custom_call_target="tpu_custom_call" | custom-call | flops 2000000000 | bytes 8000000 | tf_op jit(solution)/shard_map/templates/pallas_call | solution.py:71
  10.1 0.0 collective-permute-done.2.refs_3_
  10.1 0.0 collective-permute-done.1.refs_2_
  10.1 0.0 collective-permute-done.refs_1_
  10.1 0.0 copy-done
  10.2 0.0 copy-done.1
  10.2 0.0 copy-done.2
  10.2 0.0 copy-done.3
  10.2 3.3 %records_sum.1 = (f32[2,24,1280]{2,1,0:T(8,128)S(1)}, f32[2,24,1280]{2,1,0:T(8,128)S(1)}, bf16[128,512]{1,0:T(8,128)(2,1)S(1)}) custom-call(s32[8]{0:T(128)S(1)} %copy-done.2, s32[8]{0:T(128)S(1)} %copy-done.3, bf16[256,256]{1,0:T(8,128)(2,1)S(1)} %get-tuple-element.20.split_ref, bf16[512,512]{1,0:T(8,128)(2,1)S(1)} %get-tuple-element.16.restore_ref.refs_0_, ...), custom_call_target="tpu_custom_call" | custom-call | flops 805306368 | bytes 4000000 | tf_op jit(solution)/shard_map/records_sum/pallas_call | solution.py:219
  13.5 0.1 collective-permute-start.3
  13.6 1.5 %sum.3 = bf16[128,512]{1,0:T(8,128)(2,1)S(1)} custom-call(bf16[512,512]{1,0:T(8,128)(2,1)S(1)} %get-tuple-element.16.restore_ref.refs_0_, bf16[24,3,128,128]{3,2,1,0:T(8,128)(2,1)S(1)} %get-tuple-element.18.wide_ref.refs_1_, bf16[128,128]{1,0:T(8,128)(2,1)S(1)} %get-tuple-element.26.last_ref.refs_2_, f32[2,24,1280]{2,1,0:T(8,128)S(1)} %get-tuple-element.23.refs_3_, ...), custom_call_target="tpu_custom_call" | custom-call | flops 805306368 | bytes 4000000 | tf_op jit(solution)/shard_map/sum/pallas_call | solution.py:232
  15.1 0.0 collective-permute-done.3
  15.2 1.6 %collective-permute-start.4 = (bf16[128,512]{1,0:T(8,128)(2,1)S(1)}, bf16[128,512]{1,0:T(8,128)(2,1)S(1)}, u32[]{:S(2)}, u32[]{:S(2)}) collective-permute-start(bf16[128,512]{1,0:T(8,128)(2,1)S(1)} %add_convert_fusion), channel_id=1, source_target_pairs={{0,2},{2,0},{1,3},{3,1},{4,6},{6,4},{5,7},{7,5},{8,10},{10,8},{9,1... | collective-permute-start | bytes 393224 | tf_op jit(solution)/shard_map/ppermute | solution.py:294
  16.7 1.5 %sum.4 = bf16[128,512]{1,0:T(8,128)(2,1)S(1)} custom-call(bf16[512,512]{1,0:T(8,128)(2,1)S(1)} %get-tuple-element.16.restore_ref.refs_0_, bf16[24,3,128,128]{3,2,1,0:T(8,128)(2,1)S(1)} %get-tuple-element.18.wide_ref.refs_1_, bf16[128,128]{1,0:T(8,128)(2,1)S(1)} %get-tuple-element.26.last_ref.refs_2_, f32[2,24,1280]{2,1,0:T(8,128)S(1)} %get-tuple-element.23.refs_3_, ...), custom_call_target="tpu_custom_call" | custom-call | flops 805306368 | bytes 4000000 | tf_op jit(solution)/shard_map/sum/pallas_call | solution.py:232
  18.3 0.3 %collective-permute-start.5 = (bf16[128,512]{1,0:T(8,128)(2,1)S(1)}, bf16[128,512]{1,0:T(8,128)(2,1)S(1)}, u32[]{:S(2)}, u32[]{:S(2)}) collective-permute-start(bf16[128,512]{1,0:T(8,128)(2,1)S(1)} %sum.4), channel_id=1, source_target_pairs={{0,1},{1,0},{2,3},{3,2},{4,5},{5,4},{6,7},{7,6},{8,9},{9,8},{10,11... | collective-permute-start | bytes 393224 | tf_op jit(solution)/shard_map/ppermute | solution.py:289
  18.5 1.6 %sum.5 = f32[128,512]{1,0:T(8,128)S(1)} custom-call(bf16[512,512]{1,0:T(8,128)(2,1)S(1)} %get-tuple-element.16.restore_ref.refs_0_, bf16[24,3,128,128]{3,2,1,0:T(8,128)(2,1)S(1)} %get-tuple-element.18.wide_ref.refs_1_, bf16[128,128]{1,0:T(8,128)(2,1)S(1)} %get-tuple-element.26.last_ref.refs_2_, f32[2,24,1280]{2,1,0:T(8,128)S(1)} %get-tuple-element.23.refs_3_, ...), custom_call_target="tpu_custom_call" | custom-call | flops 805306368 | bytes 4000000 | tf_op jit(solution)/shard_map/sum/pallas_call | solution.py:232
  20.1 1.0 %collective-permute-done.4 = bf16[128,512]{1,0:T(8,128)(2,1)S(1)} collective-permute-done((bf16[128,512]{1,0:T(8,128)(2,1)S(1)}, bf16[128,512]{1,0:T(8,128)(2,1)S(1)}, u32[]{:S(2)}, u32[]{:S(2)}) %collective-permute-start.4) | collective-permute-done | bytes 131104 | tf_op jit(solution)/shard_map/ppermute | solution.py:294
  21.2 0.0 collective-permute-done.5
  21.2 0.7 %convert_add_fusion = f32[128,512]{1,0:T(8,128)} fusion(f32[128,512]{1,0:T(8,128)S(1)} %convert_add_fusion.1, bf16[128,512]{1,0:T(8,128)(2,1)S(1)} %collective-permute-done.5), kind=kLoop, calls=%fused_computation | loop fusion | flops 131072 | bytes 655360 | tf_op jit(solution)/shard_map/add | solution.py:300
  (2 shorter events, 0.1 us)
Async XLA Ops:
  0.0 7.1 %copy-start.4 = (bf16[128,8,3,256]{3,1,2,0:T(8,128)(2,1)S(1)}, bf16[128,8,3,256]{3,1,2,0:T(8,128)(2,1)}, u32[]{:S(2)}) copy-start(bf16[128,8,3,256]{3,1,2,0:T(8,128)(2,1)} %param.6) | copy-start | bytes 4718596
  0.0 7.2 %copy-start.5 = (s32[128,8]{0,1:T(8,128)S(1)}, s32[128,8]{0,1:T(8,128)}, u32[]{:S(2)}) copy-start(s32[128,8]{0,1:T(8,128)} %param.11) | copy-start | bytes 12292
  0.0 10.1 %collective-permute-start.2 = (bf16[3,8,512]{2,1,0:T(8,128)(2,1)}, bf16[3,8,512]{2,1,0:T(8,128)(2,1)S(1)}, u32[]{:S(2)}, u32[]{:S(2)}) collective-permute-start(bf16[3,8,512]{2,1,0:T(8,128)(2,1)} %bitcast.4), channel_id=1, source_target_pairs={{0,4},{4,8},{8,12},{12,0},{1,5},{5,9},{9,13},{13,1},{2,6},{6,10},{... | collective-permute-start | bytes 73736 | tf_op jit(solution)/shard_map/ppermute | solution.py:274
  3.0 7.1 %collective-permute-start.1 = (bf16[3,8,512]{2,1,0:T(8,128)(2,1)}, bf16[3,8,512]{2,1,0:T(8,128)(2,1)S(1)}, u32[]{:S(2)}, u32[]{:S(2)}) collective-permute-start(bf16[3,8,512]{2,1,0:T(8,128)(2,1)} %bitcast.5), channel_id=1, source_target_pairs={{0,8},{4,12},{8,0},{12,4},{1,9},{5,13},{9,1},{13,5},{2,10},{6,14},... | collective-permute-start | bytes 73736 | tf_op jit(solution)/shard_map/ppermute | solution.py:274
  5.6 4.5 %collective-permute-start = (bf16[3,8,512]{2,1,0:T(8,128)(2,1)}, bf16[3,8,512]{2,1,0:T(8,128)(2,1)S(1)}, u32[]{:S(2)}, u32[]{:S(2)}) collective-permute-start(bf16[3,8,512]{2,1,0:T(8,128)(2,1)} %bitcast.6), channel_id=1, source_target_pairs={{0,12},{4,0},{8,4},{12,8},{1,13},{5,1},{9,5},{13,9},{2,14},{6,2},{... | collective-permute-start | bytes 73736 | tf_op jit(solution)/shard_map/ppermute | solution.py:274
  7.2 3.0 %copy-start = (bf16[8,3,512]{2,0,1:T(8,128)(2,1)S(1)}, bf16[8,3,512]{2,0,1:T(8,128)(2,1)}, u32[]{:S(2)}) copy-start(bf16[8,3,512]{2,0,1:T(8,128)(2,1)} %param.7) | copy-start | bytes 73732
  7.2 3.0 %copy-start.1 = (bf16[8,3,512]{2,0,1:T(8,128)(2,1)S(1)}, bf16[8,3,512]{2,0,1:T(8,128)(2,1)}, u32[]{:S(2)}) copy-start(bf16[8,3,512]{2,0,1:T(8,128)(2,1)} %param.8) | copy-start | bytes 73732
  7.2 3.0 %copy-start.2 = (s32[8]{0:T(128)S(1)}, s32[8]{0:T(128)}, u32[]{:S(2)}) copy-start(s32[8]{0:T(128)} %offsets_ref.1) | copy-start | bytes 100
  7.2 3.0 %copy-start.3 = (s32[8]{0:T(128)S(1)}, s32[8]{0:T(128)}, u32[]{:S(2)}) copy-start(s32[8]{0:T(128)} %weights_ref.1) | copy-start | bytes 100
  13.5 1.6 %collective-permute-start.3 = (bf16[128,512]{1,0:T(8,128)(2,1)S(1)}, bf16[128,512]{1,0:T(8,128)(2,1)S(1)}, u32[]{:S(2)}, u32[]{:S(2)}) collective-permute-start(bf16[128,512]{1,0:T(8,128)(2,1)S(1)} %get-tuple-element.21), channel_id=1, source_target_pairs={{0,1},{1,0},{2,3},{3,2},{4,5},{5,4},{6,7},{7,6},{8,9},{9,8},{10,11... | collective-permute-start | bytes 393224 | tf_op jit(solution)/shard_map/ppermute | solution.py:289
  15.2 6.0 %collective-permute-start.4 = (bf16[128,512]{1,0:T(8,128)(2,1)S(1)}, bf16[128,512]{1,0:T(8,128)(2,1)S(1)}, u32[]{:S(2)}, u32[]{:S(2)}) collective-permute-start(bf16[128,512]{1,0:T(8,128)(2,1)S(1)} %add_convert_fusion), channel_id=1, source_target_pairs={{0,2},{2,0},{1,3},{3,1},{4,6},{6,4},{5,7},{7,5},{8,10},{10,8},{9,1... | collective-permute-start | bytes 393224 | tf_op jit(solution)/shard_map/ppermute | solution.py:294
  18.3 2.9 %collective-permute-start.5 = (bf16[128,512]{1,0:T(8,128)(2,1)S(1)}, bf16[128,512]{1,0:T(8,128)(2,1)S(1)}, u32[]{:S(2)}, u32[]{:S(2)}) collective-permute-start(bf16[128,512]{1,0:T(8,128)(2,1)S(1)} %sum.4), channel_id=1, source_target_pairs={{0,1},{1,0},{2,3},{3,2},{4,5},{5,4},{6,7},{7,6},{8,9},{9,8},{10,11... | collective-permute-start | bytes 393224 | tf_op jit(solution)/shard_map/ppermute | solution.py:289

commit v5 on v4

--- a/solution.py
+++ b/solution.py
@@ -8,6 +8,7 @@
 from jax.sharding import PartitionSpec as P
 
 EPS = 1e-05
+SLOTS = 4
 S = 2
 LANES = 128
 LENGTH = S * LANES
@@ -61,7 +62,8 @@
             wide_ref[pair, 0] = even.astype(jnp.bfloat16)
             wide_ref[pair, 1] = odd.astype(jnp.bfloat16)
             wide_ref[pair, 2] = jnp.where(lane == LANES - 1, 0.0, later(odd, 1)).astype(jnp.bfloat16)
-            last = jnp.where(lane == pair, pltpu.roll(odd, pair, axis=1), last)
+            slot = SLOTS * (pair % stations) + pair // stations
+            last = jnp.where(lane == slot, pltpu.roll(odd, slot, axis=1), last)
     last_ref[...] = last.astype(jnp.bfloat16)
 
 
@@ -86,61 +88,82 @@
     )(jnp.transpose(templates, (0, 2, 1, 3)), jnp.transpose(mask), order)
 
 
-def records(offsets_ref, weights_ref, split_ref, block_refs, phases_ref, factor_ref, raw_ref):
+def records(offsets_ref, weights_ref, split_ref, band_ref, block_refs, phases_ref, factor_ref, raw_ref):
     blocks = len(block_refs) - 1
     comps, stations, width = block_refs[0].shape
-    pairs = comps * stations
-    unit = S * LANES
-    per = width // unit
+    rows = stations * SLOTS
+    per = width // LENGTH
     for i in range(blocks + 1):
-        values = block_refs[i][...].astype(jnp.float32).reshape(pairs, block_refs[i].shape[-1])
         home = blocks if i == blocks else lax.rem(lax.axis_index("tmpl") + i, blocks)
-        for j in range(block_refs[i].shape[-1] // unit):
-            raw_ref[home * per + j] = values[:, unit * j : unit * (j + 1)]
-    parts = raw_ref.shape[0]
-    flat = raw_ref[...].reshape(parts * pairs, unit).astype(jnp.bfloat16)
+        for j in range(block_refs[i].shape[-1] // LANES):
+            for c in range(SLOTS):
+                if c < comps:
+                    values = block_refs[i][c, :, LANES * j : LANES * (j + 1)].astype(jnp.float32)
+                else:
+                    values = jnp.zeros((stations, LANES), jnp.float32)
+                raw_ref[home * per * S + j, pl.ds(c, stations, stride=SLOTS), :] = values
+    parts = raw_ref.shape[0] // S
+    flat = jnp.concatenate(
+        [jnp.concatenate([raw_ref[S * b + i] for i in range(S)], axis=1) for b in range(parts)], axis=0
+    ).astype(jnp.bfloat16)
     split = jnp.dot(flat, split_ref[...], preferred_element_type=jnp.float32)
-    full = parts * LANES
-    row = iota((stations, full), 0)
-    offset = jnp.zeros((stations, full), jnp.int32)
-    weight = jnp.zeros((stations, full), jnp.float32)
-    for s in range(stations):
-        offset = jnp.where(row == s, offsets_ref[s], offset)
-        weight = jnp.where(row == s, weights_ref[s].astype(jnp.float32), weight)
-    for c in range(comps):
-        at = c * stations
-        v = [
+    lane = iota((8, LANES), 1)
+    first = iota((8, LANES), 0) < SLOTS
+    groups = rows // 8
+    v = [[], []]
+    for q in range(groups):
+        offset = [offsets_ref[2 * q], offsets_ref[2 * q + 1]]
+        odd = jnp.where(first, offset[0] & 1, offset[1] & 1) != 0
+        held = [[split[b * rows + 8 * q : b * rows + 8 * q + 8, LANES * p : LANES * (p + 1)] for b in range(parts)] for p in range(S)]
+        for p in range(S):
+            source = [jnp.where(odd, held[1 - p][b], held[p][b]) for b in range(parts)]
+            by = [(o + p) // S for o in offset]
+            turned = [
+                jnp.where(first, pltpu.roll(x, (LANES - by[0]) % LANES, axis=1), pltpu.roll(x, (LANES - by[1]) % LANES, axis=1))
+                for x in source
+            ]
+            kept = lane < jnp.where(first, LANES - by[0], LANES - by[1])
+            v[p].append([jnp.where(kept, turned[b], turned[b + 1]) for b in range(parts - 1)])
+            phases_ref[p, 8 * q : 8 * q + 8, :] = jnp.concatenate(v[p][q], axis=1)
+    count = parts - 2
+
+    def window_sums(terms):
+        wide = [
             jnp.concatenate(
-                [split[b * pairs + at : b * pairs + at + stations, LANES * p : LANES * (p + 1)] for b in range(parts)], axis=1
+                [
+                    jnp.concatenate(
+                        [jnp.concatenate([term[q][j + i] for i in range(2)], axis=1) for q in range(groups)], axis=0
+                    ).astype(jnp.bfloat16)
+                    for j in range(count)
+                ],
+                axis=0,
             )
-            for p in range(S)
+            for term in terms
         ]
-        step = 1
-        while S * step < LENGTH:
-            taken = (offset & (S * step)) != 0
-            v = [jnp.where(taken, later(x, step), x) for x in v]
-            step *= 2
-        taken = (offset & 1) != 0
-        v = [jnp.where(taken, v[1], v[0]), jnp.where(taken, later(v[0], 1), v[1])]
-        mean = v[0] + v[1]
-        power = v[0] * v[0] + v[1] * v[1]
-        step = 1
-        while step < LANES:
-            mean = mean + later(mean, step)
-            power = power + later(power, step)
-            step *= 2
-        ahead = later(v[0], LANES)
-        for r in range(S):
-            middle = mean * (1.0 / LENGTH)
-            spread = power * (1.0 / LENGTH) - middle * middle
-            factor_ref[r, at : at + stations, :] = weight / (LENGTH * jnp.sqrt(spread + EPS))
-            phases_ref[r, at : at + stations, :] = v[r]
-            mean = mean + (ahead - v[0])
-            power = power + (ahead * ahead - v[0] * v[0])
+        band = jnp.concatenate([band_ref[...]] * len(terms), axis=0)
+        return jnp.dot(jnp.concatenate(wide, axis=1), band, preferred_element_type=jnp.float32)
+
+    square = [[[x * x for x in line] for line in v[p]] for p in range(S)]
+    high = [[[x.astype(jnp.bfloat16).astype(jnp.float32) for x in line] for line in square[p]] for p in range(S)]
+    low = [[[x - y for x, y in zip(a, b)] for a, b in zip(square[p], high[p])] for p in range(S)]
+    sums = window_sums(v)
+    powers = window_sums(high + low)
+    for q in range(groups):
+        weight = jnp.where(first, weights_ref[2 * q].astype(jnp.float32), weights_ref[2 * q + 1].astype(jnp.float32))
+        for j in range(count):
+            mean = sums[j * rows + 8 * q : j * rows + 8 * q + 8]
+            power = powers[j * rows + 8 * q : j * rows + 8 * q + 8]
+            for r in range(S):
+                middle = mean * (1.0 / LENGTH)
+                spread = power * (1.0 / LENGTH) - middle * middle
+                factor_ref[r, 8 * q : 8 * q + 8, LANES * j : LANES * (j + 1)] = weight / (LENGTH * jnp.sqrt(spread + EPS))
+                mean = mean + (v[0][q][j + 1] - v[0][q][j])
+                power = power + (square[0][q][j + 1] - square[0][q][j])
 
 
 def owner_sum(lags, precise, step, sides, away, restore_ref, wide_ref, last_ref, phases_ref, factor_ref, out_ref, sum_ref):
     pairs, _, count, _ = wide_ref.shape
+    stations = phases_ref.shape[1] // SLOTS
     side, core = lax.rem(lax.axis_index("sta") + step, sides), lax.axis_index("comp")
     owner = 2 * side + (1 - core if away else core)
     lane = iota((8, LANES), 1)
@@ -149,13 +172,14 @@
     for n in range(width // TILE):
         begin = pl.multiple_of(owner * width + n * TILE, LANES)
         extra = phases_ref[0, :, pl.ds(begin + LANES, TILE)] * factor_ref[1, :, pl.ds(begin, TILE)]
-        extra = jnp.concatenate([extra, jnp.zeros((LANES - pairs, TILE), jnp.float32)], axis=0).astype(jnp.bfloat16)
+        extra = jnp.concatenate([extra, jnp.zeros((LANES - SLOTS * stations, TILE), jnp.float32)], axis=0).astype(jnp.bfloat16)
         past = jnp.dot(last_ref[...], extra, preferred_element_type=jnp.float32)
         for pair in range(pairs):
+            slot = SLOTS * (pair % stations) + pair // stations
             rows = []
             for p in range(S):
                 line = [
-                    jnp.broadcast_to(phases_ref[p, pair : pair + 1, pl.ds(begin + LANES * j, LANES)], (8, LANES))
+                    jnp.broadcast_to(phases_ref[p, slot : slot + 1, pl.ds(begin + LANES * j, LANES)], (8, LANES))
                     for j in range(3)
                 ]
                 for g in range(0, LANES, 16):
@@ -173,7 +197,7 @@
             )
             products = jnp.dot(units, table, preferred_element_type=jnp.float32)
             for r in range(S):
-                scaled = products[r * count : (r + 1) * count] * factor_ref[r, pair : pair + 1, pl.ds(begin, TILE)]
+                scaled = products[r * count : (r + 1) * count] * factor_ref[r, slot : slot + 1, pl.ds(begin, TILE)]
                 where = (slice(r * count, (r + 1) * count), slice(n * TILE, (n + 1) * TILE))
                 if pair:
                     sum_ref[where] += scaled
@@ -187,10 +211,10 @@
     out_ref[...] = moved[:count] + moved[count:] if precise else moved.astype(jnp.bfloat16)
 
 
-def first_kernel(blocks, static, offsets_ref, weights_ref, split_ref, restore_ref, wide_ref, last_ref, *refs):
+def first_kernel(blocks, static, offsets_ref, weights_ref, split_ref, band_ref, restore_ref, wide_ref, last_ref, *refs):
     block_refs = refs[: blocks + 1]
     phases_ref, factor_ref, out_ref, raw_ref, sum_ref = refs[blocks + 1 :]
-    records(offsets_ref, weights_ref, split_ref, block_refs, phases_ref, factor_ref, raw_ref)
+    records(offsets_ref, weights_ref, split_ref, band_ref, block_refs, phases_ref, factor_ref, raw_ref)
     owner_sum(*static, restore_ref, wide_ref, last_ref, phases_ref, factor_ref, out_ref, sum_ref)
 
 
@@ -210,21 +234,24 @@
     return shape, scratch, params
 
 
-def first_sum(static, offsets, weights, split, restore, wide, last, blocks, tail):
+def first_sum(static, offsets, weights, split, band, restore, wide, last, blocks, tail):
     comps, stations, width = blocks[0].shape
-    pairs = comps * stations
-    parts = (len(blocks) * width + tail.shape[-1]) // (S * LANES)
-    table = jax.ShapeDtypeStruct((S, pairs, parts * LANES), jnp.float32)
+    rows = SLOTS * stations
+    parts = (len(blocks) * width + tail.shape[-1]) // LENGTH
     shape, scratch, params = call_parts(static, wide)
     return pl.pallas_call(
         functools.partial(first_kernel, len(blocks), static),
-        out_shape=(table, table, shape),
-        in_specs=[SMEM, SMEM] + [VMEM] * 4 + [VMEM] * (len(blocks) + 1),
+        out_shape=(
+            jax.ShapeDtypeStruct((S, rows, (parts - 1) * LANES), jnp.float32),
+            jax.ShapeDtypeStruct((S, rows, (parts - 2) * LANES), jnp.float32),
+            shape,
+        ),
+        in_specs=[SMEM, SMEM] + [VMEM] * (6 + len(blocks)),
         out_specs=(VMEM,) * 3,
-        scratch_shapes=[pltpu.VMEM((parts, pairs, S * LANES), jnp.float32), scratch],
+        scratch_shapes=[pltpu.VMEM((S * parts, rows, LANES), jnp.float32), scratch],
         name="records_sum",
         **params,
-    )(offsets, weights, split, restore, wide, last, *blocks, tail)
+    )(offsets, weights, split, band, restore, wide, last, *blocks, tail)
 
 
 def later_sum(static, restore, wide, last, tables):
@@ -240,7 +267,7 @@
     )(restore, wide, last, *tables)
 
 
-def pick_kernel(restore_ref, split_ref, order_ref):
+def pick_kernel(restore_ref, split_ref, order_ref, band_ref):
     lags = restore_ref.shape[0]
     width = lags // S
     row = iota((lags, 1), 0)
@@ -249,13 +276,18 @@
     column = iota((1, LENGTH), 1)
     split_ref[...] = ones_where(sample == S * (column % LANES) + column // LANES)
     order_ref[...] = ones_where(sample == S * (LANES - 1 - column % LANES) + column // LANES)
+    ahead = iota((2 * LANES, LANES), 0) - iota((2 * LANES, LANES), 1)
+    band_ref[...] = ones_where((ahead >= 0) & (ahead < LANES))
 
 
 def picks(lags):
     return pl.pallas_call(
         pick_kernel,
-        out_shape=tuple(jax.ShapeDtypeStruct((n, n), jnp.bfloat16) for n in (lags, LENGTH, LENGTH)),
-        out_specs=(VMEM,) * 3,
+        out_shape=tuple(
+            jax.ShapeDtypeStruct(shape, jnp.bfloat16)
+            for shape in ((lags, lags), (LENGTH, LENGTH), (LENGTH, LENGTH), (2 * LANES, LANES))
+        ),
+        out_specs=(VMEM,) * 4,
         compiler_params=pltpu.CompilerParams(vmem_limit_bytes=4 << 20),
         cost_estimate=pl.CostEstimate(flops=4 * 10**9, bytes_accessed=4096, transcendentals=0),
         name="picks",
@@ -268,7 +300,7 @@
     lags = owners * data.shape[-1] // (2 * sides)
     block = jnp.transpose(data, (1, 0, 2))
     closing = jnp.transpose(tail, (1, 0, 2))
-    restore, split, order = picks(lags)
+    restore, split, order, band = picks(lags)
     if owners <= 4:
         blocks = [block] + [
             lax.ppermute(block, "tmpl", [(i, (i - d) % owners) for i in range(owners)]) for d in range(1, owners)
@@ -282,7 +314,7 @@
     for d in range(1, sides + 1):
         precise = d == sides
         if d == 1:
-            *tables, away = first_sum((lags, False, d, sides, True), offsets, weights, split, restore, wide, last, blocks, closing)
+            *tables, away = first_sum((lags, False, d, sides, True), offsets, weights, split, band, restore, wide, last, blocks, closing)
         else:
             held, _ = lax.optimization_barrier((last, both))
             away = later_sum((lags, False, d, sides, True), restore, wide, held, tables)

time: 22 us -> 21.7 us (0.986)
  Pallas kernels: 11 us -> 10.7 us
    pallas_call x1, Pallas kernels: 3.28 us -> 2.88 us  [first_sum(): pl.pallas_call(functools.partial(first_kernel, len(blocks), static), out_...]
  transfers between devices with their start and end apart: 6 -> 6, of which waited for: 1 -> 1; matrix products, arithmetic and copies ran while one was open for 0% -> 0% of each run, Pallas kernels for 35% -> 36%
where the time goes in v5:
time: 21.7 us; the launch traced here: 21.5 us
  Pallas kernels  10.7 us (49%)
  starting transfers between devices  8.86 us (41%)
  waiting for transfers between devices  0.95 us (4%)
  other arithmetic  0.8 us (4%)
    ppermute x3, starting transfers between devices, shards(): lax.ppermute(block, 'tmpl', [(i, (i - d) % owners) for i in range(owners)])  6.96 us
    pallas_call x3, Pallas kernels, later_sum(): pl.pallas_call(functools.partial(later_kernel, static), out_shape=shape,...  4.74 us
    pallas_call x1, Pallas kernels, templates_prepared(): pl.pallas_call(template_kernel, out_shape=(jax.ShapeDtypeStruct((pairs, 3...  2.89 us
    pallas_call x1, Pallas kernels, first_sum(): pl.pallas_call(functools.partial(first_kernel, len(blocks), static), out_...  2.88 us
    ppermute x1, starting transfers between devices, shards(): lax.ppermute(both, 'sta', [(i, (i + d) % sides) for i in range(sides)])  1.55 us
    ppermute x1, waiting for transfers between devices, shards(): lax.ppermute(both, 'sta', [(i, (i + d) % sides) for i in range(sides)])  0.94 us
    add x1, other arithmetic, shards(): return total + got.astype(jnp.float32)  0.73 us
  transfers between devices with their start and end apart: 6, of which 1 were waited for; matrix products, arithmetic and copies ran while one was open for 0% of the time, Pallas kernels for 36%

profile of v5, /device:TPU:0, one launch (start us, length us, event | category | flops | bytes accessed | tf_op | source)
XLA Modules:
  0.0 21.5 jit_solution(11471994770045077883)
XLA Ops:
  0.0 0.0 copy-start.4
  0.0 0.0 copy-start.5
  0.0 3.0 %collective-permute-start.2 = (bf16[3,8,512]{2,1,0:T(8,128)(2,1)}, bf16[3,8,512]{2,1,0:T(8,128)(2,1)S(1)}, u32[]{:S(2)}, u32[]{:S(2)}) collective-permute-start(bf16[3,8,512]{2,1,0:T(8,128)(2,1)} %bitcast.4), channel_id=1, source_target_pairs={{0,4},{4,8},{8,12},{12,0},{1,5},{5,9},{9,13},{13,1},{2,6},{6,10},{... | collective-permute-start | bytes 73736 | tf_op jit(solution)/shard_map/ppermute | solution.py:306
  3.0 2.6 %collective-permute-start.1 = (bf16[3,8,512]{2,1,0:T(8,128)(2,1)}, bf16[3,8,512]{2,1,0:T(8,128)(2,1)S(1)}, u32[]{:S(2)}, u32[]{:S(2)}) collective-permute-start(bf16[3,8,512]{2,1,0:T(8,128)(2,1)} %bitcast.5), channel_id=1, source_target_pairs={{0,8},{4,12},{8,0},{12,4},{1,9},{5,13},{9,1},{13,5},{2,10},{6,14},... | collective-permute-start | bytes 73736 | tf_op jit(solution)/shard_map/ppermute | solution.py:306
  5.6 1.3 %collective-permute-start = (bf16[3,8,512]{2,1,0:T(8,128)(2,1)}, bf16[3,8,512]{2,1,0:T(8,128)(2,1)S(1)}, u32[]{:S(2)}, u32[]{:S(2)}) collective-permute-start(bf16[3,8,512]{2,1,0:T(8,128)(2,1)} %bitcast.6), channel_id=1, source_target_pairs={{0,12},{4,0},{8,4},{12,8},{1,13},{5,1},{9,5},{13,9},{2,14},{6,2},{... | collective-permute-start | bytes 73736 | tf_op jit(solution)/shard_map/ppermute | solution.py:306
  7.0 0.2 picks.1
  7.2 0.0 copy-done.4
  7.2 0.0 copy-done.5
  7.2 0.0 copy-start
  7.2 0.0 copy-start.1
  7.2 0.0 copy-start.2
  7.2 0.0 copy-start.3
  7.2 2.9 %templates.1 = (bf16[24,3,128,128]{3,2,1,0:T(8,128)(2,1)S(1)}, bf16[128,128]{1,0:T(8,128)(2,1)S(1)}) custom-call(bf16[128,3,8,256]{3,2,1,0:T(8,128)(2,1)S(1)} %bitcast.9, s32[8,128]{1,0:T(8,128)S(1)} %bitcast.10, bf16[256,256]{1,0:T(8,128)(2,1)S(1)} %get-tuple-element.18.order_ref), custom_call_target="tpu_custom_call" | custom-call | flops 2000000000 | bytes 8000000 | tf_op jit(solution)/shard_map/templates/pallas_call | solution.py:73
  10.1 0.0 collective-permute-done.2.refs_3_
  10.1 0.0 collective-permute-done.1.refs_2_
  10.1 0.0 collective-permute-done.refs_1_
  10.2 0.0 copy-done
  10.2 0.0 copy-done.1
  10.2 0.0 copy-done.2
  10.2 0.0 copy-done.3
  10.2 2.9 %records_sum.1 = (f32[2,32,1152]{2,1,0:T(8,128)S(1)}, f32[2,32,1024]{2,1,0:T(8,128)S(1)}, bf16[128,512]{1,0:T(8,128)(2,1)S(1)}) custom-call(s32[8]{0:T(128)S(1)} %copy-done.2, s32[8]{0:T(128)S(1)} %copy-done.3, bf16[256,256]{1,0:T(8,128)(2,1)S(1)} %get-tuple-element.21.split_ref, bf16[256,128]{1,0:T(8,128)(2,1)S(1)} %get-tuple-element.22.band_ref, ...), custom_call_target="tpu_custom_call" | custom-call | flops 805306368 | bytes 4000000 | tf_op jit(solution)/shard_map/records_sum/pallas_call | solution.py:242
  13.1 0.1 collective-permute-start.3
  13.2 1.6 %sum.3 = bf16[128,512]{1,0:T(8,128)(2,1)S(1)} custom-call(bf16[512,512]{1,0:T(8,128)(2,1)S(1)} %get-tuple-element.17.restore_ref.refs_0_, bf16[24,3,128,128]{3,2,1,0:T(8,128)(2,1)S(1)} %get-tuple-element.19.wide_ref.refs_1_, bf16[128,128]{1,0:T(8,128)(2,1)S(1)} %get-tuple-element.28.last_ref.refs_2_, f32[2,32,1152]{2,1,0:T(8,128)S(1)} %get-tuple-element.25.refs_3_, ...), custom_call_target="tpu_custom_call" | custom-call | flops 805306368 | bytes 4000000 | tf_op jit(solution)/shard_map/sum/pallas_call | solution.py:259
  14.7 0.0 collective-permute-done.3
  14.8 1.6 %collective-permute-start.4 = (bf16[128,512]{1,0:T(8,128)(2,1)S(1)}, bf16[128,512]{1,0:T(8,128)(2,1)S(1)}, u32[]{:S(2)}, u32[]{:S(2)}) collective-permute-start(bf16[128,512]{1,0:T(8,128)(2,1)S(1)} %add_convert_fusion), channel_id=1, source_target_pairs={{0,2},{2,0},{1,3},{3,1},{4,6},{6,4},{5,7},{7,5},{8,10},{10,8},{9,1... | collective-permute-start | bytes 393224 | tf_op jit(solution)/shard_map/ppermute | solution.py:326
  16.3 1.5 %sum.4 = bf16[128,512]{1,0:T(8,128)(2,1)S(1)} custom-call(bf16[512,512]{1,0:T(8,128)(2,1)S(1)} %get-tuple-element.17.restore_ref.refs_0_, bf16[24,3,128,128]{3,2,1,0:T(8,128)(2,1)S(1)} %get-tuple-element.19.wide_ref.refs_1_, bf16[128,128]{1,0:T(8,128)(2,1)S(1)} %get-tuple-element.28.last_ref.refs_2_, f32[2,32,1152]{2,1,0:T(8,128)S(1)} %get-tuple-element.25.refs_3_, ...), custom_call_target="tpu_custom_call" | custom-call | flops 805306368 | bytes 4000000 | tf_op jit(solution)/shard_map/sum/pallas_call | solution.py:259
  17.9 0.3 %collective-permute-start.5 = (bf16[128,512]{1,0:T(8,128)(2,1)S(1)}, bf16[128,512]{1,0:T(8,128)(2,1)S(1)}, u32[]{:S(2)}, u32[]{:S(2)}) collective-permute-start(bf16[128,512]{1,0:T(8,128)(2,1)S(1)} %sum.4), channel_id=1, source_target_pairs={{0,1},{1,0},{2,3},{3,2},{4,5},{5,4},{6,7},{7,6},{8,9},{9,8},{10,11... | collective-permute-start | bytes 393224 | tf_op jit(solution)/shard_map/ppermute | solution.py:321
  18.2 1.6 %sum.5 = f32[128,512]{1,0:T(8,128)S(1)} custom-call(bf16[512,512]{1,0:T(8,128)(2,1)S(1)} %get-tuple-element.17.restore_ref.refs_0_, bf16[24,3,128,128]{3,2,1,0:T(8,128)(2,1)S(1)} %get-tuple-element.19.wide_ref.refs_1_, bf16[128,128]{1,0:T(8,128)(2,1)S(1)} %get-tuple-element.28.last_ref.refs_2_, f32[2,32,1152]{2,1,0:T(8,128)S(1)} %get-tuple-element.25.refs_3_, ...), custom_call_target="tpu_custom_call" | custom-call | flops 805306368 | bytes 4000000 | tf_op jit(solution)/shard_map/sum/pallas_call | solution.py:259
  19.8 0.9 %collective-permute-done.4 = bf16[128,512]{1,0:T(8,128)(2,1)S(1)} collective-permute-done((bf16[128,512]{1,0:T(8,128)(2,1)S(1)}, bf16[128,512]{1,0:T(8,128)(2,1)S(1)}, u32[]{:S(2)}, u32[]{:S(2)}) %collective-permute-start.4) | collective-permute-done | bytes 131104 | tf_op jit(solution)/shard_map/ppermute | solution.py:326
  20.8 0.0 collective-permute-done.5
  20.8 0.7 %convert_add_fusion = f32[128,512]{1,0:T(8,128)} fusion(f32[128,512]{1,0:T(8,128)S(1)} %convert_add_fusion.1, bf16[128,512]{1,0:T(8,128)(2,1)S(1)} %collective-permute-done.5), kind=kLoop, calls=%fused_computation | loop fusion | flops 131072 | bytes 655360 | tf_op jit(solution)/shard_map/add | solution.py:332
  (2 shorter events, 0.1 us)
Async XLA Ops:
  0.0 7.2 %copy-start.4 = (bf16[128,8,3,256]{3,1,2,0:T(8,128)(2,1)S(1)}, bf16[128,8,3,256]{3,1,2,0:T(8,128)(2,1)}, u32[]{:S(2)}) copy-start(bf16[128,8,3,256]{3,1,2,0:T(8,128)(2,1)} %param.6) | copy-start | bytes 4718596
  0.0 7.2 %copy-start.5 = (s32[128,8]{0,1:T(8,128)S(1)}, s32[128,8]{0,1:T(8,128)}, u32[]{:S(2)}) copy-start(s32[128,8]{0,1:T(8,128)} %param.11) | copy-start | bytes 12292
  0.0 10.1 %collective-permute-start.2 = (bf16[3,8,512]{2,1,0:T(8,128)(2,1)}, bf16[3,8,512]{2,1,0:T(8,128)(2,1)S(1)}, u32[]{:S(2)}, u32[]{:S(2)}) collective-permute-start(bf16[3,8,512]{2,1,0:T(8,128)(2,1)} %bitcast.4), channel_id=1, source_target_pairs={{0,4},{4,8},{8,12},{12,0},{1,5},{5,9},{9,13},{13,1},{2,6},{6,10},{... | collective-permute-start | bytes 73736 | tf_op jit(solution)/shard_map/ppermute | solution.py:306
  3.0 7.1 %collective-permute-start.1 = (bf16[3,8,512]{2,1,0:T(8,128)(2,1)}, bf16[3,8,512]{2,1,0:T(8,128)(2,1)S(1)}, u32[]{:S(2)}, u32[]{:S(2)}) collective-permute-start(bf16[3,8,512]{2,1,0:T(8,128)(2,1)} %bitcast.5), channel_id=1, source_target_pairs={{0,8},{4,12},{8,0},{12,4},{1,9},{5,13},{9,1},{13,5},{2,10},{6,14},... | collective-permute-start | bytes 73736 | tf_op jit(solution)/shard_map/ppermute | solution.py:306
  5.6 4.5 %collective-permute-start = (bf16[3,8,512]{2,1,0:T(8,128)(2,1)}, bf16[3,8,512]{2,1,0:T(8,128)(2,1)S(1)}, u32[]{:S(2)}, u32[]{:S(2)}) collective-permute-start(bf16[3,8,512]{2,1,0:T(8,128)(2,1)} %bitcast.6), channel_id=1, source_target_pairs={{0,12},{4,0},{8,4},{12,8},{1,13},{5,1},{9,5},{13,9},{2,14},{6,2},{... | collective-permute-start | bytes 73736 | tf_op jit(solution)/shard_map/ppermute | solution.py:306
  7.2 3.0 %copy-start = (bf16[8,3,512]{2,0,1:T(8,128)(2,1)S(1)}, bf16[8,3,512]{2,0,1:T(8,128)(2,1)}, u32[]{:S(2)}) copy-start(bf16[8,3,512]{2,0,1:T(8,128)(2,1)} %param.7) | copy-start | bytes 73732
  7.2 3.0 %copy-start.1 = (bf16[8,3,512]{2,0,1:T(8,128)(2,1)S(1)}, bf16[8,3,512]{2,0,1:T(8,128)(2,1)}, u32[]{:S(2)}) copy-start(bf16[8,3,512]{2,0,1:T(8,128)(2,1)} %param.8) | copy-start | bytes 73732
  7.2 3.0 %copy-start.2 = (s32[8]{0:T(128)S(1)}, s32[8]{0:T(128)}, u32[]{:S(2)}) copy-start(s32[8]{0:T(128)} %offsets_ref.1) | copy-start | bytes 100
  7.2 3.0 %copy-start.3 = (s32[8]{0:T(128)S(1)}, s32[8]{0:T(128)}, u32[]{:S(2)}) copy-start(s32[8]{0:T(128)} %weights_ref.1) | copy-start | bytes 100
  13.1 1.6 %collective-permute-start.3 = (bf16[128,512]{1,0:T(8,128)(2,1)S(1)}, bf16[128,512]{1,0:T(8,128)(2,1)S(1)}, u32[]{:S(2)}, u32[]{:S(2)}) collective-permute-start(bf16[128,512]{1,0:T(8,128)(2,1)S(1)} %get-tuple-element.23), channel_id=1, source_target_pairs={{0,1},{1,0},{2,3},{3,2},{4,5},{5,4},{6,7},{7,6},{8,9},{9,8},{10,11... | collective-permute-start | bytes 393224 | tf_op jit(solution)/shard_map/ppermute | solution.py:321
  14.8 6.0 %collective-permute-start.4 = (bf16[128,512]{1,0:T(8,128)(2,1)S(1)}, bf16[128,512]{1,0:T(8,128)(2,1)S(1)}, u32[]{:S(2)}, u32[]{:S(2)}) collective-permute-start(bf16[128,512]{1,0:T(8,128)(2,1)S(1)} %add_convert_fusion), channel_id=1, source_target_pairs={{0,2},{2,0},{1,3},{3,1},{4,6},{6,4},{5,7},{7,5},{8,10},{10,8},{9,1... | collective-permute-start | bytes 393224 | tf_op jit(solution)/shard_map/ppermute | solution.py:326
  17.9 2.9 %collective-permute-start.5 = (bf16[128,512]{1,0:T(8,128)(2,1)S(1)}, bf16[128,512]{1,0:T(8,128)(2,1)S(1)}, u32[]{:S(2)}, u32[]{:S(2)}) collective-permute-start(bf16[128,512]{1,0:T(8,128)(2,1)S(1)} %sum.4), channel_id=1, source_target_pairs={{0,1},{1,0},{2,3},{3,2},{4,5},{5,4},{6,7},{7,6},{8,9},{9,8},{10,11... | collective-permute-start | bytes 393224 | tf_op jit(solution)/shard_map/ppermute | solution.py:321

commit v6 on v5

--- a/solution.py
+++ b/solution.py
@@ -33,6 +33,7 @@
 def template_kernel(x_ref, mask_ref, order_ref, wide_ref, last_ref, unit_ref, rows_ref):
     count, comps, stations, length = x_ref.shape
     pairs = comps * stations
+    pitch = unit_ref.shape[1] // count
     group = min(8, count)
     lane = iota((count, LANES), 1)
     last = jnp.zeros((count, LANES), jnp.float32)
@@ -43,16 +44,17 @@
         spread = jnp.sum(centred * centred, axis=-1, keepdims=True) * (1.0 / length)
         unit = centred * lax.rsqrt(spread + EPS)
         for h in range(length // LANES):
-            unit_ref[h, at * pairs : (at + group) * pairs, :] = unit[:, LANES * h : LANES * (h + 1)]
+            for t in range(group):
+                unit_ref[h, (at + t) * pitch : (at + t) * pitch + pairs, :] = unit[t * pairs : (t + 1) * pairs, LANES * h : LANES * (h + 1)]
     for s in range(stations):
         column = available[:, s : s + 1]
         for c in range(comps):
             pair = c * stations + s
             rows = jnp.concatenate(
-                [unit_ref[h, pl.ds(pair, count, stride=pairs), :] for h in range(length // LANES)], axis=1
+                [unit_ref[h, pl.ds(pair, count, stride=pitch), :] for h in range(length // LANES)], axis=1
             )
             rows_ref[pair * count : (pair + 1) * count, :] = (rows * column).astype(jnp.bfloat16)
-    batch = 8
+    batch = 3
     for at in range(0, pairs, batch):
         moved = jnp.dot(rows_ref[at * count : (at + batch) * count, :], order_ref[...], preferred_element_type=jnp.float32)
         for i in range(batch):
@@ -79,7 +81,7 @@
         in_specs=[VMEM, VMEM, VMEM],
         out_specs=(VMEM, VMEM),
         scratch_shapes=[
-            pltpu.VMEM((length // LANES, pairs * count, LANES), jnp.float32),
+            pltpu.VMEM((length // LANES, (pairs + 1) * count, LANES), jnp.float32),
             pltpu.VMEM((pairs * count, length), jnp.bfloat16),
         ],
         compiler_params=pltpu.CompilerParams(vmem_limit_bytes=16 << 20),

time: 21.7 us -> 21.3 us (0.982)
  Pallas kernels: 10.7 us -> 10.3 us
    pallas_call x1, Pallas kernels: 2.89 us -> 2.54 us  [templates_prepared(): pl.pallas_call(template_kernel, out_shape=(jax.ShapeDtypeStruct((pairs, 3...]
  transfers between devices with their start and end apart: 6 -> 6, of which waited for: 1 -> 1; matrix products, arithmetic and copies ran while one was open for 0% -> 0% of each run, Pallas kernels for 36% -> 35%
where the time goes in v6:
time: 21.3 us; the launch traced here: 21.2 us
  Pallas kernels  10.3 us (48%)
  starting transfers between devices  8.86 us (42%)
  waiting for transfers between devices  0.95 us (4%)
  other arithmetic  0.8 us (4%)
    ppermute x3, starting transfers between devices, shards(): lax.ppermute(block, 'tmpl', [(i, (i - d) % owners) for i in range(owners)])  6.96 us
    pallas_call x3, Pallas kernels, later_sum(): pl.pallas_call(functools.partial(later_kernel, static), out_shape=shape,...  4.73 us
    pallas_call x1, Pallas kernels, first_sum(): pl.pallas_call(functools.partial(first_kernel, len(blocks), static), out_...  2.88 us
    pallas_call x1, Pallas kernels, templates_prepared(): pl.pallas_call(template_kernel, out_shape=(jax.ShapeDtypeStruct((pairs, 3...  2.54 us
    ppermute x1, starting transfers between devices, shards(): lax.ppermute(both, 'sta', [(i, (i + d) % sides) for i in range(sides)])  1.55 us
    ppermute x1, waiting for transfers between devices, shards(): lax.ppermute(both, 'sta', [(i, (i + d) % sides) for i in range(sides)])  0.94 us
    add x1, other arithmetic, shards(): return total + got.astype(jnp.float32)  0.73 us
  transfers between devices with their start and end apart: 6, of which 1 were waited for; matrix products, arithmetic and copies ran while one was open for 0% of the time, Pallas kernels for 35%

profile of v6, /device:TPU:0, one launch (start us, length us, event | category | flops | bytes accessed | tf_op | source)
XLA Modules:
  0.0 21.2 jit_solution(11157068002400381660)
XLA Ops:
  0.0 0.0 copy-start.4
  0.0 0.0 copy-start.5
  0.0 3.0 %collective-permute-start.2 = (bf16[3,8,512]{2,1,0:T(8,128)(2,1)}, bf16[3,8,512]{2,1,0:T(8,128)(2,1)S(1)}, u32[]{:S(2)}, u32[]{:S(2)}) collective-permute-start(bf16[3,8,512]{2,1,0:T(8,128)(2,1)} %bitcast.4), channel_id=1, source_target_pairs={{0,4},{4,8},{8,12},{12,0},{1,5},{5,9},{9,13},{13,1},{2,6},{6,10},{... | collective-permute-start | bytes 73736 | tf_op jit(solution)/shard_map/ppermute | solution.py:308
  3.0 2.6 %collective-permute-start.1 = (bf16[3,8,512]{2,1,0:T(8,128)(2,1)}, bf16[3,8,512]{2,1,0:T(8,128)(2,1)S(1)}, u32[]{:S(2)}, u32[]{:S(2)}) collective-permute-start(bf16[3,8,512]{2,1,0:T(8,128)(2,1)} %bitcast.5), channel_id=1, source_target_pairs={{0,8},{4,12},{8,0},{12,4},{1,9},{5,13},{9,1},{13,5},{2,10},{6,14},... | collective-permute-start | bytes 73736 | tf_op jit(solution)/shard_map/ppermute | solution.py:308
  5.6 1.3 %collective-permute-start = (bf16[3,8,512]{2,1,0:T(8,128)(2,1)}, bf16[3,8,512]{2,1,0:T(8,128)(2,1)S(1)}, u32[]{:S(2)}, u32[]{:S(2)}) collective-permute-start(bf16[3,8,512]{2,1,0:T(8,128)(2,1)} %bitcast.6), channel_id=1, source_target_pairs={{0,12},{4,0},{8,4},{12,8},{1,13},{5,1},{9,5},{13,9},{2,14},{6,2},{... | collective-permute-start | bytes 73736 | tf_op jit(solution)/shard_map/ppermute | solution.py:308
  7.0 0.2 picks.1
  7.2 0.0 copy-done.4
  7.2 0.0 copy-done.5
  7.2 0.0 copy-start
  7.2 0.0 copy-start.1
  7.2 0.0 copy-start.2
  7.2 0.0 copy-start.3
  7.2 2.5 %templates.1 = (bf16[24,3,128,128]{3,2,1,0:T(8,128)(2,1)S(1)}, bf16[128,128]{1,0:T(8,128)(2,1)S(1)}) custom-call(bf16[128,3,8,256]{3,2,1,0:T(8,128)(2,1)S(1)} %bitcast.9, s32[8,128]{1,0:T(8,128)S(1)} %bitcast.10, bf16[256,256]{1,0:T(8,128)(2,1)S(1)} %get-tuple-element.18.order_ref), custom_call_target="tpu_custom_call" | custom-call | flops 2000000000 | bytes 8000000 | tf_op jit(solution)/shard_map/templates/pallas_call | solution.py:75
  9.8 0.0 collective-permute-done.2.refs_3_
  9.8 0.0 collective-permute-done.1.refs_2_
  9.8 0.0 collective-permute-done.refs_1_
  9.8 0.0 copy-done
  9.8 0.0 copy-done.1
  9.8 0.0 copy-done.2
  9.8 0.0 copy-done.3
  9.8 2.9 %records_sum.1 = (f32[2,32,1152]{2,1,0:T(8,128)S(1)}, f32[2,32,1024]{2,1,0:T(8,128)S(1)}, bf16[128,512]{1,0:T(8,128)(2,1)S(1)}) custom-call(s32[8]{0:T(128)S(1)} %copy-done.2, s32[8]{0:T(128)S(1)} %copy-done.3, bf16[256,256]{1,0:T(8,128)(2,1)S(1)} %get-tuple-element.21.split_ref, bf16[256,128]{1,0:T(8,128)(2,1)S(1)} %get-tuple-element.22.band_ref, ...), custom_call_target="tpu_custom_call" | custom-call | flops 805306368 | bytes 4000000 | tf_op jit(solution)/shard_map/records_sum/pallas_call | solution.py:244
  12.7 0.1 collective-permute-start.3
  12.8 1.6 %sum.3 = bf16[128,512]{1,0:T(8,128)(2,1)S(1)} custom-call(bf16[512,512]{1,0:T(8,128)(2,1)S(1)} %get-tuple-element.17.restore_ref.refs_0_, bf16[24,3,128,128]{3,2,1,0:T(8,128)(2,1)S(1)} %get-tuple-element.19.wide_ref.refs_1_, bf16[128,128]{1,0:T(8,128)(2,1)S(1)} %get-tuple-element.28.last_ref.refs_2_, f32[2,32,1152]{2,1,0:T(8,128)S(1)} %get-tuple-element.25.refs_3_, ...), custom_call_target="tpu_custom_call" | custom-call | flops 805306368 | bytes 4000000 | tf_op jit(solution)/shard_map/sum/pallas_call | solution.py:261
  14.4 0.0 collective-permute-done.3
  14.4 1.6 %collective-permute-start.4 = (bf16[128,512]{1,0:T(8,128)(2,1)S(1)}, bf16[128,512]{1,0:T(8,128)(2,1)S(1)}, u32[]{:S(2)}, u32[]{:S(2)}) collective-permute-start(bf16[128,512]{1,0:T(8,128)(2,1)S(1)} %add_convert_fusion), channel_id=1, source_target_pairs={{0,2},{2,0},{1,3},{3,1},{4,6},{6,4},{5,7},{7,5},{8,10},{10,8},{9,1... | collective-permute-start | bytes 393224 | tf_op jit(solution)/shard_map/ppermute | solution.py:328
  16.0 1.5 %sum.4 = bf16[128,512]{1,0:T(8,128)(2,1)S(1)} custom-call(bf16[512,512]{1,0:T(8,128)(2,1)S(1)} %get-tuple-element.17.restore_ref.refs_0_, bf16[24,3,128,128]{3,2,1,0:T(8,128)(2,1)S(1)} %get-tuple-element.19.wide_ref.refs_1_, bf16[128,128]{1,0:T(8,128)(2,1)S(1)} %get-tuple-element.28.last_ref.refs_2_, f32[2,32,1152]{2,1,0:T(8,128)S(1)} %get-tuple-element.25.refs_3_, ...), custom_call_target="tpu_custom_call" | custom-call | flops 805306368 | bytes 4000000 | tf_op jit(solution)/shard_map/sum/pallas_call | solution.py:261
  17.5 0.3 %collective-permute-start.5 = (bf16[128,512]{1,0:T(8,128)(2,1)S(1)}, bf16[128,512]{1,0:T(8,128)(2,1)S(1)}, u32[]{:S(2)}, u32[]{:S(2)}) collective-permute-start(bf16[128,512]{1,0:T(8,128)(2,1)S(1)} %sum.4), channel_id=1, source_target_pairs={{0,1},{1,0},{2,3},{3,2},{4,5},{5,4},{6,7},{7,6},{8,9},{9,8},{10,11... | collective-permute-start | bytes 393224 | tf_op jit(solution)/shard_map/ppermute | solution.py:323
  17.8 1.6 %sum.5 = f32[128,512]{1,0:T(8,128)S(1)} custom-call(bf16[512,512]{1,0:T(8,128)(2,1)S(1)} %get-tuple-element.17.restore_ref.refs_0_, bf16[24,3,128,128]{3,2,1,0:T(8,128)(2,1)S(1)} %get-tuple-element.19.wide_ref.refs_1_, bf16[128,128]{1,0:T(8,128)(2,1)S(1)} %get-tuple-element.28.last_ref.refs_2_, f32[2,32,1152]{2,1,0:T(8,128)S(1)} %get-tuple-element.25.refs_3_, ...), custom_call_target="tpu_custom_call" | custom-call | flops 805306368 | bytes 4000000 | tf_op jit(solution)/shard_map/sum/pallas_call | solution.py:261
  19.4 0.9 %collective-permute-done.4 = bf16[128,512]{1,0:T(8,128)(2,1)S(1)} collective-permute-done((bf16[128,512]{1,0:T(8,128)(2,1)S(1)}, bf16[128,512]{1,0:T(8,128)(2,1)S(1)}, u32[]{:S(2)}, u32[]{:S(2)}) %collective-permute-start.4) | collective-permute-done | bytes 131104 | tf_op jit(solution)/shard_map/ppermute | solution.py:328
  20.4 0.0 collective-permute-done.5
  20.4 0.7 %convert_add_fusion = f32[128,512]{1,0:T(8,128)} fusion(f32[128,512]{1,0:T(8,128)S(1)} %convert_add_fusion.1, bf16[128,512]{1,0:T(8,128)(2,1)S(1)} %collective-permute-done.5), kind=kLoop, calls=%fused_computation | loop fusion | flops 131072 | bytes 655360 | tf_op jit(solution)/shard_map/add | solution.py:334
  (2 shorter events, 0.1 us)
Async XLA Ops:
  0.0 7.2 %copy-start.4 = (bf16[128,8,3,256]{3,1,2,0:T(8,128)(2,1)S(1)}, bf16[128,8,3,256]{3,1,2,0:T(8,128)(2,1)}, u32[]{:S(2)}) copy-start(bf16[128,8,3,256]{3,1,2,0:T(8,128)(2,1)} %param.6) | copy-start | bytes 4718596
  0.0 7.2 %copy-start.5 = (s32[128,8]{0,1:T(8,128)S(1)}, s32[128,8]{0,1:T(8,128)}, u32[]{:S(2)}) copy-start(s32[128,8]{0,1:T(8,128)} %param.11) | copy-start | bytes 12292
  0.0 9.8 %collective-permute-start.2 = (bf16[3,8,512]{2,1,0:T(8,128)(2,1)}, bf16[3,8,512]{2,1,0:T(8,128)(2,1)S(1)}, u32[]{:S(2)}, u32[]{:S(2)}) collective-permute-start(bf16[3,8,512]{2,1,0:T(8,128)(2,1)} %bitcast.4), channel_id=1, source_target_pairs={{0,4},{4,8},{8,12},{12,0},{1,5},{5,9},{9,13},{13,1},{2,6},{6,10},{... | collective-permute-start | bytes 73736 | tf_op jit(solution)/shard_map/ppermute | solution.py:308
  3.0 6.8 %collective-permute-start.1 = (bf16[3,8,512]{2,1,0:T(8,128)(2,1)}, bf16[3,8,512]{2,1,0:T(8,128)(2,1)S(1)}, u32[]{:S(2)}, u32[]{:S(2)}) collective-permute-start(bf16[3,8,512]{2,1,0:T(8,128)(2,1)} %bitcast.5), channel_id=1, source_target_pairs={{0,8},{4,12},{8,0},{12,4},{1,9},{5,13},{9,1},{13,5},{2,10},{6,14},... | collective-permute-start | bytes 73736 | tf_op jit(solution)/shard_map/ppermute | solution.py:308
  5.6 4.2 %collective-permute-start = (bf16[3,8,512]{2,1,0:T(8,128)(2,1)}, bf16[3,8,512]{2,1,0:T(8,128)(2,1)S(1)}, u32[]{:S(2)}, u32[]{:S(2)}) collective-permute-start(bf16[3,8,512]{2,1,0:T(8,128)(2,1)} %bitcast.6), channel_id=1, source_target_pairs={{0,12},{4,0},{8,4},{12,8},{1,13},{5,1},{9,5},{13,9},{2,14},{6,2},{... | collective-permute-start | bytes 73736 | tf_op jit(solution)/shard_map/ppermute | solution.py:308
  7.2 2.6 %copy-start = (bf16[8,3,512]{2,0,1:T(8,128)(2,1)S(1)}, bf16[8,3,512]{2,0,1:T(8,128)(2,1)}, u32[]{:S(2)}) copy-start(bf16[8,3,512]{2,0,1:T(8,128)(2,1)} %param.7) | copy-start | bytes 73732
  7.2 2.6 %copy-start.1 = (bf16[8,3,512]{2,0,1:T(8,128)(2,1)S(1)}, bf16[8,3,512]{2,0,1:T(8,128)(2,1)}, u32[]{:S(2)}) copy-start(bf16[8,3,512]{2,0,1:T(8,128)(2,1)} %param.8) | copy-start | bytes 73732
  7.2 2.6 %copy-start.2 = (s32[8]{0:T(128)S(1)}, s32[8]{0:T(128)}, u32[]{:S(2)}) copy-start(s32[8]{0:T(128)} %offsets_ref.1) | copy-start | bytes 100
  7.2 2.6 %copy-start.3 = (s32[8]{0:T(128)S(1)}, s32[8]{0:T(128)}, u32[]{:S(2)}) copy-start(s32[8]{0:T(128)} %weights_ref.1) | copy-start | bytes 100
  12.7 1.6 %collective-permute-start.3 = (bf16[128,512]{1,0:T(8,128)(2,1)S(1)}, bf16[128,512]{1,0:T(8,128)(2,1)S(1)}, u32[]{:S(2)}, u32[]{:S(2)}) collective-permute-start(bf16[128,512]{1,0:T(8,128)(2,1)S(1)} %get-tuple-element.23), channel_id=1, source_target_pairs={{0,1},{1,0},{2,3},{3,2},{4,5},{5,4},{6,7},{7,6},{8,9},{9,8},{10,11... | collective-permute-start | bytes 393224 | tf_op jit(solution)/shard_map/ppermute | solution.py:323
  14.4 6.0 %collective-permute-start.4 = (bf16[128,512]{1,0:T(8,128)(2,1)S(1)}, bf16[128,512]{1,0:T(8,128)(2,1)S(1)}, u32[]{:S(2)}, u32[]{:S(2)}) collective-permute-start(bf16[128,512]{1,0:T(8,128)(2,1)S(1)} %add_convert_fusion), channel_id=1, source_target_pairs={{0,2},{2,0},{1,3},{3,1},{4,6},{6,4},{5,7},{7,5},{8,10},{10,8},{9,1... | collective-permute-start | bytes 393224 | tf_op jit(solution)/shard_map/ppermute | solution.py:328
  17.5 2.9 %collective-permute-start.5 = (bf16[128,512]{1,0:T(8,128)(2,1)S(1)}, bf16[128,512]{1,0:T(8,128)(2,1)S(1)}, u32[]{:S(2)}, u32[]{:S(2)}) collective-permute-start(bf16[128,512]{1,0:T(8,128)(2,1)S(1)} %sum.4), channel_id=1, source_target_pairs={{0,1},{1,0},{2,3},{3,2},{4,5},{5,4},{6,7},{7,6},{8,9},{9,8},{10,11... | collective-permute-start | bytes 393224 | tf_op jit(solution)/shard_map/ppermute | solution.py:323

commit v7 on v6

--- a/solution.py
+++ b/solution.py
@@ -54,7 +54,7 @@
                 [unit_ref[h, pl.ds(pair, count, stride=pitch), :] for h in range(length // LANES)], axis=1
             )
             rows_ref[pair * count : (pair + 1) * count, :] = (rows * column).astype(jnp.bfloat16)
-    batch = 3
+    batch = 2
     for at in range(0, pairs, batch):
         moved = jnp.dot(rows_ref[at * count : (at + batch) * count, :], order_ref[...], preferred_element_type=jnp.float32)
         for i in range(batch):

time: 21.3 us -> 21.3 us (level)
  no operation moved by 1% of the time
where the time goes in v7:
time: 21.3 us; the launch traced here: 21.2 us
  Pallas kernels  10.3 us (48%)
  starting transfers between devices  8.86 us (42%)
  waiting for transfers between devices  0.95 us (4%)
  other arithmetic  0.8 us (4%)
    ppermute x3, starting transfers between devices, shards(): lax.ppermute(block, 'tmpl', [(i, (i - d) % owners) for i in range(owners)])  6.96 us
    pallas_call x3, Pallas kernels, later_sum(): pl.pallas_call(functools.partial(later_kernel, static), out_shape=shape,...  4.73 us
    pallas_call x1, Pallas kernels, first_sum(): pl.pallas_call(functools.partial(first_kernel, len(blocks), static), out_...  2.88 us
    pallas_call x1, Pallas kernels, templates_prepared(): pl.pallas_call(template_kernel, out_shape=(jax.ShapeDtypeStruct((pairs, 3...  2.55 us
    ppermute x1, starting transfers between devices, shards(): lax.ppermute(both, 'sta', [(i, (i + d) % sides) for i in range(sides)])  1.55 us
    ppermute x1, waiting for transfers between devices, shards(): lax.ppermute(both, 'sta', [(i, (i + d) % sides) for i in range(sides)])  0.94 us
    add x1, other arithmetic, shards(): return total + got.astype(jnp.float32)  0.73 us
  transfers between devices with their start and end apart: 6, of which 1 were waited for; matrix products, arithmetic and copies ran while one was open for 0% of the time, Pallas kernels for 35%

profile of v7, /device:TPU:0, one launch (start us, length us, event | category | flops | bytes accessed | tf_op | source)
XLA Modules:
  0.0 21.2 jit_solution(1271377148205269656)
XLA Ops:
  0.0 0.0 copy-start.4
  0.0 0.0 copy-start.5
  0.0 3.0 %collective-permute-start.2 = (bf16[3,8,512]{2,1,0:T(8,128)(2,1)}, bf16[3,8,512]{2,1,0:T(8,128)(2,1)S(1)}, u32[]{:S(2)}, u32[]{:S(2)}) collective-permute-start(bf16[3,8,512]{2,1,0:T(8,128)(2,1)} %bitcast.4), channel_id=1, source_target_pairs={{0,4},{4,8},{8,12},{12,0},{1,5},{5,9},{9,13},{13,1},{2,6},{6,10},{... | collective-permute-start | bytes 73736 | tf_op jit(solution)/shard_map/ppermute | solution.py:308
  3.0 2.6 %collective-permute-start.1 = (bf16[3,8,512]{2,1,0:T(8,128)(2,1)}, bf16[3,8,512]{2,1,0:T(8,128)(2,1)S(1)}, u32[]{:S(2)}, u32[]{:S(2)}) collective-permute-start(bf16[3,8,512]{2,1,0:T(8,128)(2,1)} %bitcast.5), channel_id=1, source_target_pairs={{0,8},{4,12},{8,0},{12,4},{1,9},{5,13},{9,1},{13,5},{2,10},{6,14},... | collective-permute-start | bytes 73736 | tf_op jit(solution)/shard_map/ppermute | solution.py:308
  5.6 1.3 %collective-permute-start = (bf16[3,8,512]{2,1,0:T(8,128)(2,1)}, bf16[3,8,512]{2,1,0:T(8,128)(2,1)S(1)}, u32[]{:S(2)}, u32[]{:S(2)}) collective-permute-start(bf16[3,8,512]{2,1,0:T(8,128)(2,1)} %bitcast.6), channel_id=1, source_target_pairs={{0,12},{4,0},{8,4},{12,8},{1,13},{5,1},{9,5},{13,9},{2,14},{6,2},{... | collective-permute-start | bytes 73736 | tf_op jit(solution)/shard_map/ppermute | solution.py:308
  7.0 0.2 picks.1
  7.2 0.0 copy-done.4
  7.2 0.0 copy-done.5
  7.2 0.0 copy-start
  7.2 0.0 copy-start.1
  7.2 0.0 copy-start.2
  7.2 0.0 copy-start.3
  7.2 2.5 %templates.1 = (bf16[24,3,128,128]{3,2,1,0:T(8,128)(2,1)S(1)}, bf16[128,128]{1,0:T(8,128)(2,1)S(1)}) custom-call(bf16[128,3,8,256]{3,2,1,0:T(8,128)(2,1)S(1)} %bitcast.9, s32[8,128]{1,0:T(8,128)S(1)} %bitcast.10, bf16[256,256]{1,0:T(8,128)(2,1)S(1)} %get-tuple-element.18.order_ref), custom_call_target="tpu_custom_call" | custom-call | flops 2000000000 | bytes 8000000 | tf_op jit(solution)/shard_map/templates/pallas_call | solution.py:75
  9.8 0.0 collective-permute-done.2.refs_3_
  9.8 0.0 collective-permute-done.1.refs_2_
  9.8 0.0 collective-permute-done.refs_1_
  9.8 0.0 copy-done
  9.8 0.0 copy-done.1
  9.8 0.0 copy-done.2
  9.8 0.0 copy-done.3
  9.9 2.9 %records_sum.1 = (f32[2,32,1152]{2,1,0:T(8,128)S(1)}, f32[2,32,1024]{2,1,0:T(8,128)S(1)}, bf16[128,512]{1,0:T(8,128)(2,1)S(1)}) custom-call(s32[8]{0:T(128)S(1)} %copy-done.2, s32[8]{0:T(128)S(1)} %copy-done.3, bf16[256,256]{1,0:T(8,128)(2,1)S(1)} %get-tuple-element.21.split_ref, bf16[256,128]{1,0:T(8,128)(2,1)S(1)} %get-tuple-element.22.band_ref, ...), custom_call_target="tpu_custom_call" | custom-call | flops 805306368 | bytes 4000000 | tf_op jit(solution)/shard_map/records_sum/pallas_call | solution.py:244
  12.7 0.1 collective-permute-start.3
  12.8 1.6 %sum.3 = bf16[128,512]{1,0:T(8,128)(2,1)S(1)} custom-call(bf16[512,512]{1,0:T(8,128)(2,1)S(1)} %get-tuple-element.17.restore_ref.refs_0_, bf16[24,3,128,128]{3,2,1,0:T(8,128)(2,1)S(1)} %get-tuple-element.19.wide_ref.refs_1_, bf16[128,128]{1,0:T(8,128)(2,1)S(1)} %get-tuple-element.28.last_ref.refs_2_, f32[2,32,1152]{2,1,0:T(8,128)S(1)} %get-tuple-element.25.refs_3_, ...), custom_call_target="tpu_custom_call" | custom-call | flops 805306368 | bytes 4000000 | tf_op jit(solution)/shard_map/sum/pallas_call | solution.py:261
  14.4 0.0 collective-permute-done.3
  14.4 1.6 %collective-permute-start.4 = (bf16[128,512]{1,0:T(8,128)(2,1)S(1)}, bf16[128,512]{1,0:T(8,128)(2,1)S(1)}, u32[]{:S(2)}, u32[]{:S(2)}) collective-permute-start(bf16[128,512]{1,0:T(8,128)(2,1)S(1)} %add_convert_fusion), channel_id=1, source_target_pairs={{0,2},{2,0},{1,3},{3,1},{4,6},{6,4},{5,7},{7,5},{8,10},{10,8},{9,1... | collective-permute-start | bytes 393224 | tf_op jit(solution)/shard_map/ppermute | solution.py:328
  16.0 1.5 %sum.4 = bf16[128,512]{1,0:T(8,128)(2,1)S(1)} custom-call(bf16[512,512]{1,0:T(8,128)(2,1)S(1)} %get-tuple-element.17.restore_ref.refs_0_, bf16[24,3,128,128]{3,2,1,0:T(8,128)(2,1)S(1)} %get-tuple-element.19.wide_ref.refs_1_, bf16[128,128]{1,0:T(8,128)(2,1)S(1)} %get-tuple-element.28.last_ref.refs_2_, f32[2,32,1152]{2,1,0:T(8,128)S(1)} %get-tuple-element.25.refs_3_, ...), custom_call_target="tpu_custom_call" | custom-call | flops 805306368 | bytes 4000000 | tf_op jit(solution)/shard_map/sum/pallas_call | solution.py:261
  17.5 0.3 %collective-permute-start.5 = (bf16[128,512]{1,0:T(8,128)(2,1)S(1)}, bf16[128,512]{1,0:T(8,128)(2,1)S(1)}, u32[]{:S(2)}, u32[]{:S(2)}) collective-permute-start(bf16[128,512]{1,0:T(8,128)(2,1)S(1)} %sum.4), channel_id=1, source_target_pairs={{0,1},{1,0},{2,3},{3,2},{4,5},{5,4},{6,7},{7,6},{8,9},{9,8},{10,11... | collective-permute-start | bytes 393224 | tf_op jit(solution)/shard_map/ppermute | solution.py:323
  17.8 1.6 %sum.5 = f32[128,512]{1,0:T(8,128)S(1)} custom-call(bf16[512,512]{1,0:T(8,128)(2,1)S(1)} %get-tuple-element.17.restore_ref.refs_0_, bf16[24,3,128,128]{3,2,1,0:T(8,128)(2,1)S(1)} %get-tuple-element.19.wide_ref.refs_1_, bf16[128,128]{1,0:T(8,128)(2,1)S(1)} %get-tuple-element.28.last_ref.refs_2_, f32[2,32,1152]{2,1,0:T(8,128)S(1)} %get-tuple-element.25.refs_3_, ...), custom_call_target="tpu_custom_call" | custom-call | flops 805306368 | bytes 4000000 | tf_op jit(solution)/shard_map/sum/pallas_call | solution.py:261
  19.5 0.9 %collective-permute-done.4 = bf16[128,512]{1,0:T(8,128)(2,1)S(1)} collective-permute-done((bf16[128,512]{1,0:T(8,128)(2,1)S(1)}, bf16[128,512]{1,0:T(8,128)(2,1)S(1)}, u32[]{:S(2)}, u32[]{:S(2)}) %collective-permute-start.4) | collective-permute-done | bytes 131104 | tf_op jit(solution)/shard_map/ppermute | solution.py:328
  20.4 0.0 collective-permute-done.5
  20.4 0.7 %convert_add_fusion = f32[128,512]{1,0:T(8,128)} fusion(f32[128,512]{1,0:T(8,128)S(1)} %convert_add_fusion.1, bf16[128,512]{1,0:T(8,128)(2,1)S(1)} %collective-permute-done.5), kind=kLoop, calls=%fused_computation | loop fusion | flops 131072 | bytes 655360 | tf_op jit(solution)/shard_map/add | solution.py:334
  (2 shorter events, 0.1 us)
Async XLA Ops:
  0.0 7.2 %copy-start.4 = (bf16[128,8,3,256]{3,1,2,0:T(8,128)(2,1)S(1)}, bf16[128,8,3,256]{3,1,2,0:T(8,128)(2,1)}, u32[]{:S(2)}) copy-start(bf16[128,8,3,256]{3,1,2,0:T(8,128)(2,1)} %param.6) | copy-start | bytes 4718596
  0.0 7.2 %copy-start.5 = (s32[128,8]{0,1:T(8,128)S(1)}, s32[128,8]{0,1:T(8,128)}, u32[]{:S(2)}) copy-start(s32[128,8]{0,1:T(8,128)} %param.11) | copy-start | bytes 12292
  0.0 9.8 %collective-permute-start.2 = (bf16[3,8,512]{2,1,0:T(8,128)(2,1)}, bf16[3,8,512]{2,1,0:T(8,128)(2,1)S(1)}, u32[]{:S(2)}, u32[]{:S(2)}) collective-permute-start(bf16[3,8,512]{2,1,0:T(8,128)(2,1)} %bitcast.4), channel_id=1, source_target_pairs={{0,4},{4,8},{8,12},{12,0},{1,5},{5,9},{9,13},{13,1},{2,6},{6,10},{... | collective-permute-start | bytes 73736 | tf_op jit(solution)/shard_map/ppermute | solution.py:308
  3.0 6.8 %collective-permute-start.1 = (bf16[3,8,512]{2,1,0:T(8,128)(2,1)}, bf16[3,8,512]{2,1,0:T(8,128)(2,1)S(1)}, u32[]{:S(2)}, u32[]{:S(2)}) collective-permute-start(bf16[3,8,512]{2,1,0:T(8,128)(2,1)} %bitcast.5), channel_id=1, source_target_pairs={{0,8},{4,12},{8,0},{12,4},{1,9},{5,13},{9,1},{13,5},{2,10},{6,14},... | collective-permute-start | bytes 73736 | tf_op jit(solution)/shard_map/ppermute | solution.py:308
  5.6 4.2 %collective-permute-start = (bf16[3,8,512]{2,1,0:T(8,128)(2,1)}, bf16[3,8,512]{2,1,0:T(8,128)(2,1)S(1)}, u32[]{:S(2)}, u32[]{:S(2)}) collective-permute-start(bf16[3,8,512]{2,1,0:T(8,128)(2,1)} %bitcast.6), channel_id=1, source_target_pairs={{0,12},{4,0},{8,4},{12,8},{1,13},{5,1},{9,5},{13,9},{2,14},{6,2},{... | collective-permute-start | bytes 73736 | tf_op jit(solution)/shard_map/ppermute | solution.py:308
  7.2 2.6 %copy-start = (bf16[8,3,512]{2,0,1:T(8,128)(2,1)S(1)}, bf16[8,3,512]{2,0,1:T(8,128)(2,1)}, u32[]{:S(2)}) copy-start(bf16[8,3,512]{2,0,1:T(8,128)(2,1)} %param.7) | copy-start | bytes 73732
  7.2 2.6 %copy-start.1 = (bf16[8,3,512]{2,0,1:T(8,128)(2,1)S(1)}, bf16[8,3,512]{2,0,1:T(8,128)(2,1)}, u32[]{:S(2)}) copy-start(bf16[8,3,512]{2,0,1:T(8,128)(2,1)} %param.8) | copy-start | bytes 73732
  7.2 2.6 %copy-start.2 = (s32[8]{0:T(128)S(1)}, s32[8]{0:T(128)}, u32[]{:S(2)}) copy-start(s32[8]{0:T(128)} %offsets_ref.1) | copy-start | bytes 100
  7.2 2.6 %copy-start.3 = (s32[8]{0:T(128)S(1)}, s32[8]{0:T(128)}, u32[]{:S(2)}) copy-start(s32[8]{0:T(128)} %weights_ref.1) | copy-start | bytes 100
  12.7 1.6 %collective-permute-start.3 = (bf16[128,512]{1,0:T(8,128)(2,1)S(1)}, bf16[128,512]{1,0:T(8,128)(2,1)S(1)}, u32[]{:S(2)}, u32[]{:S(2)}) collective-permute-start(bf16[128,512]{1,0:T(8,128)(2,1)S(1)} %get-tuple-element.23), channel_id=1, source_target_pairs={{0,1},{1,0},{2,3},{3,2},{4,5},{5,4},{6,7},{7,6},{8,9},{9,8},{10,11... | collective-permute-start | bytes 393224 | tf_op jit(solution)/shard_map/ppermute | solution.py:323
  14.4 6.0 %collective-permute-start.4 = (bf16[128,512]{1,0:T(8,128)(2,1)S(1)}, bf16[128,512]{1,0:T(8,128)(2,1)S(1)}, u32[]{:S(2)}, u32[]{:S(2)}) collective-permute-start(bf16[128,512]{1,0:T(8,128)(2,1)S(1)} %add_convert_fusion), channel_id=1, source_target_pairs={{0,2},{2,0},{1,3},{3,1},{4,6},{6,4},{5,7},{7,5},{8,10},{10,8},{9,1... | collective-permute-start | bytes 393224 | tf_op jit(solution)/shard_map/ppermute | solution.py:328
  17.5 2.9 %collective-permute-start.5 = (bf16[128,512]{1,0:T(8,128)(2,1)S(1)}, bf16[128,512]{1,0:T(8,128)(2,1)S(1)}, u32[]{:S(2)}, u32[]{:S(2)}) collective-permute-start(bf16[128,512]{1,0:T(8,128)(2,1)S(1)} %sum.4), channel_id=1, source_target_pairs={{0,1},{1,0},{2,3},{3,2},{4,5},{5,4},{6,7},{7,6},{8,9},{9,8},{10,11... | collective-permute-start | bytes 393224 | tf_op jit(solution)/shard_map/ppermute | solution.py:323
